TPU v7x, 256 devices: a whole 4x4x8 slice. The times are simulated.
256 devices in a mesh: dp: 32 (over y, z), cent: 8 (over x, core).
Axes of the slice: x: 4, y: 4, z: 8, core: 2. Of those that a mesh axis runs over, the one named last changes fastest.
Arguments:
- embeddings: bfloat16 [16384, 768], P('dp'), may hold values from -400 to 400, as said below
- centroids: bfloat16 [16384, 768], P('cent'), may hold values from -400 to 400, as said below
Outputs:
- new_centroids: float32 [16384, 768], P(('cent', 'dp'))
Inputs may be any that keep to these rules, and one draw needn't show every extreme that they name: `embeddings`: finite real values. `centroids`: finite real values.
All inputs are finite; a program needn't handle non-finite values.
Results may differ from a plain program's by a relative error of at most 0.0038.
Values sent between devices are 32-bit elements; how exact they have to be, the bound alone decides.
A program may use at most 64 MiB of HBM per device.

v0:
```python
import jax
import jax.numpy as jnp
from jax import lax
from jax.sharding import PartitionSpec as P

FEATURE_DIM = 768
ROUNDS = 2


entropy_regularizer = 0.05


def normalize(values):
    wide = values.astype(jnp.float32)
    meansq = jnp.mean(wide * wide, axis=-1, keepdims=True)
    return (wide * lax.rsqrt(meansq + 1e-06)).astype(jnp.bfloat16)


def row_update(boltzmann_affinity, column_factor):
    partial_rows = jnp.dot(boltzmann_affinity, column_factor, precision=lax.Precision.HIGHEST)
    totals = lax.psum(partial_rows, "cent")
    return 1.0 / totals


def shards(embeddings, centroids):
    normed = normalize(embeddings)
    cent_normed = normalize(centroids)
    cosine_matches = lax.dot_general(
        normed, cent_normed, (((1,), (1,)), ((), ())), preferred_element_type=jnp.float32
    )
    boltzmann_affinity = jnp.exp(cosine_matches * (1.0 / (FEATURE_DIM * entropy_regularizer)))
    local_cents = centroids.shape[0]
    row_count = embeddings.shape[0] * lax.axis_size("dp")
    cent_count = local_cents * lax.axis_size("cent")
    balance_ratio = row_count / cent_count
    column_factor = jnp.ones((local_cents,), jnp.float32)
    for sweep in range(ROUNDS):
        row_weight = row_update(boltzmann_affinity, column_factor)
        partial_cols = jnp.dot(row_weight, boltzmann_affinity, precision=lax.Precision.HIGHEST)
        column_factor = balance_ratio / lax.psum(partial_cols, "dp")
    row_weight = row_update(boltzmann_affinity, column_factor)
    transport = (row_weight[:, None] * boltzmann_affinity * column_factor[None, :]).astype(
        jnp.bfloat16
    )
    col_mass = jnp.sum(transport, axis=0, dtype=jnp.float32)
    own_rows = local_cents // lax.axis_size("dp")
    holder_position = lax.axis_index("dp")
    weighted = lax.dot_general(
        transport, normed, (((0,), (0,)), ((), ())), preferred_element_type=jnp.float32
    )
    weighted, col_mass = lax.psum((weighted, col_mass), "dp")
    weighted = lax.dynamic_slice_in_dim(weighted, holder_position * own_rows, own_rows, 0)
    col_mass = lax.dynamic_slice_in_dim(col_mass, holder_position * own_rows, own_rows, 0)
    return weighted / col_mass[:, None]


def solution(mesh):
    in_specs = (P("dp", None), P("cent", None))
    out_specs = P(("cent", "dp"), None)
    return jax.shard_map(shards, mesh=mesh, in_specs=in_specs, out_specs=out_specs, check_vma=False)
```

profile of v0, /device:TPU:2, one launch (start us, length us, event | category | flops | bytes accessed | tf_op | source)
XLA Modules:
  0.0 423.5 jit_solution(16495555627973379805)
XLA Ops:
  6.5 0.0 all-reduce.2.cloned.1.call-start
  6.5 1.4 fusion.4
  7.9 2.6 fusion
  10.5 4.1 multiply_exponential_fusion
  14.6 0.0 copy-start
  14.6 1.9 copy-done
  16.6 3.6 fusion.9
  20.2 11.7 %psum.49 = f32[512]{0:T(512)S(1)} all-reduce(f32[512]{0:T(512)S(1)} %bitcast.25), channel_id=1, replica_groups=mesh['dp'=32,'cent'=8] {'cent'}, use_global_device_ids=true, to_apply=%region_2.0 | all-reduce | flops 512 | bytes 4096 | tf_op jit(solution)/shard_map/psum | solution.py:21
  31.9 4.3 %fusion.12 = f32[1,2048]{1,0:T(1,128)S(1)} fusion(f32[512,1]{0,1:T(1,128)S(1)} %bitcast.22, f32[512,2048]{1,0:T(8,128)} %copy-done), kind=kOutput, calls=%fused_computation.24 | convolution fusion | flops 12582912 | bytes 4204544 | tf_op jit(solution)/shard_map/dot_general | solution.py:39
  36.1 78.9 %psum.50 = f32[2048]{0:T(1024)S(1)} all-reduce(f32[2048]{0:T(1024)S(1)} %bitcast.19), channel_id=1, replica_groups=mesh['dp'=32,'cent'=8] {'dp'}, use_global_device_ids=true, to_apply=%region_3.0 | all-reduce | flops 2048 | bytes 16384 | tf_op jit(solution)/shard_map/psum | solution.py:40
  115.1 5.8 %fusion.13 = f32[1,512]{1,0:T(1,128)S(1)} fusion(f32[512,2048]{1,0:T(8,128)} %copy-done, f32[2048,1]{0,1:T(1,128)S(1)} %bitcast.20), kind=kOutput, calls=%fused_computation.25 | convolution fusion | flops 12582912 | bytes 4204544 | tf_op jit(solution)/shard_map/dot_general | solution.py:20
  120.9 12.6 %psum.51 = f32[512]{0:T(512)S(1)} all-reduce(f32[512]{0:T(512)S(1)} %bitcast.23), channel_id=1, replica_groups=mesh['dp'=32,'cent'=8] {'cent'}, use_global_device_ids=true, to_apply=%region_4.0 | all-reduce | flops 512 | bytes 4096 | tf_op jit(solution)/shard_map/psum | solution.py:21
  133.5 4.3 %fusion.14 = f32[1,2048]{1,0:T(1,128)S(1)} fusion(f32[512,1]{0,1:T(1,128)S(1)} %bitcast.24, f32[512,2048]{1,0:T(8,128)} %copy-done), kind=kOutput, calls=%fused_computation.26 | convolution fusion | flops 12582912 | bytes 4204544 | tf_op jit(solution)/shard_map/dot_general | solution.py:39
  137.8 70.6 %psum.52 = f32[2048]{0:T(1024)S(1)} all-reduce(f32[2048]{0:T(1024)S(1)} %bitcast.21), channel_id=1, replica_groups=mesh['dp'=32,'cent'=8] {'dp'}, use_global_device_ids=true, to_apply=%region_5.0 | all-reduce | flops 2048 | bytes 16384 | tf_op jit(solution)/shard_map/psum | solution.py:40
  208.5 5.8 %fusion.15 = f32[1,512]{1,0:T(1,128)S(1)} fusion(f32[512,2048]{1,0:T(8,128)} %copy-done, f32[2048,1]{0,1:T(1,128)S(1)} %bitcast.18), kind=kOutput, calls=%fused_computation.27 | convolution fusion | flops 12582912 | bytes 4204544 | tf_op jit(solution)/shard_map/dot_general | solution.py:20
  214.2 12.4 %psum.53 = f32[512]{0:T(512)S(1)} all-reduce(f32[512]{0:T(512)S(1)} %bitcast.26), channel_id=1, replica_groups=mesh['dp'=32,'cent'=8] {'cent'}, use_global_device_ids=true, to_apply=%region_6.0 | all-reduce | flops 512 | bytes 4096 | tf_op jit(solution)/shard_map/psum | solution.py:21
  226.6 0.0 copy-done.1
  226.6 6.8 %fusion.6 = f32[2048,768]{1,0:T(8,128)} fusion(bf16[512,768]{1,0:T(8,128)(2,1)S(1)} %copy-done.1, f32[512]{0:T(512)S(1)} %add_rsqrt_fusion.1, f32[512,2048]{1,0:T(8,128)} %copy-done, f32[2048]{0:T(1024)S(1)} %broadcast_divide_fusion.1, f32[512]{0:T(512)S(1)} %broadcast_divide_fusion.2), kind=kOutput, calls=%fused_computation.12 | convolution fusion | flops 1614938112 | bytes 11284480 | tf_op jit(solution)/shard_map/dot_general | solution.py:48
  233.5 0.0 all-reduce.2.cloned.1.call-update
  233.5 2.7 convert_reduce_fusion
  236.2 75.4 %psum.55 = f32[2048]{0:T(1024)S(1)} all-reduce(f32[2048]{0:T(1024)S(1)} %convert_reduce_fusion), channel_id=1, replica_groups=mesh['dp'=32,'cent'=8] {'dp'}, use_global_device_ids=true, to_apply=%region_9.0 | all-reduce | flops 2048 | bytes 16384 | tf_op jit(solution)/shard_map/psum | solution.py:51
  311.6 0.1 dynamic_slice.7
  311.7 103.3 %all-reduce.2.cloned.1.call-done = f32[2048,768]{1,0:T(8,128)} async-done(((f32[2048,768]{1,0:T(8,128)}), f32[2048,768]{1,0:T(8,128)}) %all-reduce.2.cloned.1.call-update) | async-done | bytes 6291472 | tf_op jit(solution)/shard_map/psum | solution.py:51
  415.0 1.7 dynamic-slice_divide_fusion
  (8 shorter events, 0.0 us)
Async XLA Ops:
  6.5 408.4 %all-reduce.2.cloned.1.call-start = ((), (), s32[]{:S(2)}) async-start(), calls=%async_computation | async-start | bytes 12582912 | tf_op jit(solution)/shard_map/psum | solution.py:51
  14.6 2.0 copy-start
  133.5 93.2 %copy-start.1 = (bf16[512,768]{1,0:T(8,128)(2,1)S(1)}, bf16[512,768]{1,0:T(8,128)(2,1)}, u32[]{:S(2)}) copy-start(bf16[512,768]{1,0:T(8,128)(2,1)} %param.2) | copy-start | bytes 2359300
Sparse Core Ops, SparseCore 0:
  233.6 181.2 all-reduce.1
where the time goes:
time: 424 us
  blocking collectives  262 us (62%)
  waiting for transfers between devices  103 us (24%)
  matrix products  34.7 us (8%)
  between operations  13.5 us (3%)
  other arithmetic  8.35 us (2%)
    psum x2, blocking collectives, shards(): column_factor = balance_ratio / lax.psum(partial_cols, 'dp')  150 us
    psum x1, waiting for transfers between devices, shards(): weighted, col_mass = lax.psum((weighted, col_mass), 'dp')  103 us
    psum x1, blocking collectives, shards(): weighted, col_mass = lax.psum((weighted, col_mass), 'dp')  75.4 us
    psum x3, blocking collectives, row_update(): totals = lax.psum(partial_rows, 'cent')  36.7 us
    dot_general x3, matrix products, row_update(): jnp.dot(boltzmann_affinity, column_factor, precision=lax.Precision.HIGHEST)  15.1 us
    dot_general x2, matrix products, shards(): jnp.dot(row_weight, boltzmann_affinity, precision=lax.Precision.HIGHEST)  8.61 us
  transfers between devices with their start and end apart: 1, of which 1 were waited for; matrix products, arithmetic and copies ran while one was open for 1% of the time, Pallas kernels for 0%

commit v1 on v0

v1 whole, which is shorter than its diff:
```python
import jax
import jax.numpy as jnp
import numpy as np
from jax import lax
from jax.sharding import Mesh, PartitionSpec as P

FEATURE_DIM = 768
ROUNDS = 2


entropy_regularizer = 0.05


def normalize(values):
    wide = values.astype(jnp.float32)
    meansq = jnp.mean(wide * wide, axis=-1, keepdims=True)
    return (wide * lax.rsqrt(meansq + 1e-06)).astype(jnp.bfloat16)


def cent_sum(x):
    return lax.psum(lax.psum(x, "core"), "cx")


def dp_sum(x):
    return lax.psum(lax.psum(x, "dz"), "dy")


def dp_scatter(x, ny, nz):
    rows = x.shape[0] // (ny * nz)
    rest = x.shape[1:]
    x = x.reshape((ny, nz, rows) + rest)
    x = jnp.swapaxes(x, 0, 1).reshape((nz * ny * rows,) + rest)
    x = lax.psum_scatter(x, "dz", scatter_dimension=0, tiled=True)
    return lax.psum_scatter(x, "dy", scatter_dimension=0, tiled=True)


def row_update(boltzmann_affinity, column_factor):
    partial_rows = jnp.dot(boltzmann_affinity, column_factor, precision=lax.Precision.HIGHEST)
    return 1.0 / cent_sum(partial_rows)


def shards(embeddings, centroids):
    ny = lax.axis_size("dy")
    nz = lax.axis_size("dz")
    normed = normalize(embeddings)
    cent_normed = normalize(centroids)
    cosine_matches = lax.dot_general(
        normed, cent_normed, (((1,), (1,)), ((), ())), preferred_element_type=jnp.float32
    )
    boltzmann_affinity = jnp.exp(cosine_matches * (1.0 / (FEATURE_DIM * entropy_regularizer)))
    local_cents = centroids.shape[0]
    row_count = embeddings.shape[0] * ny * nz
    cent_count = local_cents * lax.axis_size("cx") * lax.axis_size("core")
    balance_ratio = row_count / cent_count
    column_factor = jnp.ones((local_cents,), jnp.float32)
    for sweep in range(ROUNDS):
        row_weight = row_update(boltzmann_affinity, column_factor)
        partial_cols = jnp.dot(row_weight, boltzmann_affinity, precision=lax.Precision.HIGHEST)
        column_factor = balance_ratio / dp_sum(partial_cols)
    row_weight = row_update(boltzmann_affinity, column_factor)
    transport = (row_weight[:, None] * boltzmann_affinity * column_factor[None, :]).astype(
        jnp.bfloat16
    )
    col_mass = jnp.sum(transport, axis=0, dtype=jnp.float32)
    col_mass = dp_scatter(col_mass, ny, nz)
    weighted = lax.dot_general(
        transport, normed, (((0,), (0,)), ((), ())), preferred_element_type=jnp.float32
    )
    weighted = dp_scatter(weighted, ny, nz)
    return weighted / col_mass[:, None]


def split_mesh(mesh):
    devices = mesh.devices
    n_dp, n_cent = devices.shape
    try:
        ny = len({d.coords[1] for d in devices.flat})
        ncore = len({d.core_on_chip for d in devices.flat})
    except AttributeError:
        ny, ncore = 4, 2
    return Mesh(
        devices.reshape(ny, n_dp // ny, n_cent // ncore, ncore), ("dy", "dz", "cx", "core")
    )


def solution(mesh):
    sub = split_mesh(mesh)
    in_specs = (P(("dy", "dz"), None), P(("cx", "core"), None))
    out_specs = P(("cx", "core", "dy", "dz"), None)
    return jax.shard_map(shards, mesh=sub, in_specs=in_specs, out_specs=out_specs, check_vma=False)
```

time: 424 us -> 249 us (0.59)
  blocking collectives: 262 us -> 114 us
  waiting for transfers between devices: 103 us -> 72.5 us
  local copies, waits for them, and re-layouts: 2.03 us -> 6.91 us
    psum x6 -> x10, blocking collectives: 262 us -> 87.3 us  [the longest x4 52 us: dp_sum(): return lax.psum(lax.psum(x, 'dz'), 'dy')]
    psum x1 -> x0, waiting for transfers between devices: 103 us -> none  [shards(): weighted, col_mass = lax.psum((weighted, col_mass), 'dp')]
    reduce_scatter x0 -> x2, waiting for transfers between devices: none -> 72.5 us  [the longest x1 72.5 us: dp_scatter(): x = lax.psum_scatter(x, 'dz', scatter_dimension=0, tiled=True)]
    unnamed x0 -> x2, blocking collectives: none -> 26.2 us
  transfers between devices with their start and end apart: 1 -> 2, of which waited for: 1 -> 1; matrix products, arithmetic and copies ran while one was open for 1% -> 2% of each run, Pallas kernels for 0% -> 0%
where the time goes in v1:
time: 249 us; the launch traced here: 248 us
  blocking collectives  114 us (46%)
  waiting for transfers between devices  72.5 us (29%)
  matrix products  32.1 us (13%)
  between operations  14.8 us (6%)
  other arithmetic  8.35 us (3%)
  local copies, waits for them, and re-layouts  6.91 us (3%)
    reduce_scatter x1, waiting for transfers between devices, dp_scatter(): x = lax.psum_scatter(x, 'dz', scatter_dimension=0, tiled=True)  72.5 us
    psum x4, blocking collectives, dp_sum(): return lax.psum(lax.psum(x, 'dz'), 'dy')  52 us
    psum x6, blocking collectives, cent_sum(): return lax.psum(lax.psum(x, 'core'), 'cx')  35.3 us
    unnamed x2, blocking collectives  26.2 us
    dot_general x3, matrix products, row_update(): jnp.dot(boltzmann_affinity, column_factor, precision=lax.Precision.HIGHEST)  15.1 us
    dot_general x2, matrix products, shards(): jnp.dot(row_weight, boltzmann_affinity, precision=lax.Precision.HIGHEST)  8.61 us
  transfers between devices with their start and end apart: 2, of which 1 were waited for; matrix products, arithmetic and copies ran while one was open for 2% of the time, Pallas kernels for 0%

profile of v1, /device:TPU:2, one launch (start us, length us, event | category | flops | bytes accessed | tf_op | source)
XLA Modules:
  0.0 248.2 jit_solution(16660720603624140964)
XLA Ops:
  7.9 2.6 %fusion = f32[2048]{0:T(1024)S(1)} fusion(bf16[2048,768]{1,0:T(8,128)(2,1)} %param.3), kind=kLoop, calls=%fused_computation.2 | loop fusion | flops 4716544 | bytes 3153920 | tf_op jit(solution)/shard_map/reduce_sum | solution.py:16
  10.5 4.1 %multiply_exponential_fusion = f32[512,2048]{1,0:T(8,128)S(1)} fusion(bf16[2048,768]{1,0:T(8,128)(2,1)} %param.3, f32[2048]{0:T(1024)S(1)} %add_rsqrt_fusion, bf16[512,768]{1,0:T(8,128)(2,1)} %param.2, f32[512]{0:T(512)S(1)} %add_rsqrt_fusion.1), kind=kOutput, calls=%fused_computation.6 | convolution fusion | flops 1617559552 | bytes 8136704 | tf_op jit(solution)/shard_map/dot_general | solution.py:47
  14.6 2.0 copy-done
  16.7 3.6 %fusion.9 = f32[1,512]{1,0:T(1,128)S(1)} fusion(f32[512,2048]{1,0:T(8,128)S(1)} %multiply_exponential_fusion), kind=kOutput, calls=%fused_computation.15 | convolution fusion | flops 12582912 | bytes 4196352 | tf_op jit(solution)/shard_map/dot_general | solution.py:38
  20.3 2.5 psum.70
  22.7 9.9 %psum.71 = f32[512]{0:T(512)S(1)} all-reduce(f32[512]{0:T(512)S(1)} %psum.70), channel_id=1, replica_groups=mesh['dy'=4,'dz'=8,'cx'=4,'core'=2] {'cx'}, use_global_device_ids=true, to_apply=%region_3.0 | all-reduce | flops 512 | bytes 4096 | tf_op jit(solution)/shard_map/psum | solution.py:21
  32.7 4.3 %fusion.12 = f32[1,2048]{1,0:T(1,128)S(1)} fusion(f32[512,1]{0,1:T(1,128)S(1)} %bitcast.32, f32[512,2048]{1,0:T(8,128)} %copy-done), kind=kOutput, calls=%fused_computation.24 | convolution fusion | flops 12582912 | bytes 4204544 | tf_op jit(solution)/shard_map/dot_general | solution.py:58
  36.9 18.9 %psum.72 = f32[2048]{0:T(1024)S(1)} all-reduce(f32[2048]{0:T(1024)S(1)} %bitcast.29), channel_id=1, replica_groups=mesh['dy'=4,'dz'=8,'cx'=4,'core'=2] {'dz'}, use_global_device_ids=true, to_apply=%region_4.0 | all-reduce | flops 2048 | bytes 16384 | tf_op jit(solution)/shard_map/psum | solution.py:25
  55.8 10.9 %psum.73 = f32[2048]{0:T(1024)S(1)} all-reduce(f32[2048]{0:T(1024)S(1)} %psum.72), channel_id=1, replica_groups=mesh['dy'=4,'dz'=8,'cx'=4,'core'=2] {'dy'}, use_global_device_ids=true, to_apply=%region_5.0 | all-reduce | flops 2048 | bytes 16384 | tf_op jit(solution)/shard_map/psum | solution.py:25
  66.7 5.8 %fusion.13 = f32[1,512]{1,0:T(1,128)S(1)} fusion(f32[512,2048]{1,0:T(8,128)} %copy-done, f32[2048,1]{0,1:T(1,128)S(1)} %bitcast.30), kind=kOutput, calls=%fused_computation.25 | convolution fusion | flops 12582912 | bytes 4204544 | tf_op jit(solution)/shard_map/dot_general | solution.py:38
  72.5 2.5 psum.74
  75.0 10.3 %psum.75 = f32[512]{0:T(512)S(1)} all-reduce(f32[512]{0:T(512)S(1)} %psum.74), channel_id=1, replica_groups=mesh['dy'=4,'dz'=8,'cx'=4,'core'=2] {'cx'}, use_global_device_ids=true, to_apply=%region_7.0 | all-reduce | flops 512 | bytes 4096 | tf_op jit(solution)/shard_map/psum | solution.py:21
  85.2 4.3 %fusion.14 = f32[1,2048]{1,0:T(1,128)S(1)} fusion(f32[512,1]{0,1:T(1,128)S(1)} %bitcast.34, f32[512,2048]{1,0:T(8,128)} %copy-done), kind=kOutput, calls=%fused_computation.26 | convolution fusion | flops 12582912 | bytes 4204544 | tf_op jit(solution)/shard_map/dot_general | solution.py:58
  89.6 14.4 %psum.76 = f32[2048]{0:T(1024)S(1)} all-reduce(f32[2048]{0:T(1024)S(1)} %bitcast.31), channel_id=1, replica_groups=mesh['dy'=4,'dz'=8,'cx'=4,'core'=2] {'dz'}, use_global_device_ids=true, to_apply=%region_8.0 | all-reduce | flops 2048 | bytes 16384 | tf_op jit(solution)/shard_map/psum | solution.py:25
  104.0 7.8 %psum.77 = f32[2048]{0:T(1024)S(1)} all-reduce(f32[2048]{0:T(1024)S(1)} %psum.76), channel_id=1, replica_groups=mesh['dy'=4,'dz'=8,'cx'=4,'core'=2] {'dy'}, use_global_device_ids=true, to_apply=%region_9.0 | all-reduce | flops 2048 | bytes 16384 | tf_op jit(solution)/shard_map/psum | solution.py:25
  111.9 5.8 %fusion.15 = f32[1,512]{1,0:T(1,128)S(1)} fusion(f32[512,2048]{1,0:T(8,128)} %copy-done, f32[2048,1]{0,1:T(1,128)S(1)} %bitcast.27), kind=kOutput, calls=%fused_computation.27 | convolution fusion | flops 12582912 | bytes 4204544 | tf_op jit(solution)/shard_map/dot_general | solution.py:38
  117.6 2.5 psum.78
  120.1 7.7 %psum.79 = f32[512]{0:T(512)S(1)} all-reduce(f32[512]{0:T(512)S(1)} %psum.78), channel_id=1, replica_groups=mesh['dy'=4,'dz'=8,'cx'=4,'core'=2] {'cx'}, use_global_device_ids=true, to_apply=%region_11.0 | all-reduce | flops 512 | bytes 4096 | tf_op jit(solution)/shard_map/psum | solution.py:21
  127.8 4.2 %fusion.6 = f32[2048,768]{1,0:T(8,128)S(1)} fusion(bf16[512,768]{1,0:T(8,128)(2,1)S(1)} %copy-done.1, f32[512]{0:T(512)S(1)} %add_rsqrt_fusion.1, f32[512,2048]{1,0:T(8,128)} %copy-done, f32[2048]{0:T(1024)S(1)} %broadcast_divide_fusion.2, f32[512]{0:T(512)S(1)} %broadcast_divide_fusion.3), kind=kOutput, calls=%fused_computation.12 | convolution fusion | flops 1614938112 | bytes 11284480 | tf_op jit(solution)/shard_map/dot_general | solution.py:66
  132.0 3.3 %copy.7 = f32[8,4,64,768]{3,2,1,0:T(8,128)} copy(f32[8,4,64,768]{3,2,0,1:T(8,128)S(1)} %bitcast.25) | data formatting | bytes 12582912 | tf_op jit(solution)/shard_map/transpose | solution.py:32
  135.4 72.5 %reduce-scatter.3.cloned.1.call-done = f32[256,768]{1,0:T(8,128)} async-done(((f32[2048,768]{1,0:T(8,128)}), f32[256,768]{1,0:T(8,128)}) %reduce-scatter.3.cloned.1.call-update) | async-done | bytes 786448 | tf_op jit(solution)/shard_map/reduce_scatter | solution.py:33
  209.9 2.7 %convert_reduce_fusion = f32[2048]{0:T(1024)S(1)} fusion(f32[2048]{0:T(1024)S(1)} %broadcast_divide_fusion.2, f32[512,2048]{1,0:T(8,128)} %copy-done, f32[512]{0:T(512)S(1)} %broadcast_divide_fusion.3), kind=kLoop, calls=%fused_computation.4 | loop fusion | flops 5240832 | bytes 4212736 | tf_op jit(solution)/shard_map/reduce_sum | solution.py:64
  213.3 15.8 %all-reduce = f32[2048]{0:T(1024)S(1)} all-reduce(f32[2048]{0:T(1024)S(1)} %reshape.34), channel_id=4, replica_groups=mesh['dy'=4,'dz'=8,'cx'=4,'core'=2] {'dz'}, use_global_device_ids=true, to_apply=%region_15.0.clone | all-reduce | flops 2048 | bytes 16384
  229.2 10.4 %all-reduce.1 = f32[256]{0:T(256)S(1)} all-reduce(f32[256]{0:T(256)S(1)} %dynamic-slice.1), channel_id=5, replica_groups=mesh['dy'=4,'dz'=8,'cx'=4,'core'=2] {'dy'}, use_global_device_ids=true, to_apply=%region_16.0.clone | all-reduce | flops 256 | bytes 2048
  (28 shorter events, 4.7 us)
Async XLA Ops:
  6.5 201.4 %reduce-scatter.3.cloned.1.call-start = ((), (), s32[]{:S(2)}) async-start(), calls=%async_computation.2 | async-start | bytes 7077888 | tf_op jit(solution)/shard_map/reduce_scatter | solution.py:33
  14.6 2.0 copy-start
  85.2 42.6 %copy-start.1 = (bf16[512,768]{1,0:T(8,128)(2,1)S(1)}, bf16[512,768]{1,0:T(8,128)(2,1)}, u32[]{:S(2)}) copy-start(bf16[512,768]{1,0:T(8,128)(2,1)} %param.2) | copy-start | bytes 2359300
  135.4 72.6 %copy-start.3 = (u32[256]{0:T(256)S(1)}, u32[256]{0:T(256)}, u32[]{:S(2)}) copy-start(u32[256]{0:T(256)} %constant.21) | copy-start | bytes 3076
  135.4 73.3 %copy-start.2 = (u32[256]{0:T(256)S(1)}, u32[256]{0:T(256)}, u32[]{:S(2)}) copy-start(u32[256]{0:T(256)} %constant.17) | copy-start | bytes 3076
  135.4 104.3 %reduce-scatter.5.cloned.1.call-start = ((), (), s32[]{:S(2)}) async-start(), calls=%async_computation.3 | async-start | bytes 983040 | tf_op jit(solution)/shard_map/reduce_scatter | solution.py:34
Sparse Core Ops, SparseCore 0:
  135.5 72.3 reduce-scatter.2
  210.5 23.7 reduce-scatter.4

commit v2 on v1

--- a/solution.py
+++ b/solution.py
@@ -11,10 +11,14 @@
 entropy_regularizer = 0.05
 
 
-def normalize(values):
+def normalize_wide(values):
     wide = values.astype(jnp.float32)
     meansq = jnp.mean(wide * wide, axis=-1, keepdims=True)
-    return (wide * lax.rsqrt(meansq + 1e-06)).astype(jnp.bfloat16)
+    return wide * lax.rsqrt(meansq + 1e-06)
+
+
+def normalize(values):
+    return normalize_wide(values).astype(jnp.bfloat16)
 
 
 def cent_sum(x):
@@ -25,15 +29,6 @@
     return lax.psum(lax.psum(x, "dz"), "dy")
 
 
-def dp_scatter(x, ny, nz):
-    rows = x.shape[0] // (ny * nz)
-    rest = x.shape[1:]
-    x = x.reshape((ny, nz, rows) + rest)
-    x = jnp.swapaxes(x, 0, 1).reshape((nz * ny * rows,) + rest)
-    x = lax.psum_scatter(x, "dz", scatter_dimension=0, tiled=True)
-    return lax.psum_scatter(x, "dy", scatter_dimension=0, tiled=True)
-
-
 def row_update(boltzmann_affinity, column_factor):
     partial_rows = jnp.dot(boltzmann_affinity, column_factor, precision=lax.Precision.HIGHEST)
     return 1.0 / cent_sum(partial_rows)
@@ -42,7 +37,8 @@
 def shards(embeddings, centroids):
     ny = lax.axis_size("dy")
     nz = lax.axis_size("dz")
-    normed = normalize(embeddings)
+    scaled_rows = normalize_wide(embeddings)
+    normed = scaled_rows.astype(jnp.bfloat16)
     cent_normed = normalize(centroids)
     cosine_matches = lax.dot_general(
         normed, cent_normed, (((1,), (1,)), ((), ())), preferred_element_type=jnp.float32
@@ -58,15 +54,28 @@
         partial_cols = jnp.dot(row_weight, boltzmann_affinity, precision=lax.Precision.HIGHEST)
         column_factor = balance_ratio / dp_sum(partial_cols)
     row_weight = row_update(boltzmann_affinity, column_factor)
-    transport = (row_weight[:, None] * boltzmann_affinity * column_factor[None, :]).astype(
+    gathered = lax.all_gather(scaled_rows, "dy", axis=0, tiled=True)
+    unit = column_factor[0] * 0.0 + 1.0
+    gathered = (gathered * unit).astype(jnp.bfloat16)
+    gathered_weight = lax.all_gather(row_weight, "dy", axis=0, tiled=True)
+    sub_cents = local_cents // ny
+    start = lax.axis_index("dy") * sub_cents
+    sub_normed = lax.dynamic_slice_in_dim(cent_normed, start, sub_cents, 0)
+    sub_factor = lax.dynamic_slice_in_dim(column_factor, start, sub_cents, 0)
+    sub_matches = lax.dot_general(
+        gathered, sub_normed, (((1,), (1,)), ((), ())), preferred_element_type=jnp.float32
+    )
+    sub_affinity = jnp.exp(sub_matches * (1.0 / (FEATURE_DIM * entropy_regularizer)))
+    transport = (gathered_weight[:, None] * sub_affinity * sub_factor[None, :]).astype(
         jnp.bfloat16
     )
     col_mass = jnp.sum(transport, axis=0, dtype=jnp.float32)
-    col_mass = dp_scatter(col_mass, ny, nz)
     weighted = lax.dot_general(
-        transport, normed, (((0,), (0,)), ((), ())), preferred_element_type=jnp.float32
+        transport, gathered, (((0,), (0,)), ((), ())), preferred_element_type=jnp.float32
     )
-    weighted = dp_scatter(weighted, ny, nz)
+    weighted, col_mass = lax.psum_scatter(
+        (weighted, col_mass), "dz", scatter_dimension=0, tiled=True
+    )
     return weighted / col_mass[:, None]
 
 

time: 249 us -> 196 us (0.79)
  waiting for transfers between devices: 72.5 us -> 20.9 us
  local copies, waits for them, and re-layouts: 6.91 us -> 3.3 us
    reduce_scatter x2 -> x1, waiting for transfers between devices: 72.5 us -> 20.9 us  [shards(): lax.psum_scatter((weighted, col_mass), 'dz', scatter_dimension=0, tiled=T...]
    all_gather x0 -> x1, blocking collectives: none -> 10.4 us  [shards(): gathered_weight = lax.all_gather(row_weight, 'dy', axis=0, tiled=True)]
    unnamed x2 -> x1, blocking collectives: 26.2 us -> 16.2 us
    reduce_sum x3 -> x2, other arithmetic: 6.61 us -> 2.19 us  [normalize_wide(): meansq = jnp.mean(wide * wide, axis=-1, keepdims=True)]
    dot_general x1 -> x2, matrix products: 4.22 us -> 8.53 us  [the longest x1 5.48 us: shards(): lax.dot_general(gathered, sub_normed, (((1,), (1,)), ((), ())), preferred...]
    transpose x2 -> x0, local copies, waits for them, and re-layouts: 3.34 us -> none  [dp_scatter(): x = jnp.swapaxes(x, 0, 1).reshape((nz * ny * rows,) + rest)]
    mul x0 -> x1, other arithmetic: none -> 2.51 us  [normalize_wide(): return wide * lax.rsqrt(meansq + 1e-06)]
  transfers between devices with their start and end apart: 2 -> 2, of which waited for: 1 -> 1; matrix products, arithmetic and copies ran while one was open for 2% -> 14% of each run, Pallas kernels for 0% -> 0%
where the time goes in v2:
time: 196 us; the launch traced here: 195 us
  blocking collectives  115 us (59%)
  matrix products  34.2 us (17%)
  waiting for transfers between devices  20.9 us (11%)
  between operations  14.9 us (8%)
  other arithmetic  7.01 us (4%)
  local copies, waits for them, and re-layouts  3.3 us (2%)
    psum x4, blocking collectives, dp_sum(): return lax.psum(lax.psum(x, 'dz'), 'dy')  52.6 us
    psum x6, blocking collectives, cent_sum(): return lax.psum(lax.psum(x, 'core'), 'cx')  35.3 us
    reduce_scatter x1, waiting for transfers between devices, shards(): lax.psum_scatter((weighted, col_mass), 'dz', scatter_dimension=0, tiled=T...  20.9 us
    unnamed x1, blocking collectives  16.2 us
    dot_general x3, matrix products, row_update(): jnp.dot(boltzmann_affinity, column_factor, precision=lax.Precision.HIGHEST)  15.2 us
    all_gather x1, blocking collectives, shards(): gathered_weight = lax.all_gather(row_weight, 'dy', axis=0, tiled=True)  10.4 us
    dot_general x2, matrix products, shards(): jnp.dot(row_weight, boltzmann_affinity, precision=lax.Precision.HIGHEST)  8.53 us
    dot_general x1, matrix products, shards(): lax.dot_general(gathered, sub_normed, (((1,), (1,)), ((), ())), preferred...  5.48 us
  transfers between devices with their start and end apart: 2, of which 1 were waited for; matrix products, arithmetic and copies ran while one was open for 14% of the time, Pallas kernels for 0%

profile of v2, /device:TPU:2, one launch (start us, length us, event | category | flops | bytes accessed | tf_op | source)
XLA Modules:
  0.0 194.9 jit_solution(6867599611102098669)
XLA Ops:
  8.1 2.5 %convert_multiply_fusion.2 = f32[512,768]{1,0:T(8,128)} fusion(bf16[512,768]{1,0:T(8,128)(2,1)} %param.2, f32[512]{0:T(512)S(1)} %add_rsqrt_fusion.1), kind=kLoop, calls=%fused_computation.8 | loop fusion | flops 786432 | bytes 2361344 | tf_op jit(solution)/shard_map/mul | solution.py:17
  12.0 1.9 multiply_exponential_fusion
  13.9 2.0 %copy-done = f32[512,2048]{1,0:T(8,128)} copy-done((f32[512,2048]{1,0:T(8,128)}, f32[512,2048]{1,0:T(8,128)S(1)}, u32[]{:S(2)}) %copy-start) | copy-done | bytes 4194328
  15.9 3.6 %fusion.6 = f32[1,512]{1,0:T(1,128)S(1)} fusion(f32[512,2048]{1,0:T(8,128)S(1)} %multiply_exponential_fusion), kind=kOutput, calls=%fused_computation.16 | convolution fusion | flops 12582912 | bytes 4196352 | tf_op jit(solution)/shard_map/dot_general | solution.py:33
  19.6 2.5 %psum.70 = f32[512]{0:T(512)S(1)} all-reduce(f32[512]{0:T(512)S(1)} %bitcast.32), channel_id=1, replica_groups=mesh['dy'=4,'dz'=8,'cx'=4,'core'=2] {'core'}, use_global_device_ids=true, to_apply=%region_2.0 | all-reduce | flops 512 | bytes 4096 | tf_op jit(solution)/shard_map/psum | solution.py:25
  22.0 9.9 %psum.71 = f32[512]{0:T(512)S(1)} all-reduce(f32[512]{0:T(512)S(1)} %psum.70), channel_id=1, replica_groups=mesh['dy'=4,'dz'=8,'cx'=4,'core'=2] {'cx'}, use_global_device_ids=true, to_apply=%region_3.0 | all-reduce | flops 512 | bytes 4096 | tf_op jit(solution)/shard_map/psum | solution.py:25
  32.0 4.3 %fusion.10 = f32[1,2048]{1,0:T(1,128)S(1)} fusion(f32[512,1]{0,1:T(1,128)S(1)} %bitcast.29, f32[512,2048]{1,0:T(8,128)} %copy-done), kind=kOutput, calls=%fused_computation.26 | convolution fusion | flops 12582912 | bytes 4204544 | tf_op jit(solution)/shard_map/dot_general | solution.py:54
  36.2 18.9 %psum.72 = f32[2048]{0:T(1024)S(1)} all-reduce(f32[2048]{0:T(1024)S(1)} %bitcast.25), channel_id=1, replica_groups=mesh['dy'=4,'dz'=8,'cx'=4,'core'=2] {'dz'}, use_global_device_ids=true, to_apply=%region_4.0 | all-reduce | flops 2048 | bytes 16384 | tf_op jit(solution)/shard_map/psum | solution.py:29
  55.1 11.5 %psum.73 = f32[2048]{0:T(1024)S(1)} all-reduce(f32[2048]{0:T(1024)S(1)} %psum.72), channel_id=1, replica_groups=mesh['dy'=4,'dz'=8,'cx'=4,'core'=2] {'dy'}, use_global_device_ids=true, to_apply=%region_5.0 | all-reduce | flops 2048 | bytes 16384 | tf_op jit(solution)/shard_map/psum | solution.py:29
  66.6 5.8 %fusion.11 = f32[1,512]{1,0:T(1,128)S(1)} fusion(f32[512,2048]{1,0:T(8,128)} %copy-done, f32[2048,1]{0,1:T(1,128)S(1)} %bitcast.26), kind=kOutput, calls=%fused_computation.27 | convolution fusion | flops 12582912 | bytes 4204544 | tf_op jit(solution)/shard_map/dot_general | solution.py:33
  72.5 2.5 %psum.74 = f32[512]{0:T(512)S(1)} all-reduce(f32[512]{0:T(512)S(1)} %bitcast.30), channel_id=1, replica_groups=mesh['dy'=4,'dz'=8,'cx'=4,'core'=2] {'core'}, use_global_device_ids=true, to_apply=%region_6.0 | all-reduce | flops 512 | bytes 4096 | tf_op jit(solution)/shard_map/psum | solution.py:25
  74.9 10.2 %psum.75 = f32[512]{0:T(512)S(1)} all-reduce(f32[512]{0:T(512)S(1)} %psum.74), channel_id=1, replica_groups=mesh['dy'=4,'dz'=8,'cx'=4,'core'=2] {'cx'}, use_global_device_ids=true, to_apply=%region_7.0 | all-reduce | flops 512 | bytes 4096 | tf_op jit(solution)/shard_map/psum | solution.py:25
  85.2 4.3 %fusion.12 = f32[1,2048]{1,0:T(1,128)S(1)} fusion(f32[512,1]{0,1:T(1,128)S(1)} %bitcast.31, f32[512,2048]{1,0:T(8,128)} %copy-done), kind=kOutput, calls=%fused_computation.28 | convolution fusion | flops 12582912 | bytes 4204544 | tf_op jit(solution)/shard_map/dot_general | solution.py:54
  89.5 14.4 %psum.76 = f32[2048]{0:T(1024)S(1)} all-reduce(f32[2048]{0:T(1024)S(1)} %bitcast.27), channel_id=1, replica_groups=mesh['dy'=4,'dz'=8,'cx'=4,'core'=2] {'dz'}, use_global_device_ids=true, to_apply=%region_8.0 | all-reduce | flops 2048 | bytes 16384 | tf_op jit(solution)/shard_map/psum | solution.py:29
  103.9 7.8 %psum.77 = f32[2048]{0:T(1024)S(1)} all-reduce(f32[2048]{0:T(1024)S(1)} %psum.76), channel_id=1, replica_groups=mesh['dy'=4,'dz'=8,'cx'=4,'core'=2] {'dy'}, use_global_device_ids=true, to_apply=%region_9.0 | all-reduce | flops 2048 | bytes 16384 | tf_op jit(solution)/shard_map/psum | solution.py:29
  113.0 5.8 %fusion.13 = f32[1,512]{1,0:T(1,128)S(1)} fusion(f32[512,2048]{1,0:T(8,128)} %copy-done, f32[2048,1]{0,1:T(1,128)S(1)} %bitcast.24), kind=kOutput, calls=%fused_computation.29 | convolution fusion | flops 12582912 | bytes 4204544 | tf_op jit(solution)/shard_map/dot_general | solution.py:33
  118.7 2.5 %psum.78 = f32[512]{0:T(512)S(1)} all-reduce(f32[512]{0:T(512)S(1)} %bitcast.28), channel_id=1, replica_groups=mesh['dy'=4,'dz'=8,'cx'=4,'core'=2] {'core'}, use_global_device_ids=true, to_apply=%region_10.0 | all-reduce | flops 512 | bytes 4096 | tf_op jit(solution)/shard_map/psum | solution.py:25
  121.2 7.7 %psum.79 = f32[512]{0:T(512)S(1)} all-reduce(f32[512]{0:T(512)S(1)} %psum.78), channel_id=1, replica_groups=mesh['dy'=4,'dz'=8,'cx'=4,'core'=2] {'cx'}, use_global_device_ids=true, to_apply=%region_11.0 | all-reduce | flops 512 | bytes 4096 | tf_op jit(solution)/shard_map/psum | solution.py:25
  128.9 10.4 %all-gather = f32[4,1,512]{2,1,0:T(1,128)S(1)} all-gather(f32[1,1,512]{2,1,0:T(1,128)S(1)} %bitcast.34), channel_id=1, replica_groups=mesh['dy'=4,'dz'=8,'cx'=4,'core'=2] {'dy'}, dimensions={0}, use_global_device_ids=true | all-gather | bytes 10240 | tf_op jit(solution)/shard_map/all_gather | solution.py:60
  139.4 5.5 %convert_reduce_fusion = (f32[512]{0:T(512)S(1)}, bf16[2048,512]{1,0:T(8,128)(2,1)S(1)}) fusion(f32[512]{0:T(512)S(1)} %dynamic_slice.7, bf16[2048,768]{1,0:T(8,128)(2,1)} %copy-done.3, s32[]{:T(128)S(6)} %select_n.4, f32[2048,768]{1,0:T(8,128)} %all-gather.3.cloned.1.call-done, f32[]{:T(128)} %bitcast.11, f32[2048]{0:T(1024)S(1)} %bitcast.33), kind=kOutput, calls=%fused_computation.5 | convolution fusion | flops 1620049408 | bytes 9187844 | tf_op jit(solution)/shard_map/dot_general | solution.py:65
  144.9 3.1 %fusion.3 = f32[512,768]{1,0:T(8,128)} fusion(bf16[2048,512]{1,0:T(8,128)(2,1)S(1)} %get-tuple-element.6, f32[2048,768]{1,0:T(8,128)S(1)} %copy-done.2, f32[]{:T(128)} %bitcast.11), kind=kOutput, calls=%fused_computation.11 | convolution fusion | flops 1613758464 | bytes 9961476 | tf_op jit(solution)/shard_map/dot_general | solution.py:73
  149.2 16.2 %all-reduce = f32[512]{0:T(512)S(1)} all-reduce(f32[512]{0:T(512)S(1)} %get-tuple-element.5), channel_id=3, replica_groups=mesh['dy'=4,'dz'=8,'cx'=4,'core'=2] {'dz'}, use_global_device_ids=true, to_apply=%region_14.0.clone | all-reduce | flops 512 | bytes 4096
  165.4 20.9 %reduce-scatter.2.cloned.1.call-done = f32[64,768]{1,0:T(8,128)} async-done(((f32[512,768]{1,0:T(8,128)}), f32[64,768]{1,0:T(8,128)}) %reduce-scatter.2.cloned.1.call-update) | async-done | bytes 196624 | tf_op jit(solution)/shard_map/reduce_scatter | solution.py:76
  186.3 1.7 broadcast_divide_fusion
  (30 shorter events, 4.2 us)
Async XLA Ops:
  6.5 4.1 %copy-start.1 = (bf16[2048,768]{1,0:T(8,128)(2,1)S(1)}, bf16[2048,768]{1,0:T(8,128)(2,1)}, u32[]{:S(2)}) copy-start(bf16[2048,768]{1,0:T(8,128)(2,1)} %param.3) | copy-start | bytes 9437188
  6.5 132.8 %all-gather.3.cloned.1.call-start = ((), (), s32[]{:S(2)}) async-start(), calls=%async_computation.1 | async-start | bytes 7864320 | tf_op jit(solution)/shard_map/all_gather | solution.py:57
  10.6 175.8 %reduce-scatter.2.cloned.1.call-start = ((), (), s32[]{:S(2)}) async-start(), calls=%async_computation.2 | async-start | bytes 1769472 | tf_op jit(solution)/shard_map/reduce_scatter | solution.py:76
  10.7 1.3 copy-start.4
  12.0 1.9 copy-start.3
  13.9 2.0 %copy-start = (f32[512,2048]{1,0:T(8,128)}, f32[512,2048]{1,0:T(8,128)S(1)}, u32[]{:S(2)}) copy-start(f32[512,2048]{1,0:T(8,128)S(1)} %multiply_exponential_fusion) | copy-start | bytes 12582916
  139.4 5.5 %copy-start.2 = (f32[2048,768]{1,0:T(8,128)S(1)}, f32[2048,768]{1,0:T(8,128)}, u32[]{:S(2)}) copy-start(f32[2048,768]{1,0:T(8,128)} %all-gather.3.cloned.1.call-done) | copy-start | bytes 18874372
  144.8 3.1 %copy-start.5 = (u32[256]{0:T(256)S(1)}, u32[256]{0:T(256)}, u32[]{:S(2)}) copy-start(u32[256]{0:T(256)} %constant.35) | copy-start | bytes 3076
Sparse Core Ops, SparseCore 0:
  10.7 71.4 all-gather.2
  148.1 38.2 reduce-scatter.1

commit v3 on v2

--- a/solution.py
+++ b/solution.py
@@ -30,7 +30,7 @@
 
 
 def row_update(boltzmann_affinity, column_factor):
-    partial_rows = jnp.dot(boltzmann_affinity, column_factor, precision=lax.Precision.HIGHEST)
+    partial_rows = jnp.sum(boltzmann_affinity * column_factor[None, :], axis=1)
     return 1.0 / cent_sum(partial_rows)
 
 
@@ -51,7 +51,7 @@
     column_factor = jnp.ones((local_cents,), jnp.float32)
     for sweep in range(ROUNDS):
         row_weight = row_update(boltzmann_affinity, column_factor)
-        partial_cols = jnp.dot(row_weight, boltzmann_affinity, precision=lax.Precision.HIGHEST)
+        partial_cols = jnp.sum(row_weight[:, None] * boltzmann_affinity, axis=0)
         column_factor = balance_ratio / dp_sum(partial_cols)
     row_weight = row_update(boltzmann_affinity, column_factor)
     gathered = lax.all_gather(scaled_rows, "dy", axis=0, tiled=True)

time: 196 us -> 182 us (0.929)
  matrix products: 34.2 us -> 12.5 us
  other arithmetic: 7.01 us -> 17.7 us
  local copies, waits for them, and re-layouts: 3.3 us -> 1.27 us
    dot_general x5 -> x0, matrix products: 23.7 us -> none  [the longest x3 15.2 us: row_update(): jnp.dot(boltzmann_affinity, column_factor, precision=lax.Precision.HIGHEST)]
    reduce_sum x0 -> x4, other arithmetic: none -> 10.6 us  [the longest x2 5.48 us: shards(): partial_cols = jnp.sum(row_weight[:, None] * boltzmann_affinity, axis=0)]
    dot_general x1, matrix products: 1.91 us -> 3.97 us  [shards(): lax.dot_general(normed, cent_normed, (((1,), (1,)), ((), ())), preferred_...]
    unnamed x14 -> x12, local copies, waits for them, and re-layouts: 2.71 us -> 0.69 us
  transfers between devices with their start and end apart: 2 -> 2, of which waited for: 1 -> 1; matrix products, arithmetic and copies ran while one was open for 14% -> 9% of each run, Pallas kernels for 0% -> 0%
where the time goes in v3:
time: 182 us; the launch traced here: 181 us
  blocking collectives  114 us (63%)
  waiting for transfers between devices  20.9 us (11%)
  other arithmetic  17.7 us (10%)
  between operations  14.9 us (8%)
  matrix products  12.5 us (7%)
    psum x4, blocking collectives, dp_sum(): return lax.psum(lax.psum(x, 'dz'), 'dy')  52.3 us
    psum x6, blocking collectives, cent_sum(): return lax.psum(lax.psum(x, 'core'), 'cx')  35.1 us
    reduce_scatter x1, waiting for transfers between devices, shards(): lax.psum_scatter((weighted, col_mass), 'dz', scatter_dimension=0, tiled=T...  20.8 us
    unnamed x1, blocking collectives  16.2 us
    all_gather x1, blocking collectives, shards(): gathered_weight = lax.all_gather(row_weight, 'dy', axis=0, tiled=True)  10.4 us
    dot_general x1, matrix products, shards(): lax.dot_general(gathered, sub_normed, (((1,), (1,)), ((), ())), preferred...  5.49 us
    reduce_sum x2, other arithmetic, shards(): partial_cols = jnp.sum(row_weight[:, None] * boltzmann_affinity, axis=0)  5.48 us
    reduce_sum x2, other arithmetic, row_update(): partial_rows = jnp.sum(boltzmann_affinity * column_factor[None, :], axis=1)  5.17 us
  transfers between devices with their start and end apart: 2, of which 1 were waited for; matrix products, arithmetic and copies ran while one was open for 9% of the time, Pallas kernels for 0%

profile of v3, /device:TPU:2, one launch (start us, length us, event | category | flops | bytes accessed | tf_op | source)
XLA Modules:
  0.0 181.2 jit_solution(13451332309466661559)
XLA Ops:
  6.5 1.5 fusion.2
  8.1 2.5 %convert_multiply_fusion.2 = f32[512,768]{1,0:T(8,128)} fusion(bf16[512,768]{1,0:T(8,128)(2,1)} %param.2, f32[512]{0:T(512)S(1)} %add_rsqrt_fusion.1), kind=kLoop, calls=%fused_computation.12 | loop fusion | flops 786432 | bytes 2361344 | tf_op jit(solution)/shard_map/mul | solution.py:17
  10.7 0.7 fusion
  12.0 4.0 %fusion.7 = (f32[512]{0:T(512)S(1)}, f32[512,2048]{1,0:T(8,128)}) fusion(bf16[2048,768]{1,0:T(8,128)(2,1)S(1)} %fusion.1, f32[512]{0:T(512)S(1)} %add_rsqrt_fusion.1, bf16[512,768]{1,0:T(8,128)(2,1)S(1)} %copy-done.3), kind=kOutput, calls=%fused_computation.27 | convolution fusion | flops 1613889024 | bytes 8130560 | tf_op jit(solution)/shard_map/dot_general | solution.py:43
  16.0 2.4 %psum.70 = f32[512]{0:T(512)S(1)} all-reduce(f32[512]{0:T(512)S(1)} %get-tuple-element.5), channel_id=1, replica_groups=mesh['dy'=4,'dz'=8,'cx'=4,'core'=2] {'core'}, use_global_device_ids=true, to_apply=%region_3.0 | all-reduce | flops 512 | bytes 4096 | tf_op jit(solution)/shard_map/psum | solution.py:25
  18.4 9.9 %psum.71 = f32[512]{0:T(512)S(1)} all-reduce(f32[512]{0:T(512)S(1)} %psum.70), channel_id=1, replica_groups=mesh['dy'=4,'dz'=8,'cx'=4,'core'=2] {'cx'}, use_global_device_ids=true, to_apply=%region_4.0 | all-reduce | flops 512 | bytes 4096 | tf_op jit(solution)/shard_map/psum | solution.py:25
  28.3 2.9 %multiply_reduce_fusion.3 = f32[2048]{0:T(1024)S(1)} fusion(f32[512,2048]{1,0:T(8,128)} %get-tuple-element.6, f32[512]{0:T(512)S(1)} %broadcast_divide_fusion.5), kind=kLoop, calls=%fused_computation.10 | loop fusion | flops 2095104 | bytes 4204544 | tf_op jit(solution)/shard_map/reduce_sum | solution.py:54
  31.3 18.7 %psum.72 = f32[2048]{0:T(1024)S(1)} all-reduce(f32[2048]{0:T(1024)S(1)} %multiply_reduce_fusion.3), channel_id=1, replica_groups=mesh['dy'=4,'dz'=8,'cx'=4,'core'=2] {'dz'}, use_global_device_ids=true, to_apply=%region_6.0 | all-reduce | flops 2048 | bytes 16384 | tf_op jit(solution)/shard_map/psum | solution.py:29
  50.0 11.4 %psum.73 = f32[2048]{0:T(1024)S(1)} all-reduce(f32[2048]{0:T(1024)S(1)} %psum.72), channel_id=1, replica_groups=mesh['dy'=4,'dz'=8,'cx'=4,'core'=2] {'dy'}, use_global_device_ids=true, to_apply=%region_7.0 | all-reduce | flops 2048 | bytes 16384 | tf_op jit(solution)/shard_map/psum | solution.py:29
  61.4 2.6 %multiply_reduce_fusion.2 = f32[512]{0:T(512)S(1)} fusion(f32[512,2048]{1,0:T(8,128)} %get-tuple-element.6, f32[2048]{0:T(1024)S(1)} %broadcast_divide_fusion.2), kind=kLoop, calls=%fused_computation.9 | loop fusion | flops 2096640 | bytes 4204544 | tf_op jit(solution)/shard_map/reduce_sum | solution.py:33
  64.0 2.5 %psum.74 = f32[512]{0:T(512)S(1)} all-reduce(f32[512]{0:T(512)S(1)} %multiply_reduce_fusion.2), channel_id=1, replica_groups=mesh['dy'=4,'dz'=8,'cx'=4,'core'=2] {'core'}, use_global_device_ids=true, to_apply=%region_9.0 | all-reduce | flops 512 | bytes 4096 | tf_op jit(solution)/shard_map/psum | solution.py:25
  66.5 9.9 %psum.75 = f32[512]{0:T(512)S(1)} all-reduce(f32[512]{0:T(512)S(1)} %psum.74), channel_id=1, replica_groups=mesh['dy'=4,'dz'=8,'cx'=4,'core'=2] {'cx'}, use_global_device_ids=true, to_apply=%region_10.0 | all-reduce | flops 512 | bytes 4096 | tf_op jit(solution)/shard_map/psum | solution.py:25
  76.4 2.5 %multiply_reduce_fusion.1 = f32[2048]{0:T(1024)S(1)} fusion(f32[512,2048]{1,0:T(8,128)} %get-tuple-element.6, f32[512]{0:T(512)S(1)} %broadcast_divide_fusion.4), kind=kLoop, calls=%fused_computation.8 | loop fusion | flops 2095104 | bytes 4204544 | tf_op jit(solution)/shard_map/reduce_sum | solution.py:54
  79.0 14.4 %psum.76 = f32[2048]{0:T(1024)S(1)} all-reduce(f32[2048]{0:T(1024)S(1)} %multiply_reduce_fusion.1), channel_id=1, replica_groups=mesh['dy'=4,'dz'=8,'cx'=4,'core'=2] {'dz'}, use_global_device_ids=true, to_apply=%region_12.0 | all-reduce | flops 2048 | bytes 16384 | tf_op jit(solution)/shard_map/psum | solution.py:29
  93.4 7.8 %psum.77 = f32[2048]{0:T(1024)S(1)} all-reduce(f32[2048]{0:T(1024)S(1)} %psum.76), channel_id=1, replica_groups=mesh['dy'=4,'dz'=8,'cx'=4,'core'=2] {'dy'}, use_global_device_ids=true, to_apply=%region_13.0 | all-reduce | flops 2048 | bytes 16384 | tf_op jit(solution)/shard_map/psum | solution.py:29
  102.5 2.5 %multiply_reduce_fusion = f32[512]{0:T(512)S(1)} fusion(f32[512,2048]{1,0:T(8,128)} %get-tuple-element.6, f32[2048]{0:T(1024)S(1)} %broadcast_divide_fusion.1), kind=kLoop, calls=%fused_computation.7 | loop fusion | flops 2096640 | bytes 4204544 | tf_op jit(solution)/shard_map/reduce_sum | solution.py:33
  105.1 2.5 %psum.78 = f32[512]{0:T(512)S(1)} all-reduce(f32[512]{0:T(512)S(1)} %multiply_reduce_fusion), channel_id=1, replica_groups=mesh['dy'=4,'dz'=8,'cx'=4,'core'=2] {'core'}, use_global_device_ids=true, to_apply=%region_15.0 | all-reduce | flops 512 | bytes 4096 | tf_op jit(solution)/shard_map/psum | solution.py:25
  107.5 7.8 %psum.79 = f32[512]{0:T(512)S(1)} all-reduce(f32[512]{0:T(512)S(1)} %psum.78), channel_id=1, replica_groups=mesh['dy'=4,'dz'=8,'cx'=4,'core'=2] {'cx'}, use_global_device_ids=true, to_apply=%region_16.0 | all-reduce | flops 512 | bytes 4096 | tf_op jit(solution)/shard_map/psum | solution.py:25
  115.3 10.4 %all-gather = f32[4,1,512]{2,1,0:T(1,128)S(1)} all-gather(f32[1,1,512]{2,1,0:T(1,128)S(1)} %bitcast.7), channel_id=1, replica_groups=mesh['dy'=4,'dz'=8,'cx'=4,'core'=2] {'dy'}, dimensions={0}, use_global_device_ids=true | all-gather | bytes 10240 | tf_op jit(solution)/shard_map/all_gather | solution.py:60
  125.8 5.5 %convert_reduce_fusion = (f32[512]{0:T(512)S(1)}, bf16[2048,512]{1,0:T(8,128)(2,1)S(1)}) fusion(f32[512]{0:T(512)S(1)} %dynamic_slice.7, bf16[2048,768]{1,0:T(8,128)(2,1)} %copy-done.2, s32[]{:T(128)S(6)} %select_n.4, f32[2048,768]{1,0:T(8,128)} %all-gather.3.cloned.1.call-done, f32[]{:T(128)} %bitcast.2, f32[2048]{0:T(1024)S(1)} %bitcast.6), kind=kOutput, calls=%fused_computation.5 | convolution fusion | flops 1620049408 | bytes 9187844 | tf_op jit(solution)/shard_map/dot_general | solution.py:65
  131.3 3.1 %fusion.3 = f32[512,768]{1,0:T(8,128)} fusion(bf16[2048,512]{1,0:T(8,128)(2,1)S(1)} %get-tuple-element.8, f32[2048,768]{1,0:T(8,128)S(1)} %copy-done.1, f32[]{:T(128)} %bitcast.2), kind=kOutput, calls=%fused_computation.15 | convolution fusion | flops 1613758464 | bytes 9961476 | tf_op jit(solution)/shard_map/dot_general | solution.py:73
  135.6 16.2 %all-reduce = f32[512]{0:T(512)S(1)} all-reduce(f32[512]{0:T(512)S(1)} %get-tuple-element.7), channel_id=3, replica_groups=mesh['dy'=4,'dz'=8,'cx'=4,'core'=2] {'dz'}, use_global_device_ids=true, to_apply=%region_19.0.clone | all-reduce | flops 512 | bytes 4096
  151.9 20.8 %reduce-scatter.2.cloned.1.call-done = f32[64,768]{1,0:T(8,128)} async-done(((f32[512,768]{1,0:T(8,128)}), f32[64,768]{1,0:T(8,128)}) %reduce-scatter.2.cloned.1.call-update) | async-done | bytes 196624 | tf_op jit(solution)/shard_map/reduce_scatter | solution.py:76
  172.7 1.7 broadcast_divide_fusion
  (27 shorter events, 2.0 us)
Async XLA Ops:
  6.5 4.1 %copy-start = (bf16[2048,768]{1,0:T(8,128)(2,1)S(1)}, bf16[2048,768]{1,0:T(8,128)(2,1)}, u32[]{:S(2)}) copy-start(bf16[2048,768]{1,0:T(8,128)(2,1)} %param.3) | copy-start | bytes 9437188
  6.5 119.2 %all-gather.3.cloned.1.call-start = ((), (), s32[]{:S(2)}) async-start(), calls=%async_computation.1 | async-start | bytes 7864320 | tf_op jit(solution)/shard_map/all_gather | solution.py:57
  10.6 162.1 %reduce-scatter.2.cloned.1.call-start = ((), (), s32[]{:S(2)}) async-start(), calls=%async_computation.2 | async-start | bytes 1769472 | tf_op jit(solution)/shard_map/reduce_scatter | solution.py:76
  10.7 1.3 copy-start.3
  12.0 4.0 %copy-start.2 = (bf16[2048,768]{1,0:T(8,128)(2,1)}, bf16[2048,768]{1,0:T(8,128)(2,1)S(1)}, u32[]{:S(2)}) copy-start(bf16[2048,768]{1,0:T(8,128)(2,1)S(1)} %fusion.1) | copy-start | bytes 9437188
  125.8 5.5 %copy-start.1 = (f32[2048,768]{1,0:T(8,128)S(1)}, f32[2048,768]{1,0:T(8,128)}, u32[]{:S(2)}) copy-start(f32[2048,768]{1,0:T(8,128)} %all-gather.3.cloned.1.call-done) | copy-start | bytes 18874372
  131.3 3.1 %copy-start.4 = (u32[256]{0:T(256)S(1)}, u32[256]{0:T(256)}, u32[]{:S(2)}) copy-start(u32[256]{0:T(256)} %constant.35) | copy-start | bytes 3076
Sparse Core Ops, SparseCore 0:
  10.7 71.4 all-gather.2
  134.5 38.1 reduce-scatter.1

commit v4 on v3

--- a/solution.py
+++ b/solution.py
@@ -53,11 +53,9 @@
         row_weight = row_update(boltzmann_affinity, column_factor)
         partial_cols = jnp.sum(row_weight[:, None] * boltzmann_affinity, axis=0)
         column_factor = balance_ratio / dp_sum(partial_cols)
-    row_weight = row_update(boltzmann_affinity, column_factor)
-    gathered = lax.all_gather(scaled_rows, "dy", axis=0, tiled=True)
-    unit = column_factor[0] * 0.0 + 1.0
-    gathered = (gathered * unit).astype(jnp.bfloat16)
-    gathered_weight = lax.all_gather(row_weight, "dy", axis=0, tiled=True)
+    scaled_all = lax.all_gather(scaled_rows, "dy", axis=0, tiled=True)
+    unit = scaled_rows[0, 0] * 0.0 + 1.0
+    gathered = (scaled_all * unit).astype(jnp.bfloat16)
     sub_cents = local_cents // ny
     start = lax.axis_index("dy") * sub_cents
     sub_normed = lax.dynamic_slice_in_dim(cent_normed, start, sub_cents, 0)
@@ -66,6 +64,8 @@
         gathered, sub_normed, (((1,), (1,)), ((), ())), preferred_element_type=jnp.float32
     )
     sub_affinity = jnp.exp(sub_matches * (1.0 / (FEATURE_DIM * entropy_regularizer)))
+    sub_rows = jnp.sum(sub_affinity * sub_factor[None, :], axis=1)
+    gathered_weight = 1.0 / lax.psum(cent_sum(sub_rows), "dy")
     transport = (gathered_weight[:, None] * sub_affinity * sub_factor[None, :]).astype(
         jnp.bfloat16
     )

time: 182 us -> 184 us (1.011)
  matrix products: 12.5 us -> 18.4 us
  waiting for transfers between devices: 20.9 us -> 16.4 us
    all_gather x1 -> x0, blocking collectives: 10.4 us -> none  [shards(): gathered_weight = lax.all_gather(row_weight, 'dy', axis=0, tiled=True)]
    psum x0 -> x1, blocking collectives: none -> 9.86 us  [shards(): gathered_weight = 1.0 / lax.psum(cent_sum(sub_rows), 'dy')]
    reduce_scatter x1, waiting for transfers between devices: 20.8 us -> 16.4 us  [shards(): lax.psum_scatter((weighted, col_mass), 'dz', scatter_dimension=0, tiled=T...]
    dot_general x1, matrix products: 3.05 us -> 7.25 us  [shards(): lax.dot_general(transport, gathered, (((0,), (0,)), ((), ())), preferred_...]
    reduce_sum x0 -> x1, other arithmetic: none -> 3.05 us  [shards(): col_mass = jnp.sum(transport, axis=0, dtype=jnp.float32)]
    reduce_sum x2 -> x1, other arithmetic: 5.17 us -> 2.58 us  [row_update(): partial_rows = jnp.sum(boltzmann_affinity * column_factor[None, :], axis=1)]
  transfers between devices with their start and end apart: 2 -> 2, of which waited for: 1 -> 1; matrix products, arithmetic and copies ran while one was open for 9% -> 10% of each run, Pallas kernels for 0% -> 0%
where the time goes in v4:
time: 184 us; the launch traced here: 183 us
  blocking collectives  114 us (62%)
  matrix products  18.4 us (10%)
  other arithmetic  17.8 us (10%)
  waiting for transfers between devices  16.4 us (9%)
  between operations  14.9 us (8%)
  local copies, waits for them, and re-layouts  1.87 us (1%)
    psum x4, blocking collectives, dp_sum(): return lax.psum(lax.psum(x, 'dz'), 'dy')  52.6 us
    psum x6, blocking collectives, cent_sum(): return lax.psum(lax.psum(x, 'core'), 'cx')  35.3 us
    reduce_scatter x1, waiting for transfers between devices, shards(): lax.psum_scatter((weighted, col_mass), 'dz', scatter_dimension=0, tiled=T...  16.4 us
    unnamed x1, blocking collectives  16.2 us
    psum x1, blocking collectives, shards(): gathered_weight = 1.0 / lax.psum(cent_sum(sub_rows), 'dy')  9.86 us
    dot_general x1, matrix products, shards(): lax.dot_general(transport, gathered, (((0,), (0,)), ((), ())), preferred_...  7.25 us
    dot_general x1, matrix products, shards(): lax.dot_general(gathered, sub_normed, (((1,), (1,)), ((), ())), preferred...  7.18 us
    reduce_sum x2, other arithmetic, shards(): partial_cols = jnp.sum(row_weight[:, None] * boltzmann_affinity, axis=0)  5.12 us
  transfers between devices with their start and end apart: 2, of which 1 were waited for; matrix products, arithmetic and copies ran while one was open for 10% of the time, Pallas kernels for 0%

profile of v4, /device:TPU:2, one launch (start us, length us, event | category | flops | bytes accessed | tf_op | source)
XLA Modules:
  0.0 183.3 jit_solution(3839484986110184235)
XLA Ops:
  6.5 1.5 fusion.2
  8.1 2.5 %convert_multiply_fusion.2 = f32[512,768]{1,0:T(8,128)} fusion(bf16[512,768]{1,0:T(8,128)(2,1)} %param.2, f32[512]{0:T(512)S(1)} %add_rsqrt_fusion.1), kind=kLoop, calls=%fused_computation.13 | loop fusion | flops 786432 | bytes 2361344 | tf_op jit(solution)/shard_map/mul | solution.py:17
  10.6 1.2 slice.4
  13.8 4.0 %fusion.8 = (f32[512]{0:T(512)S(1)}, f32[512,2048]{1,0:T(8,128)}) fusion(bf16[2048,768]{1,0:T(8,128)(2,1)S(1)} %fusion.1, f32[512]{0:T(512)S(1)} %add_rsqrt_fusion.1, bf16[512,768]{1,0:T(8,128)(2,1)S(1)} %copy-done.2), kind=kOutput, calls=%fused_computation.29 | convolution fusion | flops 1613889024 | bytes 8130560 | tf_op jit(solution)/shard_map/dot_general | solution.py:43
  17.8 2.4 %psum.77 = f32[512]{0:T(512)S(1)} all-reduce(f32[512]{0:T(512)S(1)} %get-tuple-element.5), channel_id=1, replica_groups=mesh['dy'=4,'dz'=8,'cx'=4,'core'=2] {'core'}, use_global_device_ids=true, to_apply=%region_3.0 | all-reduce | flops 512 | bytes 4096 | tf_op jit(solution)/shard_map/psum | solution.py:25
  20.2 9.9 %psum.78 = f32[512]{0:T(512)S(1)} all-reduce(f32[512]{0:T(512)S(1)} %psum.77), channel_id=1, replica_groups=mesh['dy'=4,'dz'=8,'cx'=4,'core'=2] {'cx'}, use_global_device_ids=true, to_apply=%region_4.0 | all-reduce | flops 512 | bytes 4096 | tf_op jit(solution)/shard_map/psum | solution.py:25
  30.2 2.6 %multiply_reduce_fusion.3 = f32[2048]{0:T(1024)S(1)} fusion(f32[512,2048]{1,0:T(8,128)} %get-tuple-element.6, f32[512]{0:T(512)S(1)} %broadcast_divide_fusion.4), kind=kLoop, calls=%fused_computation.10 | loop fusion | flops 2095104 | bytes 4204544 | tf_op jit(solution)/shard_map/reduce_sum | solution.py:54
  32.8 18.9 %psum.79 = f32[2048]{0:T(1024)S(1)} all-reduce(f32[2048]{0:T(1024)S(1)} %multiply_reduce_fusion.3), channel_id=1, replica_groups=mesh['dy'=4,'dz'=8,'cx'=4,'core'=2] {'dz'}, use_global_device_ids=true, to_apply=%region_6.0 | all-reduce | flops 2048 | bytes 16384 | tf_op jit(solution)/shard_map/psum | solution.py:29
  51.6 11.5 %psum.80 = f32[2048]{0:T(1024)S(1)} all-reduce(f32[2048]{0:T(1024)S(1)} %psum.79), channel_id=1, replica_groups=mesh['dy'=4,'dz'=8,'cx'=4,'core'=2] {'dy'}, use_global_device_ids=true, to_apply=%region_7.0 | all-reduce | flops 2048 | bytes 16384 | tf_op jit(solution)/shard_map/psum | solution.py:29
  63.1 2.6 %multiply_reduce_fusion.2 = f32[512]{0:T(512)S(1)} fusion(f32[512,2048]{1,0:T(8,128)} %get-tuple-element.6, f32[2048]{0:T(1024)S(1)} %broadcast_divide_fusion.2), kind=kLoop, calls=%fused_computation.9 | loop fusion | flops 2096640 | bytes 4204544 | tf_op jit(solution)/shard_map/reduce_sum | solution.py:33
  65.7 2.5 %psum.81 = f32[512]{0:T(512)S(1)} all-reduce(f32[512]{0:T(512)S(1)} %multiply_reduce_fusion.2), channel_id=1, replica_groups=mesh['dy'=4,'dz'=8,'cx'=4,'core'=2] {'core'}, use_global_device_ids=true, to_apply=%region_9.0 | all-reduce | flops 512 | bytes 4096 | tf_op jit(solution)/shard_map/psum | solution.py:25
  68.2 10.1 %psum.82 = f32[512]{0:T(512)S(1)} all-reduce(f32[512]{0:T(512)S(1)} %psum.81), channel_id=1, replica_groups=mesh['dy'=4,'dz'=8,'cx'=4,'core'=2] {'cx'}, use_global_device_ids=true, to_apply=%region_10.0 | all-reduce | flops 512 | bytes 4096 | tf_op jit(solution)/shard_map/psum | solution.py:25
  78.3 2.5 %multiply_reduce_fusion.1 = f32[2048]{0:T(1024)S(1)} fusion(f32[512,2048]{1,0:T(8,128)} %get-tuple-element.6, f32[512]{0:T(512)S(1)} %broadcast_divide_fusion.3), kind=kLoop, calls=%fused_computation.8 | loop fusion | flops 2095104 | bytes 4204544 | tf_op jit(solution)/shard_map/reduce_sum | solution.py:54
  80.9 14.4 %psum.83 = f32[2048]{0:T(1024)S(1)} all-reduce(f32[2048]{0:T(1024)S(1)} %multiply_reduce_fusion.1), channel_id=1, replica_groups=mesh['dy'=4,'dz'=8,'cx'=4,'core'=2] {'dz'}, use_global_device_ids=true, to_apply=%region_12.0 | all-reduce | flops 2048 | bytes 16384 | tf_op jit(solution)/shard_map/psum | solution.py:29
  95.3 7.8 %psum.84 = f32[2048]{0:T(1024)S(1)} all-reduce(f32[2048]{0:T(1024)S(1)} %psum.83), channel_id=1, replica_groups=mesh['dy'=4,'dz'=8,'cx'=4,'core'=2] {'dy'}, use_global_device_ids=true, to_apply=%region_13.0 | all-reduce | flops 2048 | bytes 16384 | tf_op jit(solution)/shard_map/psum | solution.py:29
  103.2 7.2 %multiply_reduce_fusion = (f32[2048]{0:T(1024)S(1)}, f32[2048,512]{1,0:T(8,128)}) fusion(f32[512]{0:T(512)S(1)} %dynamic-slice_divide_fusion, bf16[2048,768]{1,0:T(8,128)(2,1)} %copy-done.1, s32[]{:T(128)S(6)} %select_n.4, f32[2048,768]{1,0:T(8,128)} %all-gather.2.cloned.1.call-done, f32[]{:T(128)} %bitcast), kind=kOutput, calls=%fused_computation.7 | convolution fusion | flops 1616902144 | bytes 11282948 | tf_op jit(solution)/shard_map/dot_general | solution.py:63
  110.4 2.5 %psum.85 = f32[2048]{0:T(1024)S(1)} all-reduce(f32[2048]{0:T(1024)S(1)} %get-tuple-element.7), channel_id=1, replica_groups=mesh['dy'=4,'dz'=8,'cx'=4,'core'=2] {'core'}, use_global_device_ids=true, to_apply=%region_15.0 | all-reduce | flops 2048 | bytes 16384 | tf_op jit(solution)/shard_map/psum | solution.py:25
  112.9 7.8 %psum.86 = f32[2048]{0:T(1024)S(1)} all-reduce(f32[2048]{0:T(1024)S(1)} %psum.85), channel_id=1, replica_groups=mesh['dy'=4,'dz'=8,'cx'=4,'core'=2] {'cx'}, use_global_device_ids=true, to_apply=%region_16.0 | all-reduce | flops 2048 | bytes 16384 | tf_op jit(solution)/shard_map/psum | solution.py:25
  120.7 9.9 %psum.87 = f32[2048]{0:T(1024)S(1)} all-reduce(f32[2048]{0:T(1024)S(1)} %psum.86), channel_id=1, replica_groups=mesh['dy'=4,'dz'=8,'cx'=4,'core'=2] {'dy'}, use_global_device_ids=true, to_apply=%region_17.0 | all-reduce | flops 2048 | bytes 16384 | tf_op jit(solution)/shard_map/psum | solution.py:68
  130.6 7.3 %fusion.3 = f32[512,768]{1,0:T(8,128)} fusion(f32[2048,768]{1,0:T(8,128)} %all-gather.2.cloned.1.call-done, f32[]{:T(128)} %bitcast, f32[2048,512]{1,0:T(8,128)} %get-tuple-element.8, f32[2048]{0:T(1024)S(1)} %broadcast_divide_fusion.1, f32[512]{0:T(512)S(1)} %dynamic-slice_divide_fusion), kind=kOutput, calls=%fused_computation.16 | convolution fusion | flops 1617952768 | bytes 12068868 | tf_op jit(solution)/shard_map/dot_general | solution.py:73
  139.1 3.0 %convert_reduce_fusion = f32[512]{0:T(512)S(1)} fusion(f32[512]{0:T(512)S(1)} %dynamic-slice_divide_fusion, f32[2048,512]{1,0:T(8,128)} %get-tuple-element.8, f32[2048]{0:T(1024)S(1)} %broadcast_divide_fusion.1), kind=kLoop, calls=%fused_computation.5 | loop fusion | flops 6290944 | bytes 4206592 | tf_op jit(solution)/shard_map/reduce_sum | solution.py:72
  142.2 16.2 %all-reduce = f32[512]{0:T(512)S(1)} all-reduce(f32[512]{0:T(512)S(1)} %convert_reduce_fusion), channel_id=3, replica_groups=mesh['dy'=4,'dz'=8,'cx'=4,'core'=2] {'dz'}, use_global_device_ids=true, to_apply=%region_20.0.clone | all-reduce | flops 512 | bytes 4096
  158.5 16.4 %reduce-scatter.2.cloned.1.call-done = f32[64,768]{1,0:T(8,128)} async-done(((f32[512,768]{1,0:T(8,128)}), f32[64,768]{1,0:T(8,128)}) %reduce-scatter.2.cloned.1.call-update) | async-done | bytes 196624 | tf_op jit(solution)/shard_map/reduce_scatter | solution.py:76
  174.8 1.7 broadcast_divide_fusion
  (24 shorter events, 2.1 us)
Async XLA Ops:
  6.5 6.0 %copy-start = (bf16[2048,768]{1,0:T(8,128)(2,1)S(1)}, bf16[2048,768]{1,0:T(8,128)(2,1)}, u32[]{:S(2)}) copy-start(bf16[2048,768]{1,0:T(8,128)(2,1)} %param.3) | copy-start | bytes 9437188
  6.5 96.7 %all-gather.2.cloned.1.call-start = ((), (), s32[]{:S(2)}) async-start(), calls=%async_computation.1 | async-start | bytes 7864320 | tf_op jit(solution)/shard_map/all_gather | solution.py:56
  10.6 164.2 %reduce-scatter.2.cloned.1.call-start = ((), (), s32[]{:S(2)}) async-start(), calls=%async_computation.2 | async-start | bytes 1769472 | tf_op jit(solution)/shard_map/reduce_scatter | solution.py:76
  12.5 1.3 copy-start.2
  13.8 4.0 %copy-start.1 = (bf16[2048,768]{1,0:T(8,128)(2,1)}, bf16[2048,768]{1,0:T(8,128)(2,1)S(1)}, u32[]{:S(2)}) copy-start(bf16[2048,768]{1,0:T(8,128)(2,1)S(1)} %fusion.1) | copy-start | bytes 9437188
  130.6 7.3 %copy-start.3 = (u32[256]{0:T(256)S(1)}, u32[256]{0:T(256)}, u32[]{:S(2)}) copy-start(u32[256]{0:T(256)} %constant.35) | copy-start | bytes 3076
Sparse Core Ops, SparseCore 0:
  10.7 71.4 all-gather.1
  138.0 36.7 reduce-scatter.1

commit v5 on v3

--- a/solution.py
+++ b/solution.py
@@ -22,7 +22,13 @@
 
 
 def cent_sum(x):
-    return lax.psum(lax.psum(x, "core"), "cx")
+    n = lax.axis_size("cx") * lax.axis_size("core")
+    step = 1
+    while step < n:
+        pairs = [(i, i ^ step) for i in range(n)]
+        x = x + lax.ppermute(x, ("cx", "core"), pairs)
+        step *= 2
+    return x
 
 
 def dp_sum(x):

time: 182 us -> 171 us (0.940)
  blocking collectives: 114 us -> 80.5 us
  waiting for transfers between devices: 20.9 us -> 40.8 us
  starting transfers between devices: 0.04 us -> 9.8 us
  other arithmetic: 17.7 us -> 13 us
  matrix products: 12.5 us -> 10.6 us
    psum x6 -> x0, blocking collectives: 35.1 us -> none  [cent_sum(): return lax.psum(lax.psum(x, 'core'), 'cx')]
    ppermute x0 -> x9, waiting for transfers between devices: none -> 19 us  [cent_sum(): x = x + lax.ppermute(x, ('cx', 'core'), pairs)]
    ppermute x0 -> x9, starting transfers between devices: none -> 9.76 us  [cent_sum(): x = x + lax.ppermute(x, ('cx', 'core'), pairs)]
    reduce_sum x2, other arithmetic: 5.48 us -> 0.71 us  [shards(): partial_cols = jnp.sum(row_weight[:, None] * boltzmann_affinity, axis=0)]
    dot_general x1, matrix products: 3.97 us -> 2.03 us  [shards(): lax.dot_general(normed, cent_normed, (((1,), (1,)), ((), ())), preferred_...]
  transfers between devices with their start and end apart: 2 -> 11, of which waited for: 1 -> 10; matrix products, arithmetic and copies ran while one was open for 9% -> 6% of each run, Pallas kernels for 0% -> 0%
where the time goes in v5:
time: 171 us
  blocking collectives  80.5 us (47%)
  waiting for transfers between devices  40.8 us (24%)
  between operations  14.9 us (9%)
  other arithmetic  13 us (8%)
  matrix products  10.6 us (6%)
  starting transfers between devices  9.8 us (6%)
    psum x4, blocking collectives, dp_sum(): return lax.psum(lax.psum(x, 'dz'), 'dy')  53.7 us
    reduce_scatter x1, waiting for transfers between devices, shards(): lax.psum_scatter((weighted, col_mass), 'dz', scatter_dimension=0, tiled=T...  21.8 us
    ppermute x9, waiting for transfers between devices, cent_sum(): x = x + lax.ppermute(x, ('cx', 'core'), pairs)  19 us
    unnamed x1, blocking collectives  16.2 us
    all_gather x1, blocking collectives, shards(): gathered_weight = lax.all_gather(row_weight, 'dy', axis=0, tiled=True)  10.6 us
    ppermute x9, starting transfers between devices, cent_sum(): x = x + lax.ppermute(x, ('cx', 'core'), pairs)  9.76 us
    dot_general x1, matrix products, shards(): lax.dot_general(gathered, sub_normed, (((1,), (1,)), ((), ())), preferred...  5.48 us
    reduce_sum x2, other arithmetic, row_update(): partial_rows = jnp.sum(boltzmann_affinity * column_factor[None, :], axis=1)  5.25 us
  transfers between devices with their start and end apart: 11, of which 10 were waited for; matrix products, arithmetic and copies ran while one was open for 6% of the time, Pallas kernels for 0%

profile of v5, /device:TPU:2, one launch (start us, length us, event | category | flops | bytes accessed | tf_op | source)
XLA Modules:
  0.0 170.9 jit_solution(9029280698614667426)
XLA Ops:
  8.1 2.5 %convert_multiply_fusion.2 = f32[512,768]{1,0:T(8,128)} fusion(bf16[512,768]{1,0:T(8,128)(2,1)} %param.2, f32[512]{0:T(512)S(1)} %add_rsqrt_fusion.1), kind=kLoop, calls=%fused_computation.12 | loop fusion | flops 786432 | bytes 2361344 | tf_op jit(solution)/shard_map/mul | solution.py:17
  12.0 2.0 %fusion.7 = (f32[512]{0:T(512)S(1)}, f32[512,2048]{1,0:T(8,128)S(1)}) fusion(bf16[2048,768]{1,0:T(8,128)(2,1)S(1)} %fusion.1, f32[512]{0:T(512)S(1)} %add_rsqrt_fusion.1, bf16[512,768]{1,0:T(8,128)(2,1)S(1)} %copy-done.5), kind=kOutput, calls=%fused_computation.27 | convolution fusion | flops 1613889024 | bytes 8130560 | tf_op jit(solution)/shard_map/dot_general | solution.py:49
  15.3 2.2 %collective-permute-start.1 = (f32[512]{0:T(512)S(1)}, f32[512]{0:T(512)S(1)}, u32[]{:S(2)}, u32[]{:S(2)}) collective-permute-start(f32[512]{0:T(512)S(1)} %add.75), channel_id=1, source_target_pairs={{0,2},{1,3},{2,0},{3,1},{4,6},{5,7},{6,4},{7,5},{8,10},{9,11},{10,... | collective-permute-start | bytes 6152 | tf_op jit(solution)/shard_map/ppermute | solution.py:29
  17.5 1.6 collective-permute-done.1
  19.1 1.9 %collective-permute-start.2 = (f32[512]{0:T(512)S(1)}, f32[512]{0:T(512)S(1)}, u32[]{:S(2)}, u32[]{:S(2)}) collective-permute-start(f32[512]{0:T(512)S(1)} %add.76), channel_id=1, source_target_pairs={{0,4},{1,5},{2,6},{3,7},{4,0},{5,1},{6,2},{7,3},{8,12},{9,13},{10,... | collective-permute-start | bytes 6152 | tf_op jit(solution)/shard_map/ppermute | solution.py:29
  21.0 3.2 %collective-permute-done.2 = f32[512]{0:T(512)S(1)} collective-permute-done((f32[512]{0:T(512)S(1)}, f32[512]{0:T(512)S(1)}, u32[]{:S(2)}, u32[]{:S(2)}) %collective-permute-start.2) | collective-permute-done | bytes 2080 | tf_op jit(solution)/shard_map/ppermute | solution.py:29
  24.5 20.0 %psum.28 = f32[2048]{0:T(1024)S(1)} all-reduce(f32[2048]{0:T(1024)S(1)} %multiply_reduce_fusion.3), channel_id=1, replica_groups=mesh['dy'=4,'dz'=8,'cx'=4,'core'=2] {'dz'}, use_global_device_ids=true, to_apply=%region_4.0 | all-reduce | flops 2048 | bytes 16384 | tf_op jit(solution)/shard_map/psum | solution.py:35
  44.6 11.5 %psum.29 = f32[2048]{0:T(1024)S(1)} all-reduce(f32[2048]{0:T(1024)S(1)} %psum.28), channel_id=1, replica_groups=mesh['dy'=4,'dz'=8,'cx'=4,'core'=2] {'dy'}, use_global_device_ids=true, to_apply=%region_5.0 | all-reduce | flops 2048 | bytes 16384 | tf_op jit(solution)/shard_map/psum | solution.py:35
  56.1 2.7 %multiply_reduce_fusion.2 = f32[512]{0:T(512)S(1)} fusion(f32[512,2048]{1,0:T(8,128)} %copy-done, f32[2048]{0:T(1024)S(1)} %broadcast_divide_fusion.2), kind=kLoop, calls=%fused_computation.9 | loop fusion | flops 2096640 | bytes 4204544 | tf_op jit(solution)/shard_map/reduce_sum | solution.py:39
  60.6 3.1 %collective-permute-done.4 = f32[512]{0:T(512)S(1)} collective-permute-done((f32[512]{0:T(512)S(1)}, f32[512]{0:T(512)S(1)}, u32[]{:S(2)}, u32[]{:S(2)}) %collective-permute-start.4) | collective-permute-done | bytes 2080 | tf_op jit(solution)/shard_map/ppermute | solution.py:29
  63.6 2.1 %collective-permute-start.5 = (f32[512]{0:T(512)S(1)}, f32[512]{0:T(512)S(1)}, u32[]{:S(2)}, u32[]{:S(2)}) collective-permute-start(f32[512]{0:T(512)S(1)} %add.79), channel_id=1, source_target_pairs={{0,4},{1,5},{2,6},{3,7},{4,0},{5,1},{6,2},{7,3},{8,12},{9,13},{10,... | collective-permute-start | bytes 6152 | tf_op jit(solution)/shard_map/ppermute | solution.py:29
  65.8 3.0 %collective-permute-done.5 = f32[512]{0:T(512)S(1)} collective-permute-done((f32[512]{0:T(512)S(1)}, f32[512]{0:T(512)S(1)}, u32[]{:S(2)}, u32[]{:S(2)}) %collective-permute-start.5) | collective-permute-done | bytes 2080 | tf_op jit(solution)/shard_map/ppermute | solution.py:29
  69.1 14.4 %psum.30 = f32[2048]{0:T(1024)S(1)} all-reduce(f32[2048]{0:T(1024)S(1)} %multiply_reduce_fusion.1), channel_id=1, replica_groups=mesh['dy'=4,'dz'=8,'cx'=4,'core'=2] {'dz'}, use_global_device_ids=true, to_apply=%region_8.0 | all-reduce | flops 2048 | bytes 16384 | tf_op jit(solution)/shard_map/psum | solution.py:35
  83.5 7.8 %psum.31 = f32[2048]{0:T(1024)S(1)} all-reduce(f32[2048]{0:T(1024)S(1)} %psum.30), channel_id=1, replica_groups=mesh['dy'=4,'dz'=8,'cx'=4,'core'=2] {'dy'}, use_global_device_ids=true, to_apply=%region_9.0 | all-reduce | flops 2048 | bytes 16384 | tf_op jit(solution)/shard_map/psum | solution.py:35
  91.4 2.5 %multiply_reduce_fusion = f32[512]{0:T(512)S(1)} fusion(f32[512,2048]{1,0:T(8,128)} %copy-done, f32[2048]{0:T(1024)S(1)} %broadcast_divide_fusion.1), kind=kLoop, calls=%fused_computation.7 | loop fusion | flops 2096640 | bytes 4204544 | tf_op jit(solution)/shard_map/reduce_sum | solution.py:39
  95.7 3.1 %collective-permute-done.7 = f32[512]{0:T(512)S(1)} collective-permute-done((f32[512]{0:T(512)S(1)}, f32[512]{0:T(512)S(1)}, u32[]{:S(2)}, u32[]{:S(2)}) %collective-permute-start.7) | collective-permute-done | bytes 2080 | tf_op jit(solution)/shard_map/ppermute | solution.py:29
  98.8 2.1 %collective-permute-start.8 = (f32[512]{0:T(512)S(1)}, f32[512]{0:T(512)S(1)}, u32[]{:S(2)}, u32[]{:S(2)}) collective-permute-start(f32[512]{0:T(512)S(1)} %add.82), channel_id=1, source_target_pairs={{0,4},{1,5},{2,6},{3,7},{4,0},{5,1},{6,2},{7,3},{8,12},{9,13},{10,... | collective-permute-start | bytes 6152 | tf_op jit(solution)/shard_map/ppermute | solution.py:29
  102.1 1.7 %collective-permute-done.8 = f32[512]{0:T(512)S(1)} collective-permute-done((f32[512]{0:T(512)S(1)}, f32[512]{0:T(512)S(1)}, u32[]{:S(2)}, u32[]{:S(2)}) %collective-permute-start.8) | collective-permute-done | bytes 2080 | tf_op jit(solution)/shard_map/ppermute | solution.py:29
  103.8 10.6 %all-gather = f32[4,1,512]{2,1,0:T(1,128)S(1)} all-gather(f32[1,1,512]{2,1,0:T(1,128)S(1)} %bitcast.6), channel_id=1, replica_groups=mesh['dy'=4,'dz'=8,'cx'=4,'core'=2] {'dy'}, dimensions={0}, use_global_device_ids=true | all-gather | bytes 10240 | tf_op jit(solution)/shard_map/all_gather | solution.py:66
  114.5 5.5 %convert_reduce_fusion = (f32[512]{0:T(512)S(1)}, bf16[2048,512]{1,0:T(8,128)(2,1)S(1)}) fusion(f32[512]{0:T(512)S(1)} %dynamic_slice.7, bf16[2048,768]{1,0:T(8,128)(2,1)} %copy-done.4, s32[]{:T(128)S(6)} %select_n.4, f32[2048,768]{1,0:T(8,128)} %all-gather.3.cloned.1.call-done, f32[]{:T(128)} %bitcast.2, f32[2048]{0:T(1024)S(1)} %bitcast.7), kind=kOutput, calls=%fused_computation.5 | convolution fusion | flops 1620049408 | bytes 9187844 | tf_op jit(solution)/shard_map/dot_general | solution.py:71
  120.0 3.0 %fusion.3 = f32[512,768]{1,0:T(8,128)} fusion(bf16[2048,512]{1,0:T(8,128)(2,1)S(1)} %get-tuple-element.8, f32[2048,768]{1,0:T(8,128)S(1)} %copy-done.3, f32[]{:T(128)} %bitcast.2), kind=kOutput, calls=%fused_computation.15 | convolution fusion | flops 1613758464 | bytes 9961476 | tf_op jit(solution)/shard_map/dot_general | solution.py:79
  124.3 16.2 %all-reduce = f32[512]{0:T(512)S(1)} all-reduce(f32[512]{0:T(512)S(1)} %get-tuple-element.7), channel_id=3, replica_groups=mesh['dy'=4,'dz'=8,'cx'=4,'core'=2] {'dz'}, use_global_device_ids=true, to_apply=%region_13.0.clone | all-reduce | flops 512 | bytes 4096
  140.5 21.8 %reduce-scatter.2.cloned.1.call-done = f32[64,768]{1,0:T(8,128)} async-done(((f32[512,768]{1,0:T(8,128)}), f32[64,768]{1,0:T(8,128)}) %reduce-scatter.2.cloned.1.call-update) | async-done | bytes 196624 | tf_op jit(solution)/shard_map/reduce_scatter | solution.py:82
  162.3 1.7 broadcast_divide_fusion
  (49 shorter events, 9.7 us)
Async XLA Ops:
  6.5 4.1 %copy-start.2 = (bf16[2048,768]{1,0:T(8,128)(2,1)S(1)}, bf16[2048,768]{1,0:T(8,128)(2,1)}, u32[]{:S(2)}) copy-start(bf16[2048,768]{1,0:T(8,128)(2,1)} %param.3) | copy-start | bytes 9437188
  6.5 107.9 %all-gather.3.cloned.1.call-start = ((), (), s32[]{:S(2)}) async-start(), calls=%async_computation.1 | async-start | bytes 7864320 | tf_op jit(solution)/shard_map/all_gather | solution.py:63
  10.6 151.8 %reduce-scatter.2.cloned.1.call-start = ((), (), s32[]{:S(2)}) async-start(), calls=%async_computation.2 | async-start | bytes 1769472 | tf_op jit(solution)/shard_map/reduce_scatter | solution.py:82
  10.7 1.3 copy-start.5
  12.0 2.0 %copy-start.4 = (bf16[2048,768]{1,0:T(8,128)(2,1)}, bf16[2048,768]{1,0:T(8,128)(2,1)S(1)}, u32[]{:S(2)}) copy-start(bf16[2048,768]{1,0:T(8,128)(2,1)S(1)} %fusion.1) | copy-start | bytes 9437188
  14.0 10.2 %copy-start = (f32[512,2048]{1,0:T(8,128)}, f32[512,2048]{1,0:T(8,128)S(1)}, u32[]{:S(2)}) copy-start(f32[512,2048]{1,0:T(8,128)S(1)} %get-tuple-element.6) | copy-start | bytes 12582916
  14.0 1.3 collective-permute-start
  15.3 3.8 %collective-permute-start.1 = (f32[512]{0:T(512)S(1)}, f32[512]{0:T(512)S(1)}, u32[]{:S(2)}, u32[]{:S(2)}) collective-permute-start(f32[512]{0:T(512)S(1)} %add.75), channel_id=1, source_target_pairs={{0,2},{1,3},{2,0},{3,1},{4,6},{5,7},{6,4},{7,5},{8,10},{9,11},{10,... | collective-permute-start | bytes 6152 | tf_op jit(solution)/shard_map/ppermute | solution.py:29
  19.1 5.1 %collective-permute-start.2 = (f32[512]{0:T(512)S(1)}, f32[512]{0:T(512)S(1)}, u32[]{:S(2)}, u32[]{:S(2)}) collective-permute-start(f32[512]{0:T(512)S(1)} %add.76), channel_id=1, source_target_pairs={{0,4},{1,5},{2,6},{3,7},{4,0},{5,1},{6,2},{7,3},{8,12},{9,13},{10,... | collective-permute-start | bytes 6152 | tf_op jit(solution)/shard_map/ppermute | solution.py:29
  56.0 12.7 %copy-start.1 = (f32[512,2048]{1,0:T(8,128)S(1)}, f32[512,2048]{1,0:T(8,128)}, u32[]{:S(2)}) copy-start(f32[512,2048]{1,0:T(8,128)} %copy-done) | copy-start | bytes 12582916
  58.8 1.2 collective-permute-start.3
  60.0 3.6 %collective-permute-start.4 = (f32[512]{0:T(512)S(1)}, f32[512]{0:T(512)S(1)}, u32[]{:S(2)}, u32[]{:S(2)}) collective-permute-start(f32[512]{0:T(512)S(1)} %add.78), channel_id=1, source_target_pairs={{0,2},{1,3},{2,0},{3,1},{4,6},{5,7},{6,4},{7,5},{8,10},{9,11},{10,... | collective-permute-start | bytes 6152 | tf_op jit(solution)/shard_map/ppermute | solution.py:29
  63.6 5.1 %collective-permute-start.5 = (f32[512]{0:T(512)S(1)}, f32[512]{0:T(512)S(1)}, u32[]{:S(2)}, u32[]{:S(2)}) collective-permute-start(f32[512]{0:T(512)S(1)} %add.79), channel_id=1, source_target_pairs={{0,4},{1,5},{2,6},{3,7},{4,0},{5,1},{6,2},{7,3},{8,12},{9,13},{10,... | collective-permute-start | bytes 6152 | tf_op jit(solution)/shard_map/ppermute | solution.py:29
  93.9 1.2 collective-permute-start.6
  95.2 3.6 %collective-permute-start.7 = (f32[512]{0:T(512)S(1)}, f32[512]{0:T(512)S(1)}, u32[]{:S(2)}, u32[]{:S(2)}) collective-permute-start(f32[512]{0:T(512)S(1)} %add.81), channel_id=1, source_target_pairs={{0,2},{1,3},{2,0},{3,1},{4,6},{5,7},{6,4},{7,5},{8,10},{9,11},{10,... | collective-permute-start | bytes 6152 | tf_op jit(solution)/shard_map/ppermute | solution.py:29
  98.8 5.1 %collective-permute-start.8 = (f32[512]{0:T(512)S(1)}, f32[512]{0:T(512)S(1)}, u32[]{:S(2)}, u32[]{:S(2)}) collective-permute-start(f32[512]{0:T(512)S(1)} %add.82), channel_id=1, source_target_pairs={{0,4},{1,5},{2,6},{3,7},{4,0},{5,1},{6,2},{7,3},{8,12},{9,13},{10,... | collective-permute-start | bytes 6152 | tf_op jit(solution)/shard_map/ppermute | solution.py:29
  114.5 5.5 %copy-start.3 = (f32[2048,768]{1,0:T(8,128)S(1)}, f32[2048,768]{1,0:T(8,128)}, u32[]{:S(2)}) copy-start(f32[2048,768]{1,0:T(8,128)} %all-gather.3.cloned.1.call-done) | copy-start | bytes 18874372
  120.0 3.1 %copy-start.6 = (u32[256]{0:T(256)S(1)}, u32[256]{0:T(256)}, u32[]{:S(2)}) copy-start(u32[256]{0:T(256)} %constant.35) | copy-start | bytes 3076
Sparse Core Ops, SparseCore 0:
  10.7 71.4 all-gather.2
  123.2 39.1 reduce-scatter.1

commit v6 on v5

--- a/solution.py
+++ b/solution.py
@@ -21,18 +21,31 @@
     return normalize_wide(values).astype(jnp.bfloat16)
 
 
-def cent_sum(x):
-    n = lax.axis_size("cx") * lax.axis_size("core")
+def doubling_sum(x, axes):
+    n = 1
+    for a in axes:
+        n *= lax.axis_size(a)
     step = 1
     while step < n:
         pairs = [(i, i ^ step) for i in range(n)]
-        x = x + lax.ppermute(x, ("cx", "core"), pairs)
+        x = x + lax.ppermute(x, axes, pairs)
         step *= 2
     return x
 
 
+def cent_sum(x):
+    return doubling_sum(x, ("cx", "core"))
+
+
 def dp_sum(x):
-    return lax.psum(lax.psum(x, "dz"), "dy")
+    return doubling_sum(x, ("dy", "dz"))
+
+
+def doubling_gather(x, axis):
+    n = lax.axis_size(axis)
+    slots = jnp.zeros((n,) + x.shape, x.dtype)
+    slots = lax.dynamic_update_index_in_dim(slots, x, lax.axis_index(axis), 0)
+    return doubling_sum(slots, (axis,)).reshape((n * x.shape[0],) + x.shape[1:])
 
 
 def row_update(boltzmann_affinity, column_factor):
@@ -63,7 +76,7 @@
     gathered = lax.all_gather(scaled_rows, "dy", axis=0, tiled=True)
     unit = column_factor[0] * 0.0 + 1.0
     gathered = (gathered * unit).astype(jnp.bfloat16)
-    gathered_weight = lax.all_gather(row_weight, "dy", axis=0, tiled=True)
+    gathered_weight = doubling_gather(row_weight, "dy")
     sub_cents = local_cents // ny
     start = lax.axis_index("dy") * sub_cents
     sub_normed = lax.dynamic_slice_in_dim(cent_normed, start, sub_cents, 0)

time: 171 us -> 166 us (0.971)
  blocking collectives: 80.5 us -> 18.6 us
  starting transfers between devices: 9.8 us -> 45.7 us
  waiting for transfers between devices: 40.8 us -> 65.7 us
  other arithmetic: 13 us -> 8.52 us
    psum x4 -> x0, blocking collectives: 53.7 us -> none  [dp_sum(): return lax.psum(lax.psum(x, 'dz'), 'dy')]
    ppermute x9 -> x21, starting transfers between devices: 9.76 us -> 45.7 us  [doubling_sum(): x = x + lax.ppermute(x, axes, pairs)]
    ppermute x9 -> x21, waiting for transfers between devices: 19 us -> 43.3 us  [doubling_sum(): x = x + lax.ppermute(x, axes, pairs)]
    all_gather x1 -> x0, blocking collectives: 10.6 us -> none  [shards(): gathered_weight = lax.all_gather(row_weight, 'dy', axis=0, tiled=True)]
    reduce_sum x2, other arithmetic: 5.25 us -> 0.73 us  [row_update(): partial_rows = jnp.sum(boltzmann_affinity * column_factor[None, :], axis=1)]
    unnamed x1, blocking collectives: 16.2 us -> 18.6 us
  transfers between devices with their start and end apart: 11 -> 23, of which waited for: 10 -> 22; matrix products, arithmetic and copies ran while one was open for 6% -> 4% of each run, Pallas kernels for 0% -> 0%
where the time goes in v6:
time: 166 us; the launch traced here: 165 us
  waiting for transfers between devices  65.7 us (40%)
  starting transfers between devices  45.7 us (28%)
  blocking collectives  18.6 us (11%)
  between operations  14.9 us (9%)
  matrix products  10.6 us (6%)
  other arithmetic  8.52 us (5%)
    ppermute x21, starting transfers between devices, doubling_sum(): x = x + lax.ppermute(x, axes, pairs)  45.7 us
    ppermute x21, waiting for transfers between devices, doubling_sum(): x = x + lax.ppermute(x, axes, pairs)  43.3 us
    reduce_scatter x1, waiting for transfers between devices, shards(): lax.psum_scatter((weighted, col_mass), 'dz', scatter_dimension=0, tiled=T...  22.3 us
    unnamed x1, blocking collectives  18.6 us
    dot_general x1, matrix products, shards(): lax.dot_general(gathered, sub_normed, (((1,), (1,)), ((), ())), preferred...  5.49 us
  transfers between devices with their start and end apart: 23, of which 22 were waited for; matrix products, arithmetic and copies ran while one was open for 4% of the time, Pallas kernels for 0%

profile of v6, /device:TPU:2, one launch (start us, length us, event | category | flops | bytes accessed | tf_op | source)
XLA Modules:
  0.0 165.3 jit_solution(508212447471688211)
XLA Ops:
  8.1 2.5 %convert_multiply_fusion.2 = f32[512,768]{1,0:T(8,128)} fusion(bf16[512,768]{1,0:T(8,128)(2,1)} %param.2, f32[512]{0:T(512)S(1)} %add_rsqrt_fusion.1), kind=kLoop, calls=%fused_computation.12 | loop fusion | flops 786432 | bytes 2361344 | tf_op jit(solution)/shard_map/mul | solution.py:17
  15.3 2.2 %collective-permute-start.1 = (f32[512]{0:T(512)S(1)}, f32[512]{0:T(512)S(1)}, u32[]{:S(2)}, u32[]{:S(2)}) collective-permute-start(f32[512]{0:T(512)S(1)} %add.108), channel_id=1, source_target_pairs={{0,2},{1,3},{2,0},{3,1},{4,6},{5,7},{6,4},{7,5},{8,10},{9,11},{10,... | collective-permute-start | bytes 6152 | tf_op jit(solution)/shard_map/ppermute | solution.py:31
  21.0 3.2 %collective-permute-done.2 = f32[512]{0:T(512)S(1)} collective-permute-done((f32[512]{0:T(512)S(1)}, f32[512]{0:T(512)S(1)}, u32[]{:S(2)}, u32[]{:S(2)}) %collective-permute-start.2) | collective-permute-done | bytes 2080 | tf_op jit(solution)/shard_map/ppermute | solution.py:31
  28.3 3.0 %collective-permute-start.4 = (f32[2048]{0:T(1024)S(1)}, f32[2048]{0:T(1024)S(1)}, u32[]{:S(2)}, u32[]{:S(2)}) collective-permute-start(f32[2048]{0:T(1024)S(1)} %add.111), channel_id=1, source_target_pairs={{0,16},{8,24},{16,0},{24,8},{32,48},{40,56},{48,32},{56,40},{64,80... | collective-permute-start | bytes 24584 | tf_op jit(solution)/shard_map/ppermute | solution.py:31
  33.0 6.8 %collective-permute-start.5 = (f32[2048]{0:T(1024)S(1)}, f32[2048]{0:T(1024)S(1)}, u32[]{:S(2)}, u32[]{:S(2)}) collective-permute-start(f32[2048]{0:T(1024)S(1)} %add.112), channel_id=1, source_target_pairs={{0,32},{8,40},{16,48},{24,56},{32,0},{40,8},{48,16},{56,24},{64,96... | collective-permute-start | bytes 24584 | tf_op jit(solution)/shard_map/ppermute | solution.py:31
  43.0 2.4 %collective-permute-done.6 = f32[2048]{0:T(1024)S(1)} collective-permute-done((f32[2048]{0:T(1024)S(1)}, f32[2048]{0:T(1024)S(1)}, u32[]{:S(2)}, u32[]{:S(2)}) %collective-permute-start.6) | collective-permute-done | bytes 8224 | tf_op jit(solution)/shard_map/ppermute | solution.py:31
  45.4 3.2 %collective-permute-start.7 = (f32[2048]{0:T(1024)S(1)}, f32[2048]{0:T(1024)S(1)}, u32[]{:S(2)}, u32[]{:S(2)}) collective-permute-start(f32[2048]{0:T(1024)S(1)} %add.114), channel_id=1, source_target_pairs={{0,128},{8,136},{16,144},{24,152},{32,160},{40,168},{48,176},{56,1... | collective-permute-start | bytes 24584 | tf_op jit(solution)/shard_map/ppermute | solution.py:31
  48.6 2.3 %collective-permute-done.7 = f32[2048]{0:T(1024)S(1)} collective-permute-done((f32[2048]{0:T(1024)S(1)}, f32[2048]{0:T(1024)S(1)}, u32[]{:S(2)}, u32[]{:S(2)}) %collective-permute-start.7) | collective-permute-done | bytes 8224 | tf_op jit(solution)/shard_map/ppermute | solution.py:31
  53.5 2.5 %collective-permute-done.9 = f32[512]{0:T(512)S(1)} collective-permute-done((f32[512]{0:T(512)S(1)}, f32[512]{0:T(512)S(1)}, u32[]{:S(2)}, u32[]{:S(2)}) %collective-permute-start.9) | collective-permute-done | bytes 2080 | tf_op jit(solution)/shard_map/ppermute | solution.py:31
  58.2 3.0 %collective-permute-done.10 = f32[512]{0:T(512)S(1)} collective-permute-done((f32[512]{0:T(512)S(1)}, f32[512]{0:T(512)S(1)}, u32[]{:S(2)}, u32[]{:S(2)}) %collective-permute-start.10) | collective-permute-done | bytes 2080 | tf_op jit(solution)/shard_map/ppermute | solution.py:31
  62.6 2.6 %collective-permute-done.11 = f32[2048]{0:T(1024)S(1)} collective-permute-done((f32[2048]{0:T(1024)S(1)}, f32[2048]{0:T(1024)S(1)}, u32[]{:S(2)}, u32[]{:S(2)}) %collective-permute-start.11) | collective-permute-done | bytes 8224 | tf_op jit(solution)/shard_map/ppermute | solution.py:31
  67.3 2.5 %collective-permute-done.12 = f32[2048]{0:T(1024)S(1)} collective-permute-done((f32[2048]{0:T(1024)S(1)}, f32[2048]{0:T(1024)S(1)}, u32[]{:S(2)}, u32[]{:S(2)}) %collective-permute-start.12) | collective-permute-done | bytes 8224 | tf_op jit(solution)/shard_map/ppermute | solution.py:31
  69.8 5.9 %collective-permute-start.13 = (f32[2048]{0:T(1024)S(1)}, f32[2048]{0:T(1024)S(1)}, u32[]{:S(2)}, u32[]{:S(2)}) collective-permute-start(f32[2048]{0:T(1024)S(1)} %add.120), channel_id=1, source_target_pairs={{0,32},{8,40},{16,48},{24,56},{32,0},{40,8},{48,16},{56,24},{64,96... | collective-permute-start | bytes 24584 | tf_op jit(solution)/shard_map/ppermute | solution.py:31
  79.0 2.3 %collective-permute-done.14 = f32[2048]{0:T(1024)S(1)} collective-permute-done((f32[2048]{0:T(1024)S(1)}, f32[2048]{0:T(1024)S(1)}, u32[]{:S(2)}, u32[]{:S(2)}) %collective-permute-start.14) | collective-permute-done | bytes 8224 | tf_op jit(solution)/shard_map/ppermute | solution.py:31
  81.3 3.1 %collective-permute-start.15 = (f32[2048]{0:T(1024)S(1)}, f32[2048]{0:T(1024)S(1)}, u32[]{:S(2)}, u32[]{:S(2)}) collective-permute-start(f32[2048]{0:T(1024)S(1)} %add.122), channel_id=1, source_target_pairs={{0,128},{8,136},{16,144},{24,152},{32,160},{40,168},{48,176},{56,1... | collective-permute-start | bytes 24584 | tf_op jit(solution)/shard_map/ppermute | solution.py:31
  89.1 2.7 %collective-permute-done.17 = f32[512]{0:T(512)S(1)} collective-permute-done((f32[512]{0:T(512)S(1)}, f32[512]{0:T(512)S(1)}, u32[]{:S(2)}, u32[]{:S(2)}) %collective-permute-start.17) | collective-permute-done | bytes 2080 | tf_op jit(solution)/shard_map/ppermute | solution.py:31
  91.7 2.2 %collective-permute-start.18 = (f32[512]{0:T(512)S(1)}, f32[512]{0:T(512)S(1)}, u32[]{:S(2)}, u32[]{:S(2)}) collective-permute-start(f32[512]{0:T(512)S(1)} %add.125), channel_id=1, source_target_pairs={{0,4},{1,5},{2,6},{3,7},{4,0},{5,1},{6,2},{7,3},{8,12},{9,13},{10,... | collective-permute-start | bytes 6152 | tf_op jit(solution)/shard_map/ppermute | solution.py:31
  93.9 2.9 %collective-permute-done.18 = f32[512]{0:T(512)S(1)} collective-permute-done((f32[512]{0:T(512)S(1)}, f32[512]{0:T(512)S(1)}, u32[]{:S(2)}, u32[]{:S(2)}) %collective-permute-start.18) | collective-permute-done | bytes 2080 | tf_op jit(solution)/shard_map/ppermute | solution.py:31
  98.3 2.3 %collective-permute-done.19 = f32[4,512]{1,0:T(4,128)S(1)} collective-permute-done((f32[4,512]{1,0:T(4,128)S(1)}, f32[4,512]{1,0:T(4,128)S(1)}, u32[]{:S(2)}, u32[]{:S(2)}) %collective-permute-start.19) | collective-permute-done | bytes 8224 | tf_op jit(solution)/shard_map/ppermute | solution.py:31
  100.7 3.2 %collective-permute-start.20 = (f32[4,512]{1,0:T(4,128)S(1)}, f32[4,512]{1,0:T(4,128)S(1)}, u32[]{:S(2)}, u32[]{:S(2)}) collective-permute-start(f32[4,512]{1,0:T(4,128)S(1)} %add.128), channel_id=1, source_target_pairs={{0,128},{64,192},{128,0},{192,64},{1,129},{65,193},{129,1},{193,65... | collective-permute-start | bytes 24584 | tf_op jit(solution)/shard_map/ppermute | solution.py:31
  105.9 5.5 %convert_reduce_fusion = (f32[512]{0:T(512)S(1)}, bf16[2048,512]{1,0:T(8,128)(2,1)S(1)}) fusion(f32[512]{0:T(512)S(1)} %dynamic_slice.7, bf16[2048,768]{1,0:T(8,128)(2,1)} %copy-done.2, s32[]{:T(128)S(6)} %select_n.9, f32[2048,768]{1,0:T(8,128)} %all-gather.2.cloned.1.call-done, f32[]{:T(128)} %bitcast.1, f32[2048]{0:T(1024)S(1)} %bitcast.10), kind=kOutput, calls=%fused_computation.5 | convolution fusion | flops 1620049408 | bytes 9187844 | tf_op jit(solution)/shard_map/dot_general | solution.py:84
  111.5 3.1 %fusion.3 = f32[512,768]{1,0:T(8,128)} fusion(bf16[2048,512]{1,0:T(8,128)(2,1)S(1)} %get-tuple-element.8, f32[2048,768]{1,0:T(8,128)S(1)} %copy-done.1, f32[]{:T(128)} %bitcast.1), kind=kOutput, calls=%fused_computation.15 | convolution fusion | flops 1613758464 | bytes 9961476 | tf_op jit(solution)/shard_map/dot_general | solution.py:92
  115.8 18.6 %all-reduce = f32[512]{0:T(512)S(1)} all-reduce(f32[512]{0:T(512)S(1)} %get-tuple-element.7), channel_id=3, replica_groups=mesh['dy'=4,'dz'=8,'cx'=4,'core'=2] {'dz'}, use_global_device_ids=true, to_apply=%region_9.10.clone | all-reduce | flops 512 | bytes 4096
  134.4 22.3 %reduce-scatter.2.cloned.1.call-done = f32[64,768]{1,0:T(8,128)} async-done(((f32[512,768]{1,0:T(8,128)}), f32[64,768]{1,0:T(8,128)}) %reduce-scatter.2.cloned.1.call-update) | async-done | bytes 196624 | tf_op jit(solution)/shard_map/reduce_scatter | solution.py:95
  (78 shorter events, 40.0 us)
Async XLA Ops:
  6.5 99.4 %all-gather.2.cloned.1.call-start = ((), (), s32[]{:S(2)}) async-start(), calls=%async_computation.1 | async-start | bytes 7864320 | tf_op jit(solution)/shard_map/all_gather | solution.py:76
  10.6 146.2 %reduce-scatter.2.cloned.1.call-start = ((), (), s32[]{:S(2)}) async-start(), calls=%async_computation.2 | async-start | bytes 1769472 | tf_op jit(solution)/shard_map/reduce_scatter | solution.py:95
  14.0 1.3 collective-permute-start
  15.3 3.8 %collective-permute-start.1 = (f32[512]{0:T(512)S(1)}, f32[512]{0:T(512)S(1)}, u32[]{:S(2)}, u32[]{:S(2)}) collective-permute-start(f32[512]{0:T(512)S(1)} %add.108), channel_id=1, source_target_pairs={{0,2},{1,3},{2,0},{3,1},{4,6},{5,7},{6,4},{7,5},{8,10},{9,11},{10,... | collective-permute-start | bytes 6152 | tf_op jit(solution)/shard_map/ppermute | solution.py:31
  19.1 5.1 %collective-permute-start.2 = (f32[512]{0:T(512)S(1)}, f32[512]{0:T(512)S(1)}, u32[]{:S(2)}, u32[]{:S(2)}) collective-permute-start(f32[512]{0:T(512)S(1)} %add.109), channel_id=1, source_target_pairs={{0,4},{1,5},{2,6},{3,7},{4,0},{5,1},{6,2},{7,3},{8,12},{9,13},{10,... | collective-permute-start | bytes 6152 | tf_op jit(solution)/shard_map/ppermute | solution.py:31
  24.6 3.7 %collective-permute-start.3 = (f32[2048]{0:T(1024)S(1)}, f32[2048]{0:T(1024)S(1)}, u32[]{:S(2)}, u32[]{:S(2)}) collective-permute-start(f32[2048]{0:T(1024)S(1)} %multiply_reduce_fusion.3), channel_id=1, source_target_pairs={{0,8},{8,0},{16,24},{24,16},{32,40},{40,32},{48,56},{56,48},{64,72... | collective-permute-start | bytes 24584 | tf_op jit(solution)/shard_map/ppermute | solution.py:31
  28.3 4.7 %collective-permute-start.4 = (f32[2048]{0:T(1024)S(1)}, f32[2048]{0:T(1024)S(1)}, u32[]{:S(2)}, u32[]{:S(2)}) collective-permute-start(f32[2048]{0:T(1024)S(1)} %add.111), channel_id=1, source_target_pairs={{0,16},{8,24},{16,0},{24,8},{32,48},{40,56},{48,32},{56,40},{64,80... | collective-permute-start | bytes 24584 | tf_op jit(solution)/shard_map/ppermute | solution.py:31
  33.0 8.5 %collective-permute-start.5 = (f32[2048]{0:T(1024)S(1)}, f32[2048]{0:T(1024)S(1)}, u32[]{:S(2)}, u32[]{:S(2)}) collective-permute-start(f32[2048]{0:T(1024)S(1)} %add.112), channel_id=1, source_target_pairs={{0,32},{8,40},{16,48},{24,56},{32,0},{40,8},{48,16},{56,24},{64,96... | collective-permute-start | bytes 24584 | tf_op jit(solution)/shard_map/ppermute | solution.py:31
  41.5 3.9 %collective-permute-start.6 = (f32[2048]{0:T(1024)S(1)}, f32[2048]{0:T(1024)S(1)}, u32[]{:S(2)}, u32[]{:S(2)}) collective-permute-start(f32[2048]{0:T(1024)S(1)} %add.113), channel_id=1, source_target_pairs={{0,64},{8,72},{16,80},{24,88},{32,96},{40,104},{48,112},{56,120},{... | collective-permute-start | bytes 24584 | tf_op jit(solution)/shard_map/ppermute | solution.py:31
  45.4 5.5 %collective-permute-start.7 = (f32[2048]{0:T(1024)S(1)}, f32[2048]{0:T(1024)S(1)}, u32[]{:S(2)}, u32[]{:S(2)}) collective-permute-start(f32[2048]{0:T(1024)S(1)} %add.114), channel_id=1, source_target_pairs={{0,128},{8,136},{16,144},{24,152},{32,160},{40,168},{48,176},{56,1... | collective-permute-start | bytes 24584 | tf_op jit(solution)/shard_map/ppermute | solution.py:31
  51.2 1.2 collective-permute-start.8
  52.5 3.6 %collective-permute-start.9 = (f32[512]{0:T(512)S(1)}, f32[512]{0:T(512)S(1)}, u32[]{:S(2)}, u32[]{:S(2)}) collective-permute-start(f32[512]{0:T(512)S(1)} %add.116), channel_id=1, source_target_pairs={{0,2},{1,3},{2,0},{3,1},{4,6},{5,7},{6,4},{7,5},{8,10},{9,11},{10,... | collective-permute-start | bytes 6152 | tf_op jit(solution)/shard_map/ppermute | solution.py:31
  56.1 5.1 %collective-permute-start.10 = (f32[512]{0:T(512)S(1)}, f32[512]{0:T(512)S(1)}, u32[]{:S(2)}, u32[]{:S(2)}) collective-permute-start(f32[512]{0:T(512)S(1)} %add.117), channel_id=1, source_target_pairs={{0,4},{1,5},{2,6},{3,7},{4,0},{5,1},{6,2},{7,3},{8,12},{9,13},{10,... | collective-permute-start | bytes 6152 | tf_op jit(solution)/shard_map/ppermute | solution.py:31
  61.5 3.7 %collective-permute-start.11 = (f32[2048]{0:T(1024)S(1)}, f32[2048]{0:T(1024)S(1)}, u32[]{:S(2)}, u32[]{:S(2)}) collective-permute-start(f32[2048]{0:T(1024)S(1)} %multiply_reduce_fusion.1), channel_id=1, source_target_pairs={{0,8},{8,0},{16,24},{24,16},{32,40},{40,32},{48,56},{56,48},{64,72... | collective-permute-start | bytes 24584 | tf_op jit(solution)/shard_map/ppermute | solution.py:31
  65.3 4.5 %collective-permute-start.12 = (f32[2048]{0:T(1024)S(1)}, f32[2048]{0:T(1024)S(1)}, u32[]{:S(2)}, u32[]{:S(2)}) collective-permute-start(f32[2048]{0:T(1024)S(1)} %add.119), channel_id=1, source_target_pairs={{0,16},{8,24},{16,0},{24,8},{32,48},{40,56},{48,32},{56,40},{64,80... | collective-permute-start | bytes 24584 | tf_op jit(solution)/shard_map/ppermute | solution.py:31
  69.8 7.6 %collective-permute-start.13 = (f32[2048]{0:T(1024)S(1)}, f32[2048]{0:T(1024)S(1)}, u32[]{:S(2)}, u32[]{:S(2)}) collective-permute-start(f32[2048]{0:T(1024)S(1)} %add.120), channel_id=1, source_target_pairs={{0,32},{8,40},{16,48},{24,56},{32,0},{40,8},{48,16},{56,24},{64,96... | collective-permute-start | bytes 24584 | tf_op jit(solution)/shard_map/ppermute | solution.py:31
  77.4 3.9 %collective-permute-start.14 = (f32[2048]{0:T(1024)S(1)}, f32[2048]{0:T(1024)S(1)}, u32[]{:S(2)}, u32[]{:S(2)}) collective-permute-start(f32[2048]{0:T(1024)S(1)} %add.121), channel_id=1, source_target_pairs={{0,64},{8,72},{16,80},{24,88},{32,96},{40,104},{48,112},{56,120},{... | collective-permute-start | bytes 24584 | tf_op jit(solution)/shard_map/ppermute | solution.py:31
  81.3 5.2 %collective-permute-start.15 = (f32[2048]{0:T(1024)S(1)}, f32[2048]{0:T(1024)S(1)}, u32[]{:S(2)}, u32[]{:S(2)}) collective-permute-start(f32[2048]{0:T(1024)S(1)} %add.122), channel_id=1, source_target_pairs={{0,128},{8,136},{16,144},{24,152},{32,160},{40,168},{48,176},{56,1... | collective-permute-start | bytes 24584 | tf_op jit(solution)/shard_map/ppermute | solution.py:31
  86.9 1.2 collective-permute-start.16
  88.1 3.6 %collective-permute-start.17 = (f32[512]{0:T(512)S(1)}, f32[512]{0:T(512)S(1)}, u32[]{:S(2)}, u32[]{:S(2)}) collective-permute-start(f32[512]{0:T(512)S(1)} %add.124), channel_id=1, source_target_pairs={{0,2},{1,3},{2,0},{3,1},{4,6},{5,7},{6,4},{7,5},{8,10},{9,11},{10,... | collective-permute-start | bytes 6152 | tf_op jit(solution)/shard_map/ppermute | solution.py:31
  91.7 5.1 %collective-permute-start.18 = (f32[512]{0:T(512)S(1)}, f32[512]{0:T(512)S(1)}, u32[]{:S(2)}, u32[]{:S(2)}) collective-permute-start(f32[512]{0:T(512)S(1)} %add.125), channel_id=1, source_target_pairs={{0,4},{1,5},{2,6},{3,7},{4,0},{5,1},{6,2},{7,3},{8,12},{9,13},{10,... | collective-permute-start | bytes 6152 | tf_op jit(solution)/shard_map/ppermute | solution.py:31
  96.9 3.7 %collective-permute-start.19 = (f32[4,512]{1,0:T(4,128)S(1)}, f32[4,512]{1,0:T(4,128)S(1)}, u32[]{:S(2)}, u32[]{:S(2)}) collective-permute-start(f32[4,512]{1,0:T(4,128)S(1)} %dynamic_update_slice.6), channel_id=1, source_target_pairs={{0,64},{64,0},{128,192},{192,128},{1,65},{65,1},{129,193},{193,129... | collective-permute-start | bytes 24584 | tf_op jit(solution)/shard_map/ppermute | solution.py:31
  100.7 5.2 %collective-permute-start.20 = (f32[4,512]{1,0:T(4,128)S(1)}, f32[4,512]{1,0:T(4,128)S(1)}, u32[]{:S(2)}, u32[]{:S(2)}) collective-permute-start(f32[4,512]{1,0:T(4,128)S(1)} %add.128), channel_id=1, source_target_pairs={{0,128},{64,192},{128,0},{192,64},{1,129},{65,193},{129,1},{193,65... | collective-permute-start | bytes 24584 | tf_op jit(solution)/shard_map/ppermute | solution.py:31
  105.9 5.5 %copy-start.1 = (f32[2048,768]{1,0:T(8,128)S(1)}, f32[2048,768]{1,0:T(8,128)}, u32[]{:S(2)}) copy-start(f32[2048,768]{1,0:T(8,128)} %all-gather.2.cloned.1.call-done) | copy-start | bytes 18874372
  (4 other events, 10.6 us)
Sparse Core Ops, SparseCore 0:
  10.7 71.4 all-gather.1
  114.7 42.0 reduce-scatter.1

commit v7 on v6

--- a/solution.py
+++ b/solution.py
@@ -92,8 +92,10 @@
     weighted = lax.dot_general(
         transport, gathered, (((0,), (0,)), ((), ())), preferred_element_type=jnp.float32
     )
-    weighted, col_mass = lax.psum_scatter(
-        (weighted, col_mass), "dz", scatter_dimension=0, tiled=True
+    weighted = lax.psum_scatter(weighted, "dz", scatter_dimension=0, tiled=True)
+    own = weighted.shape[0]
+    col_mass = lax.dynamic_slice_in_dim(
+        doubling_sum(col_mass, ("dz",)), lax.axis_index("dz") * own, own, 0
     )
     return weighted / col_mass[:, None]
 

time: 166 us -> 165 us (level)
  blocking collectives: 18.6 us -> 0 us
  waiting for transfers between devices: 65.7 us -> 76.4 us
  starting transfers between devices: 45.7 us -> 54.8 us
    unnamed x1 -> x0, blocking collectives: 18.6 us -> none
    ppermute x21 -> x24, starting transfers between devices: 45.7 us -> 54.7 us  [doubling_sum(): x = x + lax.ppermute(x, axes, pairs)]
    ppermute x21 -> x24, waiting for transfers between devices: 43.3 us -> 49.9 us  [doubling_sum(): x = x + lax.ppermute(x, axes, pairs)]
    reduce_scatter x1, waiting for transfers between devices: 22.3 us -> 26.5 us  [shards(): weighted = lax.psum_scatter(weighted, 'dz', scatter_dimension=0, tiled=True)]
  transfers between devices with their start and end apart: 23 -> 26, of which waited for: 22 -> 25; matrix products, arithmetic and copies ran while one was open for 4% -> 3% of each run, Pallas kernels for 0% -> 0%
where the time goes in v7:
time: 165 us
  waiting for transfers between devices  76.4 us (46%)
  starting transfers between devices  54.8 us (33%)
  between operations  14.2 us (9%)
  matrix products  10.6 us (6%)
  other arithmetic  8.52 us (5%)
    ppermute x24, starting transfers between devices, doubling_sum(): x = x + lax.ppermute(x, axes, pairs)  54.7 us
    ppermute x24, waiting for transfers between devices, doubling_sum(): x = x + lax.ppermute(x, axes, pairs)  49.9 us
    reduce_scatter x1, waiting for transfers between devices, shards(): weighted = lax.psum_scatter(weighted, 'dz', scatter_dimension=0, tiled=True)  26.5 us
    dot_general x1, matrix products, shards(): lax.dot_general(gathered, sub_normed, (((1,), (1,)), ((), ())), preferred...  5.49 us
  transfers between devices with their start and end apart: 26, of which 25 were waited for; matrix products, arithmetic and copies ran while one was open for 3% of the time, Pallas kernels for 0%

profile of v7, /device:TPU:2, one launch (start us, length us, event | category | flops | bytes accessed | tf_op | source)
XLA Modules:
  0.0 165.3 jit_solution(15626415610093178559)
XLA Ops:
  8.1 2.5 %convert_multiply_fusion.2 = f32[512,768]{1,0:T(8,128)} fusion(bf16[512,768]{1,0:T(8,128)(2,1)} %param.2, f32[512]{0:T(512)S(1)} %add_rsqrt_fusion.1), kind=kLoop, calls=%fused_computation.12 | loop fusion | flops 786432 | bytes 2361344 | tf_op jit(solution)/shard_map/mul | solution.py:17
  21.0 3.2 %collective-permute-done.2 = f32[512]{0:T(512)S(1)} collective-permute-done((f32[512]{0:T(512)S(1)}, f32[512]{0:T(512)S(1)}, u32[]{:S(2)}, u32[]{:S(2)}) %collective-permute-start.2) | collective-permute-done | bytes 2080 | tf_op jit(solution)/shard_map/ppermute | solution.py:31
  28.3 3.1 %collective-permute-start.4 = (f32[2048]{0:T(1024)S(1)}, f32[2048]{0:T(1024)S(1)}, u32[]{:S(2)}, u32[]{:S(2)}) collective-permute-start(f32[2048]{0:T(1024)S(1)} %add.121), channel_id=1, source_target_pairs={{0,16},{8,24},{16,0},{24,8},{32,48},{40,56},{48,32},{56,40},{64,80... | collective-permute-start | bytes 24584 | tf_op jit(solution)/shard_map/ppermute | solution.py:31
  33.0 6.8 %collective-permute-start.5 = (f32[2048]{0:T(1024)S(1)}, f32[2048]{0:T(1024)S(1)}, u32[]{:S(2)}, u32[]{:S(2)}) collective-permute-start(f32[2048]{0:T(1024)S(1)} %add.122), channel_id=1, source_target_pairs={{0,32},{8,40},{16,48},{24,56},{32,0},{40,8},{48,16},{56,24},{64,96... | collective-permute-start | bytes 24584 | tf_op jit(solution)/shard_map/ppermute | solution.py:31
  43.0 2.4 %collective-permute-done.6 = f32[2048]{0:T(1024)S(1)} collective-permute-done((f32[2048]{0:T(1024)S(1)}, f32[2048]{0:T(1024)S(1)}, u32[]{:S(2)}, u32[]{:S(2)}) %collective-permute-start.6) | collective-permute-done | bytes 8224 | tf_op jit(solution)/shard_map/ppermute | solution.py:31
  45.4 3.2 %collective-permute-start.7 = (f32[2048]{0:T(1024)S(1)}, f32[2048]{0:T(1024)S(1)}, u32[]{:S(2)}, u32[]{:S(2)}) collective-permute-start(f32[2048]{0:T(1024)S(1)} %add.124), channel_id=1, source_target_pairs={{0,128},{8,136},{16,144},{24,152},{32,160},{40,168},{48,176},{56,1... | collective-permute-start | bytes 24584 | tf_op jit(solution)/shard_map/ppermute | solution.py:31
  48.6 2.3 %collective-permute-done.7 = f32[2048]{0:T(1024)S(1)} collective-permute-done((f32[2048]{0:T(1024)S(1)}, f32[2048]{0:T(1024)S(1)}, u32[]{:S(2)}, u32[]{:S(2)}) %collective-permute-start.7) | collective-permute-done | bytes 8224 | tf_op jit(solution)/shard_map/ppermute | solution.py:31
  53.5 2.5 %collective-permute-done.9 = f32[512]{0:T(512)S(1)} collective-permute-done((f32[512]{0:T(512)S(1)}, f32[512]{0:T(512)S(1)}, u32[]{:S(2)}, u32[]{:S(2)}) %collective-permute-start.9) | collective-permute-done | bytes 2080 | tf_op jit(solution)/shard_map/ppermute | solution.py:31
  58.2 3.0 %collective-permute-done.10 = f32[512]{0:T(512)S(1)} collective-permute-done((f32[512]{0:T(512)S(1)}, f32[512]{0:T(512)S(1)}, u32[]{:S(2)}, u32[]{:S(2)}) %collective-permute-start.10) | collective-permute-done | bytes 2080 | tf_op jit(solution)/shard_map/ppermute | solution.py:31
  62.6 2.6 %collective-permute-done.11 = f32[2048]{0:T(1024)S(1)} collective-permute-done((f32[2048]{0:T(1024)S(1)}, f32[2048]{0:T(1024)S(1)}, u32[]{:S(2)}, u32[]{:S(2)}) %collective-permute-start.11) | collective-permute-done | bytes 8224 | tf_op jit(solution)/shard_map/ppermute | solution.py:31
  67.3 2.5 %collective-permute-done.12 = f32[2048]{0:T(1024)S(1)} collective-permute-done((f32[2048]{0:T(1024)S(1)}, f32[2048]{0:T(1024)S(1)}, u32[]{:S(2)}, u32[]{:S(2)}) %collective-permute-start.12) | collective-permute-done | bytes 8224 | tf_op jit(solution)/shard_map/ppermute | solution.py:31
  69.8 5.9 %collective-permute-start.13 = (f32[2048]{0:T(1024)S(1)}, f32[2048]{0:T(1024)S(1)}, u32[]{:S(2)}, u32[]{:S(2)}) collective-permute-start(f32[2048]{0:T(1024)S(1)} %add.130), channel_id=1, source_target_pairs={{0,32},{8,40},{16,48},{24,56},{32,0},{40,8},{48,16},{56,24},{64,96... | collective-permute-start | bytes 24584 | tf_op jit(solution)/shard_map/ppermute | solution.py:31
  79.0 2.3 %collective-permute-done.14 = f32[2048]{0:T(1024)S(1)} collective-permute-done((f32[2048]{0:T(1024)S(1)}, f32[2048]{0:T(1024)S(1)}, u32[]{:S(2)}, u32[]{:S(2)}) %collective-permute-start.14) | collective-permute-done | bytes 8224 | tf_op jit(solution)/shard_map/ppermute | solution.py:31
  81.3 3.1 %collective-permute-start.15 = (f32[2048]{0:T(1024)S(1)}, f32[2048]{0:T(1024)S(1)}, u32[]{:S(2)}, u32[]{:S(2)}) collective-permute-start(f32[2048]{0:T(1024)S(1)} %add.132), channel_id=1, source_target_pairs={{0,128},{8,136},{16,144},{24,152},{32,160},{40,168},{48,176},{56,1... | collective-permute-start | bytes 24584 | tf_op jit(solution)/shard_map/ppermute | solution.py:31
  89.0 2.7 %collective-permute-done.17 = f32[512]{0:T(512)S(1)} collective-permute-done((f32[512]{0:T(512)S(1)}, f32[512]{0:T(512)S(1)}, u32[]{:S(2)}, u32[]{:S(2)}) %collective-permute-start.17) | collective-permute-done | bytes 2080 | tf_op jit(solution)/shard_map/ppermute | solution.py:31
  93.9 2.9 %collective-permute-done.18 = f32[512]{0:T(512)S(1)} collective-permute-done((f32[512]{0:T(512)S(1)}, f32[512]{0:T(512)S(1)}, u32[]{:S(2)}, u32[]{:S(2)}) %collective-permute-start.18) | collective-permute-done | bytes 2080 | tf_op jit(solution)/shard_map/ppermute | solution.py:31
  98.3 2.3 %collective-permute-done.19 = f32[4,512]{1,0:T(4,128)S(1)} collective-permute-done((f32[4,512]{1,0:T(4,128)S(1)}, f32[4,512]{1,0:T(4,128)S(1)}, u32[]{:S(2)}, u32[]{:S(2)}) %collective-permute-start.19) | collective-permute-done | bytes 8224 | tf_op jit(solution)/shard_map/ppermute | solution.py:31
  100.7 3.2 %collective-permute-start.20 = (f32[4,512]{1,0:T(4,128)S(1)}, f32[4,512]{1,0:T(4,128)S(1)}, u32[]{:S(2)}, u32[]{:S(2)}) collective-permute-start(f32[4,512]{1,0:T(4,128)S(1)} %add.138), channel_id=1, source_target_pairs={{0,128},{64,192},{128,0},{192,64},{1,129},{65,193},{129,1},{193,65... | collective-permute-start | bytes 24584 | tf_op jit(solution)/shard_map/ppermute | solution.py:31
  105.9 5.5 %convert_reduce_fusion = (f32[512]{0:T(512)S(1)}, bf16[2048,512]{1,0:T(8,128)(2,1)S(1)}) fusion(f32[512]{0:T(512)S(1)} %dynamic_slice.10, bf16[2048,768]{1,0:T(8,128)(2,1)} %copy-done.2, s32[]{:T(128)S(6)} %select_n.12, f32[2048,768]{1,0:T(8,128)} %all-gather.2.cloned.1.call-done, f32[]{:T(128)} %bitcast.1, f32[2048]{0:T(1024)S(1)} %bitcast.9), kind=kOutput, calls=%fused_computation.5 | convolution fusion | flops 1620049408 | bytes 9187844 | tf_op jit(solution)/shard_map/dot_general | solution.py:84
  111.4 3.0 %fusion.3 = f32[512,768]{1,0:T(8,128)} fusion(bf16[2048,512]{1,0:T(8,128)(2,1)S(1)} %get-tuple-element.8, f32[2048,768]{1,0:T(8,128)S(1)} %copy-done.1, f32[]{:T(128)} %bitcast.1), kind=kOutput, calls=%fused_computation.15 | convolution fusion | flops 1613758464 | bytes 9961476 | tf_op jit(solution)/shard_map/dot_general | solution.py:92
  115.6 2.6 %collective-permute-done.21 = f32[512]{0:T(512)S(1)} collective-permute-done((f32[512]{0:T(512)S(1)}, f32[512]{0:T(512)S(1)}, u32[]{:S(2)}, u32[]{:S(2)}) %collective-permute-start.21) | collective-permute-done | bytes 2080 | tf_op jit(solution)/shard_map/ppermute | solution.py:31
  120.2 2.4 %collective-permute-done.22 = f32[512]{0:T(512)S(1)} collective-permute-done((f32[512]{0:T(512)S(1)}, f32[512]{0:T(512)S(1)}, u32[]{:S(2)}, u32[]{:S(2)}) %collective-permute-start.22) | collective-permute-done | bytes 2080 | tf_op jit(solution)/shard_map/ppermute | solution.py:31
  122.7 6.0 %collective-permute-start.23 = (f32[512]{0:T(512)S(1)}, f32[512]{0:T(512)S(1)}, u32[]{:S(2)}, u32[]{:S(2)}) collective-permute-start(f32[512]{0:T(512)S(1)} %add.144), channel_id=1, source_target_pairs={{0,32},{8,40},{16,48},{24,56},{32,0},{40,8},{48,16},{56,24},{1,33}... | collective-permute-start | bytes 6152 | tf_op jit(solution)/shard_map/ppermute | solution.py:31
  130.3 26.5 %reduce-scatter.2.cloned.1.call-done = f32[64,768]{1,0:T(8,128)} async-done(((f32[512,768]{1,0:T(8,128)}), f32[64,768]{1,0:T(8,128)}) %reduce-scatter.2.cloned.1.call-update) | async-done | bytes 196624 | tf_op jit(solution)/shard_map/reduce_scatter | solution.py:95
  (83 shorter events, 48.6 us)
Async XLA Ops:
  6.5 99.4 %all-gather.2.cloned.1.call-start = ((), (), s32[]{:S(2)}) async-start(), calls=%async_computation.1 | async-start | bytes 7864320 | tf_op jit(solution)/shard_map/all_gather | solution.py:76
  10.6 146.2 %reduce-scatter.2.cloned.1.call-start = ((), (), s32[]{:S(2)}) async-start(), calls=%async_computation.2 | async-start | bytes 1769472 | tf_op jit(solution)/shard_map/reduce_scatter | solution.py:95
  14.0 1.3 collective-permute-start
  15.3 3.8 %collective-permute-start.1 = (f32[512]{0:T(512)S(1)}, f32[512]{0:T(512)S(1)}, u32[]{:S(2)}, u32[]{:S(2)}) collective-permute-start(f32[512]{0:T(512)S(1)} %add.118), channel_id=1, source_target_pairs={{0,2},{1,3},{2,0},{3,1},{4,6},{5,7},{6,4},{7,5},{8,10},{9,11},{10,... | collective-permute-start | bytes 6152 | tf_op jit(solution)/shard_map/ppermute | solution.py:31
  19.1 5.1 %collective-permute-start.2 = (f32[512]{0:T(512)S(1)}, f32[512]{0:T(512)S(1)}, u32[]{:S(2)}, u32[]{:S(2)}) collective-permute-start(f32[512]{0:T(512)S(1)} %add.119), channel_id=1, source_target_pairs={{0,4},{1,5},{2,6},{3,7},{4,0},{5,1},{6,2},{7,3},{8,12},{9,13},{10,... | collective-permute-start | bytes 6152 | tf_op jit(solution)/shard_map/ppermute | solution.py:31
  24.5 3.7 %collective-permute-start.3 = (f32[2048]{0:T(1024)S(1)}, f32[2048]{0:T(1024)S(1)}, u32[]{:S(2)}, u32[]{:S(2)}) collective-permute-start(f32[2048]{0:T(1024)S(1)} %multiply_reduce_fusion.3), channel_id=1, source_target_pairs={{0,8},{8,0},{16,24},{24,16},{32,40},{40,32},{48,56},{56,48},{64,72... | collective-permute-start | bytes 24584 | tf_op jit(solution)/shard_map/ppermute | solution.py:31
  28.3 4.7 %collective-permute-start.4 = (f32[2048]{0:T(1024)S(1)}, f32[2048]{0:T(1024)S(1)}, u32[]{:S(2)}, u32[]{:S(2)}) collective-permute-start(f32[2048]{0:T(1024)S(1)} %add.121), channel_id=1, source_target_pairs={{0,16},{8,24},{16,0},{24,8},{32,48},{40,56},{48,32},{56,40},{64,80... | collective-permute-start | bytes 24584 | tf_op jit(solution)/shard_map/ppermute | solution.py:31
  33.0 8.5 %collective-permute-start.5 = (f32[2048]{0:T(1024)S(1)}, f32[2048]{0:T(1024)S(1)}, u32[]{:S(2)}, u32[]{:S(2)}) collective-permute-start(f32[2048]{0:T(1024)S(1)} %add.122), channel_id=1, source_target_pairs={{0,32},{8,40},{16,48},{24,56},{32,0},{40,8},{48,16},{56,24},{64,96... | collective-permute-start | bytes 24584 | tf_op jit(solution)/shard_map/ppermute | solution.py:31
  41.4 3.9 %collective-permute-start.6 = (f32[2048]{0:T(1024)S(1)}, f32[2048]{0:T(1024)S(1)}, u32[]{:S(2)}, u32[]{:S(2)}) collective-permute-start(f32[2048]{0:T(1024)S(1)} %add.123), channel_id=1, source_target_pairs={{0,64},{8,72},{16,80},{24,88},{32,96},{40,104},{48,112},{56,120},{... | collective-permute-start | bytes 24584 | tf_op jit(solution)/shard_map/ppermute | solution.py:31
  45.4 5.5 %collective-permute-start.7 = (f32[2048]{0:T(1024)S(1)}, f32[2048]{0:T(1024)S(1)}, u32[]{:S(2)}, u32[]{:S(2)}) collective-permute-start(f32[2048]{0:T(1024)S(1)} %add.124), channel_id=1, source_target_pairs={{0,128},{8,136},{16,144},{24,152},{32,160},{40,168},{48,176},{56,1... | collective-permute-start | bytes 24584 | tf_op jit(solution)/shard_map/ppermute | solution.py:31
  52.5 3.6 %collective-permute-start.9 = (f32[512]{0:T(512)S(1)}, f32[512]{0:T(512)S(1)}, u32[]{:S(2)}, u32[]{:S(2)}) collective-permute-start(f32[512]{0:T(512)S(1)} %add.126), channel_id=1, source_target_pairs={{0,2},{1,3},{2,0},{3,1},{4,6},{5,7},{6,4},{7,5},{8,10},{9,11},{10,... | collective-permute-start | bytes 6152 | tf_op jit(solution)/shard_map/ppermute | solution.py:31
  56.1 5.1 %collective-permute-start.10 = (f32[512]{0:T(512)S(1)}, f32[512]{0:T(512)S(1)}, u32[]{:S(2)}, u32[]{:S(2)}) collective-permute-start(f32[512]{0:T(512)S(1)} %add.127), channel_id=1, source_target_pairs={{0,4},{1,5},{2,6},{3,7},{4,0},{5,1},{6,2},{7,3},{8,12},{9,13},{10,... | collective-permute-start | bytes 6152 | tf_op jit(solution)/shard_map/ppermute | solution.py:31
  61.5 3.7 %collective-permute-start.11 = (f32[2048]{0:T(1024)S(1)}, f32[2048]{0:T(1024)S(1)}, u32[]{:S(2)}, u32[]{:S(2)}) collective-permute-start(f32[2048]{0:T(1024)S(1)} %multiply_reduce_fusion.1), channel_id=1, source_target_pairs={{0,8},{8,0},{16,24},{24,16},{32,40},{40,32},{48,56},{56,48},{64,72... | collective-permute-start | bytes 24584 | tf_op jit(solution)/shard_map/ppermute | solution.py:31
  65.3 4.5 %collective-permute-start.12 = (f32[2048]{0:T(1024)S(1)}, f32[2048]{0:T(1024)S(1)}, u32[]{:S(2)}, u32[]{:S(2)}) collective-permute-start(f32[2048]{0:T(1024)S(1)} %add.129), channel_id=1, source_target_pairs={{0,16},{8,24},{16,0},{24,8},{32,48},{40,56},{48,32},{56,40},{64,80... | collective-permute-start | bytes 24584 | tf_op jit(solution)/shard_map/ppermute | solution.py:31
  69.8 7.6 %collective-permute-start.13 = (f32[2048]{0:T(1024)S(1)}, f32[2048]{0:T(1024)S(1)}, u32[]{:S(2)}, u32[]{:S(2)}) collective-permute-start(f32[2048]{0:T(1024)S(1)} %add.130), channel_id=1, source_target_pairs={{0,32},{8,40},{16,48},{24,56},{32,0},{40,8},{48,16},{56,24},{64,96... | collective-permute-start | bytes 24584 | tf_op jit(solution)/shard_map/ppermute | solution.py:31
  77.4 3.9 %collective-permute-start.14 = (f32[2048]{0:T(1024)S(1)}, f32[2048]{0:T(1024)S(1)}, u32[]{:S(2)}, u32[]{:S(2)}) collective-permute-start(f32[2048]{0:T(1024)S(1)} %add.131), channel_id=1, source_target_pairs={{0,64},{8,72},{16,80},{24,88},{32,96},{40,104},{48,112},{56,120},{... | collective-permute-start | bytes 24584 | tf_op jit(solution)/shard_map/ppermute | solution.py:31
  81.3 5.2 %collective-permute-start.15 = (f32[2048]{0:T(1024)S(1)}, f32[2048]{0:T(1024)S(1)}, u32[]{:S(2)}, u32[]{:S(2)}) collective-permute-start(f32[2048]{0:T(1024)S(1)} %add.132), channel_id=1, source_target_pairs={{0,128},{8,136},{16,144},{24,152},{32,160},{40,168},{48,176},{56,1... | collective-permute-start | bytes 24584 | tf_op jit(solution)/shard_map/ppermute | solution.py:31
  88.1 3.6 %collective-permute-start.17 = (f32[512]{0:T(512)S(1)}, f32[512]{0:T(512)S(1)}, u32[]{:S(2)}, u32[]{:S(2)}) collective-permute-start(f32[512]{0:T(512)S(1)} %add.134), channel_id=1, source_target_pairs={{0,2},{1,3},{2,0},{3,1},{4,6},{5,7},{6,4},{7,5},{8,10},{9,11},{10,... | collective-permute-start | bytes 6152 | tf_op jit(solution)/shard_map/ppermute | solution.py:31
  91.7 5.1 %collective-permute-start.18 = (f32[512]{0:T(512)S(1)}, f32[512]{0:T(512)S(1)}, u32[]{:S(2)}, u32[]{:S(2)}) collective-permute-start(f32[512]{0:T(512)S(1)} %add.135), channel_id=1, source_target_pairs={{0,4},{1,5},{2,6},{3,7},{4,0},{5,1},{6,2},{7,3},{8,12},{9,13},{10,... | collective-permute-start | bytes 6152 | tf_op jit(solution)/shard_map/ppermute | solution.py:31
  96.9 3.7 %collective-permute-start.19 = (f32[4,512]{1,0:T(4,128)S(1)}, f32[4,512]{1,0:T(4,128)S(1)}, u32[]{:S(2)}, u32[]{:S(2)}) collective-permute-start(f32[4,512]{1,0:T(4,128)S(1)} %dynamic_update_slice.6), channel_id=1, source_target_pairs={{0,64},{64,0},{128,192},{192,128},{1,65},{65,1},{129,193},{193,129... | collective-permute-start | bytes 24584 | tf_op jit(solution)/shard_map/ppermute | solution.py:31
  100.7 5.2 %collective-permute-start.20 = (f32[4,512]{1,0:T(4,128)S(1)}, f32[4,512]{1,0:T(4,128)S(1)}, u32[]{:S(2)}, u32[]{:S(2)}) collective-permute-start(f32[4,512]{1,0:T(4,128)S(1)} %add.138), channel_id=1, source_target_pairs={{0,128},{64,192},{128,0},{192,64},{1,129},{65,193},{129,1},{193,65... | collective-permute-start | bytes 24584 | tf_op jit(solution)/shard_map/ppermute | solution.py:31
  114.5 3.7 %collective-permute-start.21 = (f32[512]{0:T(512)S(1)}, f32[512]{0:T(512)S(1)}, u32[]{:S(2)}, u32[]{:S(2)}) collective-permute-start(f32[512]{0:T(512)S(1)} %get-tuple-element.7), channel_id=1, source_target_pairs={{0,8},{8,0},{16,24},{24,16},{32,40},{40,32},{48,56},{56,48},{1,9},... | collective-permute-start | bytes 6152 | tf_op jit(solution)/shard_map/ppermute | solution.py:31
  118.2 4.5 %collective-permute-start.22 = (f32[512]{0:T(512)S(1)}, f32[512]{0:T(512)S(1)}, u32[]{:S(2)}, u32[]{:S(2)}) collective-permute-start(f32[512]{0:T(512)S(1)} %add.143), channel_id=1, source_target_pairs={{0,16},{8,24},{16,0},{24,8},{32,48},{40,56},{48,32},{56,40},{1,17}... | collective-permute-start | bytes 6152 | tf_op jit(solution)/shard_map/ppermute | solution.py:31
  122.7 7.5 %collective-permute-start.23 = (f32[512]{0:T(512)S(1)}, f32[512]{0:T(512)S(1)}, u32[]{:S(2)}, u32[]{:S(2)}) collective-permute-start(f32[512]{0:T(512)S(1)} %add.144), channel_id=1, source_target_pairs={{0,32},{8,40},{16,48},{24,56},{32,0},{40,8},{48,16},{56,24},{1,33}... | collective-permute-start | bytes 6152 | tf_op jit(solution)/shard_map/ppermute | solution.py:31
  (6 other events, 15.5 us)
Sparse Core Ops, SparseCore 0:
  10.7 71.4 all-gather.1
  114.6 42.1 reduce-scatter.1

commit v8 on v6

--- a/solution.py
+++ b/solution.py
@@ -22,23 +22,25 @@
 
 
 def doubling_sum(x, axes):
-    n = 1
     for a in axes:
-        n *= lax.axis_size(a)
-    step = 1
-    while step < n:
-        pairs = [(i, i ^ step) for i in range(n)]
-        x = x + lax.ppermute(x, axes, pairs)
-        step *= 2
+        n = lax.axis_size(a)
+        step = 1
+        while step < n:
+            if 2 * step == n:
+                pairs = [(i, n - 1 - i) for i in range(n)]
+            else:
+                pairs = [(i, i ^ step) for i in range(n)]
+            x = x + lax.ppermute(x, a, pairs)
+            step *= 2
     return x
 
 
 def cent_sum(x):
-    return doubling_sum(x, ("cx", "core"))
+    return doubling_sum(x, ("core", "cx"))
 
 
 def dp_sum(x):
-    return doubling_sum(x, ("dy", "dz"))
+    return doubling_sum(x, ("dz", "dy"))
 
 
 def doubling_gather(x, axis):

time: 166 us -> 161 us (0.970)
  starting transfers between devices: 45.7 us -> 42.2 us
    ppermute x21, waiting for transfers between devices: 43.3 us -> 39.2 us  [doubling_sum(): x = x + lax.ppermute(x, a, pairs)]
    ppermute x21, starting transfers between devices: 45.7 us -> 42.2 us  [doubling_sum(): x = x + lax.ppermute(x, a, pairs)]
    reduce_scatter x1, waiting for transfers between devices: 22.3 us -> 25.2 us  [shards(): lax.psum_scatter((weighted, col_mass), 'dz', scatter_dimension=0, tiled=T...]
where the time goes in v8:
time: 161 us
  waiting for transfers between devices  64.4 us (40%)
  starting transfers between devices  42.2 us (26%)
  blocking collectives  19 us (12%)
  between operations  14.9 us (9%)
  matrix products  10.6 us (7%)
  other arithmetic  8.52 us (5%)
    ppermute x21, starting transfers between devices, doubling_sum(): x = x + lax.ppermute(x, a, pairs)  42.2 us
    ppermute x21, waiting for transfers between devices, doubling_sum(): x = x + lax.ppermute(x, a, pairs)  39.2 us
    reduce_scatter x1, waiting for transfers between devices, shards(): lax.psum_scatter((weighted, col_mass), 'dz', scatter_dimension=0, tiled=T...  25.2 us
    unnamed x1, blocking collectives  19 us
    dot_general x1, matrix products, shards(): lax.dot_general(gathered, sub_normed, (((1,), (1,)), ((), ())), preferred...  5.49 us
  transfers between devices with their start and end apart: 23, of which 22 were waited for; matrix products, arithmetic and copies ran while one was open for 4% of the time, Pallas kernels for 0%

profile of v8, /device:TPU:2, one launch (start us, length us, event | category | flops | bytes accessed | tf_op | source)
XLA Modules:
  0.0 161.0 jit_solution(7440590085891438639)
XLA Ops:
  8.1 2.5 %convert_multiply_fusion.2 = f32[512,768]{1,0:T(8,128)} fusion(bf16[512,768]{1,0:T(8,128)(2,1)} %param.2, f32[512]{0:T(512)S(1)} %add_rsqrt_fusion.1), kind=kLoop, calls=%fused_computation.12 | loop fusion | flops 786432 | bytes 2361344 | tf_op jit(solution)/shard_map/mul | solution.py:17
  12.0 2.0 %fusion.8 = (f32[512]{0:T(512)S(1)}, f32[512,2048]{1,0:T(8,128)S(1)}) fusion(bf16[2048,768]{1,0:T(8,128)(2,1)S(1)} %fusion.1, f32[512]{0:T(512)S(1)} %add_rsqrt_fusion.1, bf16[512,768]{1,0:T(8,128)(2,1)S(1)} %copy-done.3), kind=kOutput, calls=%fused_computation.30 | convolution fusion | flops 1613889024 | bytes 8130560 | tf_op jit(solution)/shard_map/dot_general | solution.py:64
  15.3 2.2 %collective-permute-start.1 = (f32[512]{0:T(512)S(1)}, f32[512]{0:T(512)S(1)}, u32[]{:S(2)}, u32[]{:S(2)}) collective-permute-start(f32[512]{0:T(512)S(1)} %add.108), channel_id=1, source_target_pairs={{0,2},{2,0},{4,6},{6,4},{1,3},{3,1},{5,7},{7,5},{8,10},{10,8},{12,... | collective-permute-start | bytes 6152 | tf_op jit(solution)/shard_map/ppermute | solution.py:33
  20.4 2.3 %collective-permute-done.2 = f32[512]{0:T(512)S(1)} collective-permute-done((f32[512]{0:T(512)S(1)}, f32[512]{0:T(512)S(1)}, u32[]{:S(2)}, u32[]{:S(2)}) %collective-permute-start.2) | collective-permute-done | bytes 2080 | tf_op jit(solution)/shard_map/ppermute | solution.py:33
  26.8 3.0 %collective-permute-start.4 = (f32[2048]{0:T(1024)S(1)}, f32[2048]{0:T(1024)S(1)}, u32[]{:S(2)}, u32[]{:S(2)}) collective-permute-start(f32[2048]{0:T(1024)S(1)} %add.111), channel_id=1, source_target_pairs={{0,16},{8,24},{16,0},{24,8},{32,48},{40,56},{48,32},{56,40},{1,17}... | collective-permute-start | bytes 24584 | tf_op jit(solution)/shard_map/ppermute | solution.py:33
  31.5 5.5 %collective-permute-start.5 = (f32[2048]{0:T(1024)S(1)}, f32[2048]{0:T(1024)S(1)}, u32[]{:S(2)}, u32[]{:S(2)}) collective-permute-start(f32[2048]{0:T(1024)S(1)} %add.112), channel_id=1, source_target_pairs={{0,56},{8,48},{16,40},{24,32},{32,24},{40,16},{48,8},{56,0},{1,57}... | collective-permute-start | bytes 24584 | tf_op jit(solution)/shard_map/ppermute | solution.py:33
  40.2 2.4 %collective-permute-done.6 = f32[2048]{0:T(1024)S(1)} collective-permute-done((f32[2048]{0:T(1024)S(1)}, f32[2048]{0:T(1024)S(1)}, u32[]{:S(2)}, u32[]{:S(2)}) %collective-permute-start.6) | collective-permute-done | bytes 8224 | tf_op jit(solution)/shard_map/ppermute | solution.py:33
  42.6 3.0 %collective-permute-start.7 = (f32[2048]{0:T(1024)S(1)}, f32[2048]{0:T(1024)S(1)}, u32[]{:S(2)}, u32[]{:S(2)}) collective-permute-start(f32[2048]{0:T(1024)S(1)} %add.114), channel_id=1, source_target_pairs={{0,192},{64,128},{128,64},{192,0},{1,193},{65,129},{129,65},{193,1... | collective-permute-start | bytes 24584 | tf_op jit(solution)/shard_map/ppermute | solution.py:33
  45.6 2.1 %collective-permute-done.7 = f32[2048]{0:T(1024)S(1)} collective-permute-done((f32[2048]{0:T(1024)S(1)}, f32[2048]{0:T(1024)S(1)}, u32[]{:S(2)}, u32[]{:S(2)}) %collective-permute-start.7) | collective-permute-done | bytes 8224 | tf_op jit(solution)/shard_map/ppermute | solution.py:33
  56.9 2.0 %collective-permute-start.11 = (f32[2048]{0:T(1024)S(1)}, f32[2048]{0:T(1024)S(1)}, u32[]{:S(2)}, u32[]{:S(2)}) collective-permute-start(f32[2048]{0:T(1024)S(1)} %multiply_reduce_fusion.1), channel_id=1, source_target_pairs={{0,8},{8,0},{16,24},{24,16},{32,40},{40,32},{48,56},{56,48},{1,9},... | collective-permute-start | bytes 24584 | tf_op jit(solution)/shard_map/ppermute | solution.py:33
  60.6 2.5 %collective-permute-start.12 = (f32[2048]{0:T(1024)S(1)}, f32[2048]{0:T(1024)S(1)}, u32[]{:S(2)}, u32[]{:S(2)}) collective-permute-start(f32[2048]{0:T(1024)S(1)} %add.119), channel_id=1, source_target_pairs={{0,16},{8,24},{16,0},{24,8},{32,48},{40,56},{48,32},{56,40},{1,17}... | collective-permute-start | bytes 24584 | tf_op jit(solution)/shard_map/ppermute | solution.py:33
  63.1 2.1 %collective-permute-done.12 = f32[2048]{0:T(1024)S(1)} collective-permute-done((f32[2048]{0:T(1024)S(1)}, f32[2048]{0:T(1024)S(1)}, u32[]{:S(2)}, u32[]{:S(2)}) %collective-permute-start.12) | collective-permute-done | bytes 8224 | tf_op jit(solution)/shard_map/ppermute | solution.py:33
  65.2 4.0 %collective-permute-start.13 = (f32[2048]{0:T(1024)S(1)}, f32[2048]{0:T(1024)S(1)}, u32[]{:S(2)}, u32[]{:S(2)}) collective-permute-start(f32[2048]{0:T(1024)S(1)} %add.120), channel_id=1, source_target_pairs={{0,56},{8,48},{16,40},{24,32},{32,24},{40,16},{48,8},{56,0},{1,57}... | collective-permute-start | bytes 24584 | tf_op jit(solution)/shard_map/ppermute | solution.py:33
  71.2 3.6 %collective-permute-done.14 = f32[2048]{0:T(1024)S(1)} collective-permute-done((f32[2048]{0:T(1024)S(1)}, f32[2048]{0:T(1024)S(1)}, u32[]{:S(2)}, u32[]{:S(2)}) %collective-permute-start.14) | collective-permute-done | bytes 8224 | tf_op jit(solution)/shard_map/ppermute | solution.py:33
  74.8 3.0 %collective-permute-start.15 = (f32[2048]{0:T(1024)S(1)}, f32[2048]{0:T(1024)S(1)}, u32[]{:S(2)}, u32[]{:S(2)}) collective-permute-start(f32[2048]{0:T(1024)S(1)} %add.122), channel_id=1, source_target_pairs={{0,192},{64,128},{128,64},{192,0},{1,193},{65,129},{129,65},{193,1... | collective-permute-start | bytes 24584 | tf_op jit(solution)/shard_map/ppermute | solution.py:33
  77.8 2.1 %collective-permute-done.15 = f32[2048]{0:T(1024)S(1)} collective-permute-done((f32[2048]{0:T(1024)S(1)}, f32[2048]{0:T(1024)S(1)}, u32[]{:S(2)}, u32[]{:S(2)}) %collective-permute-start.15) | collective-permute-done | bytes 8224 | tf_op jit(solution)/shard_map/ppermute | solution.py:33
  81.6 2.7 %collective-permute-start.17 = (f32[512]{0:T(512)S(1)}, f32[512]{0:T(512)S(1)}, u32[]{:S(2)}, u32[]{:S(2)}) collective-permute-start(f32[512]{0:T(512)S(1)} %add.124), channel_id=1, source_target_pairs={{0,2},{2,0},{4,6},{6,4},{1,3},{3,1},{5,7},{7,5},{8,10},{10,8},{12,... | collective-permute-start | bytes 6152 | tf_op jit(solution)/shard_map/ppermute | solution.py:33
  85.8 2.1 %collective-permute-start.18 = (f32[512]{0:T(512)S(1)}, f32[512]{0:T(512)S(1)}, u32[]{:S(2)}, u32[]{:S(2)}) collective-permute-start(f32[512]{0:T(512)S(1)} %add.125), channel_id=1, source_target_pairs={{0,6},{2,4},{4,2},{6,0},{1,7},{3,5},{5,3},{7,1},{8,14},{10,12},{12... | collective-permute-start | bytes 6152 | tf_op jit(solution)/shard_map/ppermute | solution.py:33
  89.7 3.6 %collective-permute-done.19 = f32[4,512]{1,0:T(4,128)S(1)} collective-permute-done((f32[4,512]{1,0:T(4,128)S(1)}, f32[4,512]{1,0:T(4,128)S(1)}, u32[]{:S(2)}, u32[]{:S(2)}) %collective-permute-start.19) | collective-permute-done | bytes 8224 | tf_op jit(solution)/shard_map/ppermute | solution.py:33
  93.4 3.1 %collective-permute-start.20 = (f32[4,512]{1,0:T(4,128)S(1)}, f32[4,512]{1,0:T(4,128)S(1)}, u32[]{:S(2)}, u32[]{:S(2)}) collective-permute-start(f32[4,512]{1,0:T(4,128)S(1)} %add.128), channel_id=1, source_target_pairs={{0,192},{64,128},{128,64},{192,0},{1,193},{65,129},{129,65},{193,1... | collective-permute-start | bytes 24584 | tf_op jit(solution)/shard_map/ppermute | solution.py:33
  98.4 5.5 %convert_reduce_fusion = (f32[512]{0:T(512)S(1)}, bf16[2048,512]{1,0:T(8,128)(2,1)S(1)}) fusion(f32[512]{0:T(512)S(1)} %dynamic_slice.7, bf16[2048,768]{1,0:T(8,128)(2,1)} %copy-done.2, s32[]{:T(128)S(6)} %select_n.9, f32[2048,768]{1,0:T(8,128)} %all-gather.2.cloned.1.call-done, f32[]{:T(128)} %bitcast.1, f32[2048]{0:T(1024)S(1)} %bitcast.10), kind=kOutput, calls=%fused_computation.5 | convolution fusion | flops 1620049408 | bytes 9187844 | tf_op jit(solution)/shard_map/dot_general | solution.py:86
  103.9 3.1 %fusion.3 = f32[512,768]{1,0:T(8,128)} fusion(bf16[2048,512]{1,0:T(8,128)(2,1)S(1)} %get-tuple-element.8, f32[2048,768]{1,0:T(8,128)S(1)} %copy-done.1, f32[]{:T(128)} %bitcast.1), kind=kOutput, calls=%fused_computation.15 | convolution fusion | flops 1613758464 | bytes 9961476 | tf_op jit(solution)/shard_map/dot_general | solution.py:94
  108.2 19.0 %all-reduce = f32[512]{0:T(512)S(1)} all-reduce(f32[512]{0:T(512)S(1)} %get-tuple-element.7), channel_id=3, replica_groups=mesh['dy'=4,'dz'=8,'cx'=4,'core'=2] {'dz'}, use_global_device_ids=true, to_apply=%region_9.10.clone | all-reduce | flops 512 | bytes 4096
  127.3 25.2 %reduce-scatter.2.cloned.1.call-done = f32[64,768]{1,0:T(8,128)} async-done(((f32[512,768]{1,0:T(8,128)}), f32[64,768]{1,0:T(8,128)}) %reduce-scatter.2.cloned.1.call-update) | async-done | bytes 196624 | tf_op jit(solution)/shard_map/reduce_scatter | solution.py:97
  (78 shorter events, 37.3 us)
Async XLA Ops:
  6.5 91.8 %all-gather.2.cloned.1.call-start = ((), (), s32[]{:S(2)}) async-start(), calls=%async_computation.1 | async-start | bytes 7864320 | tf_op jit(solution)/shard_map/all_gather | solution.py:78
  10.6 141.9 %reduce-scatter.2.cloned.1.call-start = ((), (), s32[]{:S(2)}) async-start(), calls=%async_computation.2 | async-start | bytes 1769472 | tf_op jit(solution)/shard_map/reduce_scatter | solution.py:97
  14.0 1.3 collective-permute-start
  15.3 3.8 %collective-permute-start.1 = (f32[512]{0:T(512)S(1)}, f32[512]{0:T(512)S(1)}, u32[]{:S(2)}, u32[]{:S(2)}) collective-permute-start(f32[512]{0:T(512)S(1)} %add.108), channel_id=1, source_target_pairs={{0,2},{2,0},{4,6},{6,4},{1,3},{3,1},{5,7},{7,5},{8,10},{10,8},{12,... | collective-permute-start | bytes 6152 | tf_op jit(solution)/shard_map/ppermute | solution.py:33
  19.1 3.6 %collective-permute-start.2 = (f32[512]{0:T(512)S(1)}, f32[512]{0:T(512)S(1)}, u32[]{:S(2)}, u32[]{:S(2)}) collective-permute-start(f32[512]{0:T(512)S(1)} %add.109), channel_id=1, source_target_pairs={{0,6},{2,4},{4,2},{6,0},{1,7},{3,5},{5,3},{7,1},{8,14},{10,12},{12... | collective-permute-start | bytes 6152 | tf_op jit(solution)/shard_map/ppermute | solution.py:33
  23.0 3.7 %collective-permute-start.3 = (f32[2048]{0:T(1024)S(1)}, f32[2048]{0:T(1024)S(1)}, u32[]{:S(2)}, u32[]{:S(2)}) collective-permute-start(f32[2048]{0:T(1024)S(1)} %multiply_reduce_fusion.3), channel_id=1, source_target_pairs={{0,8},{8,0},{16,24},{24,16},{32,40},{40,32},{48,56},{56,48},{1,9},... | collective-permute-start | bytes 24584 | tf_op jit(solution)/shard_map/ppermute | solution.py:33
  26.8 4.7 %collective-permute-start.4 = (f32[2048]{0:T(1024)S(1)}, f32[2048]{0:T(1024)S(1)}, u32[]{:S(2)}, u32[]{:S(2)}) collective-permute-start(f32[2048]{0:T(1024)S(1)} %add.111), channel_id=1, source_target_pairs={{0,16},{8,24},{16,0},{24,8},{32,48},{40,56},{48,32},{56,40},{1,17}... | collective-permute-start | bytes 24584 | tf_op jit(solution)/shard_map/ppermute | solution.py:33
  31.5 7.1 %collective-permute-start.5 = (f32[2048]{0:T(1024)S(1)}, f32[2048]{0:T(1024)S(1)}, u32[]{:S(2)}, u32[]{:S(2)}) collective-permute-start(f32[2048]{0:T(1024)S(1)} %add.112), channel_id=1, source_target_pairs={{0,56},{8,48},{16,40},{24,32},{32,24},{40,16},{48,8},{56,0},{1,57}... | collective-permute-start | bytes 24584 | tf_op jit(solution)/shard_map/ppermute | solution.py:33
  38.6 3.9 %collective-permute-start.6 = (f32[2048]{0:T(1024)S(1)}, f32[2048]{0:T(1024)S(1)}, u32[]{:S(2)}, u32[]{:S(2)}) collective-permute-start(f32[2048]{0:T(1024)S(1)} %add.113), channel_id=1, source_target_pairs={{0,64},{64,0},{128,192},{192,128},{1,65},{65,1},{129,193},{193,129... | collective-permute-start | bytes 24584 | tf_op jit(solution)/shard_map/ppermute | solution.py:33
  42.6 5.2 %collective-permute-start.7 = (f32[2048]{0:T(1024)S(1)}, f32[2048]{0:T(1024)S(1)}, u32[]{:S(2)}, u32[]{:S(2)}) collective-permute-start(f32[2048]{0:T(1024)S(1)} %add.114), channel_id=1, source_target_pairs={{0,192},{64,128},{128,64},{192,0},{1,193},{65,129},{129,65},{193,1... | collective-permute-start | bytes 24584 | tf_op jit(solution)/shard_map/ppermute | solution.py:33
  48.1 1.2 collective-permute-start.8
  49.3 3.6 %collective-permute-start.9 = (f32[512]{0:T(512)S(1)}, f32[512]{0:T(512)S(1)}, u32[]{:S(2)}, u32[]{:S(2)}) collective-permute-start(f32[512]{0:T(512)S(1)} %add.116), channel_id=1, source_target_pairs={{0,2},{2,0},{4,6},{6,4},{1,3},{3,1},{5,7},{7,5},{8,10},{10,8},{12,... | collective-permute-start | bytes 6152 | tf_op jit(solution)/shard_map/ppermute | solution.py:33
  52.9 3.6 %collective-permute-start.10 = (f32[512]{0:T(512)S(1)}, f32[512]{0:T(512)S(1)}, u32[]{:S(2)}, u32[]{:S(2)}) collective-permute-start(f32[512]{0:T(512)S(1)} %add.117), channel_id=1, source_target_pairs={{0,6},{2,4},{4,2},{6,0},{1,7},{3,5},{5,3},{7,1},{8,14},{10,12},{12... | collective-permute-start | bytes 6152 | tf_op jit(solution)/shard_map/ppermute | solution.py:33
  56.9 3.7 %collective-permute-start.11 = (f32[2048]{0:T(1024)S(1)}, f32[2048]{0:T(1024)S(1)}, u32[]{:S(2)}, u32[]{:S(2)}) collective-permute-start(f32[2048]{0:T(1024)S(1)} %multiply_reduce_fusion.1), channel_id=1, source_target_pairs={{0,8},{8,0},{16,24},{24,16},{32,40},{40,32},{48,56},{56,48},{1,9},... | collective-permute-start | bytes 24584 | tf_op jit(solution)/shard_map/ppermute | solution.py:33
  60.6 4.5 %collective-permute-start.12 = (f32[2048]{0:T(1024)S(1)}, f32[2048]{0:T(1024)S(1)}, u32[]{:S(2)}, u32[]{:S(2)}) collective-permute-start(f32[2048]{0:T(1024)S(1)} %add.119), channel_id=1, source_target_pairs={{0,16},{8,24},{16,0},{24,8},{32,48},{40,56},{48,32},{56,40},{1,17}... | collective-permute-start | bytes 24584 | tf_op jit(solution)/shard_map/ppermute | solution.py:33
  65.2 5.7 %collective-permute-start.13 = (f32[2048]{0:T(1024)S(1)}, f32[2048]{0:T(1024)S(1)}, u32[]{:S(2)}, u32[]{:S(2)}) collective-permute-start(f32[2048]{0:T(1024)S(1)} %add.120), channel_id=1, source_target_pairs={{0,56},{8,48},{16,40},{24,32},{32,24},{40,16},{48,8},{56,0},{1,57}... | collective-permute-start | bytes 24584 | tf_op jit(solution)/shard_map/ppermute | solution.py:33
  70.8 4.0 %collective-permute-start.14 = (f32[2048]{0:T(1024)S(1)}, f32[2048]{0:T(1024)S(1)}, u32[]{:S(2)}, u32[]{:S(2)}) collective-permute-start(f32[2048]{0:T(1024)S(1)} %add.121), channel_id=1, source_target_pairs={{0,64},{64,0},{128,192},{192,128},{1,65},{65,1},{129,193},{193,129... | collective-permute-start | bytes 24584 | tf_op jit(solution)/shard_map/ppermute | solution.py:33
  74.8 5.2 %collective-permute-start.15 = (f32[2048]{0:T(1024)S(1)}, f32[2048]{0:T(1024)S(1)}, u32[]{:S(2)}, u32[]{:S(2)}) collective-permute-start(f32[2048]{0:T(1024)S(1)} %add.122), channel_id=1, source_target_pairs={{0,192},{64,128},{128,64},{192,0},{1,193},{65,129},{129,65},{193,1... | collective-permute-start | bytes 24584 | tf_op jit(solution)/shard_map/ppermute | solution.py:33
  80.3 1.2 collective-permute-start.16
  81.6 4.2 %collective-permute-start.17 = (f32[512]{0:T(512)S(1)}, f32[512]{0:T(512)S(1)}, u32[]{:S(2)}, u32[]{:S(2)}) collective-permute-start(f32[512]{0:T(512)S(1)} %add.124), channel_id=1, source_target_pairs={{0,2},{2,0},{4,6},{6,4},{1,3},{3,1},{5,7},{7,5},{8,10},{10,8},{12,... | collective-permute-start | bytes 6152 | tf_op jit(solution)/shard_map/ppermute | solution.py:33
  85.8 3.7 %collective-permute-start.18 = (f32[512]{0:T(512)S(1)}, f32[512]{0:T(512)S(1)}, u32[]{:S(2)}, u32[]{:S(2)}) collective-permute-start(f32[512]{0:T(512)S(1)} %add.125), channel_id=1, source_target_pairs={{0,6},{2,4},{4,2},{6,0},{1,7},{3,5},{5,3},{7,1},{8,14},{10,12},{12... | collective-permute-start | bytes 6152 | tf_op jit(solution)/shard_map/ppermute | solution.py:33
  89.6 3.7 %collective-permute-start.19 = (f32[4,512]{1,0:T(4,128)S(1)}, f32[4,512]{1,0:T(4,128)S(1)}, u32[]{:S(2)}, u32[]{:S(2)}) collective-permute-start(f32[4,512]{1,0:T(4,128)S(1)} %dynamic_update_slice.6), channel_id=1, source_target_pairs={{0,64},{64,0},{128,192},{192,128},{1,65},{65,1},{129,193},{193,129... | collective-permute-start | bytes 24584 | tf_op jit(solution)/shard_map/ppermute | solution.py:33
  93.4 4.9 %collective-permute-start.20 = (f32[4,512]{1,0:T(4,128)S(1)}, f32[4,512]{1,0:T(4,128)S(1)}, u32[]{:S(2)}, u32[]{:S(2)}) collective-permute-start(f32[4,512]{1,0:T(4,128)S(1)} %add.128), channel_id=1, source_target_pairs={{0,192},{64,128},{128,64},{192,0},{1,193},{65,129},{129,65},{193,1... | collective-permute-start | bytes 24584 | tf_op jit(solution)/shard_map/ppermute | solution.py:33
  98.4 5.5 %copy-start.1 = (f32[2048,768]{1,0:T(8,128)S(1)}, f32[2048,768]{1,0:T(8,128)}, u32[]{:S(2)}) copy-start(f32[2048,768]{1,0:T(8,128)} %all-gather.2.cloned.1.call-done) | copy-start | bytes 18874372
  (4 other events, 10.6 us)
Sparse Core Ops, SparseCore 0:
  10.7 71.4 all-gather.1
  107.1 45.3 reduce-scatter.1

commit v9 on v8

--- a/solution.py
+++ b/solution.py
@@ -50,6 +50,20 @@
     return doubling_sum(slots, (axis,)).reshape((n * x.shape[0],) + x.shape[1:])
 
 
+def ring_gather(x, axis):
+    n = lax.axis_size(axis)
+    blocks = [x]
+    for k in range(1, n):
+        blocks.append(lax.ppermute(x, axis, [(i, (i + k) % n) for i in range(n)]))
+    return jnp.concatenate(blocks, axis=0)
+
+
+def exchange_sum(x, axis):
+    n = lax.axis_size(axis)
+    parts = x.reshape((n, x.shape[0] // n) + x.shape[1:])
+    return jnp.sum(lax.all_to_all(parts, axis, 0, 0, tiled=False), axis=0)
+
+
 def row_update(boltzmann_affinity, column_factor):
     partial_rows = jnp.sum(boltzmann_affinity * column_factor[None, :], axis=1)
     return 1.0 / cent_sum(partial_rows)
@@ -75,10 +89,10 @@
         partial_cols = jnp.sum(row_weight[:, None] * boltzmann_affinity, axis=0)
         column_factor = balance_ratio / dp_sum(partial_cols)
     row_weight = row_update(boltzmann_affinity, column_factor)
-    gathered = lax.all_gather(scaled_rows, "dy", axis=0, tiled=True)
+    gathered = ring_gather(scaled_rows, "dy")
     unit = column_factor[0] * 0.0 + 1.0
     gathered = (gathered * unit).astype(jnp.bfloat16)
-    gathered_weight = doubling_gather(row_weight, "dy")
+    gathered_weight = ring_gather(row_weight, "dy")
     sub_cents = local_cents // ny
     start = lax.axis_index("dy") * sub_cents
     sub_normed = lax.dynamic_slice_in_dim(cent_normed, start, sub_cents, 0)
@@ -94,9 +108,8 @@
     weighted = lax.dot_general(
         transport, gathered, (((0,), (0,)), ((), ())), preferred_element_type=jnp.float32
     )
-    weighted, col_mass = lax.psum_scatter(
-        (weighted, col_mass), "dz", scatter_dimension=0, tiled=True
-    )
+    weighted = exchange_sum(weighted, "dz")
+    col_mass = exchange_sum(col_mass, "dz")
     return weighted / col_mass[:, None]
 
 

time: 161 us -> 193 us (1.20)
  starting transfers between devices: 42.2 us -> 73.1 us
  waiting for transfers between devices: 64.4 us -> 92.9 us
  blocking collectives: 19 us -> 0 us
  between operations: 14.9 us -> 0.79 us
  matrix products: 10.6 us -> 15.1 us
    all_to_all x0 -> x2, waiting for transfers between devices: none -> 37 us  [exchange_sum(): return jnp.sum(lax.all_to_all(parts, axis, 0, 0, tiled=False), axis=0)]
    reduce_scatter x1 -> x0, waiting for transfers between devices: 25.2 us -> none  [shards(): lax.psum_scatter((weighted, col_mass), 'dz', scatter_dimension=0, tiled=T...]
    unnamed x1 -> x0, blocking collectives: 19 us -> none
    ppermute x21 -> x19, starting transfers between devices: 42.2 us -> 55.4 us  [doubling_sum(): x = x + lax.ppermute(x, a, pairs)]
    all_to_all x0 -> x2, starting transfers between devices: none -> 13 us  [exchange_sum(): return jnp.sum(lax.all_to_all(parts, axis, 0, 0, tiled=False), axis=0)]
    ppermute x21 -> x19, waiting for transfers between devices: 39.2 us -> 50.2 us  [doubling_sum(): x = x + lax.ppermute(x, a, pairs)]
    ppermute x0 -> x6, waiting for transfers between devices: none -> 5.67 us  [ring_gather(): blocks.append(lax.ppermute(x, axis, [(i, (i + k) % n) for i in range(n)]))]
    ppermute x0 -> x6, starting transfers between devices: none -> 4.73 us  [ring_gather(): blocks.append(lax.ppermute(x, axis, [(i, (i + k) % n) for i in range(n)]))]
  transfers between devices with their start and end apart: 23 -> 27, of which waited for: 22 -> 22; matrix products, arithmetic and copies ran while one was open for 4% -> 5% of each run, Pallas kernels for 0% -> 0%
where the time goes in v9:
time: 193 us; the launch traced here: 191 us
  waiting for transfers between devices  92.9 us (48%)
  starting transfers between devices  73.1 us (38%)
  matrix products  15.1 us (8%)
  other arithmetic  7.32 us (4%)
    ppermute x19, starting transfers between devices, doubling_sum(): x = x + lax.ppermute(x, a, pairs)  55.4 us
    ppermute x19, waiting for transfers between devices, doubling_sum(): x = x + lax.ppermute(x, a, pairs)  50.2 us
    all_to_all x2, waiting for transfers between devices, exchange_sum(): return jnp.sum(lax.all_to_all(parts, axis, 0, 0, tiled=False), axis=0)  37 us
    all_to_all x2, starting transfers between devices, exchange_sum(): return jnp.sum(lax.all_to_all(parts, axis, 0, 0, tiled=False), axis=0)  13 us
    dot_general x1, matrix products, shards(): lax.dot_general(gathered, sub_normed, (((1,), (1,)), ((), ())), preferred...  6.55 us
    dot_general x1, matrix products, shards(): lax.dot_general(transport, gathered, (((0,), (0,)), ((), ())), preferred_...  6.5 us
    ppermute x6, waiting for transfers between devices, ring_gather(): blocks.append(lax.ppermute(x, axis, [(i, (i + k) % n) for i in range(n)]))  5.67 us
    ppermute x6, starting transfers between devices, ring_gather(): blocks.append(lax.ppermute(x, axis, [(i, (i + k) % n) for i in range(n)]))  4.73 us
  transfers between devices with their start and end apart: 27, of which 22 were waited for; matrix products, arithmetic and copies ran while one was open for 5% of the time, Pallas kernels for 0%

profile of v9, /device:TPU:2, one launch (start us, length us, event | category | flops | bytes accessed | tf_op | source)
XLA Modules:
  0.0 191.1 jit_solution(18272267686004169152)
XLA Ops:
  0.0 2.7 %fusion = f32[2048]{0:T(1024)S(1)} fusion(bf16[2048,768]{1,0:T(8,128)(2,1)} %param.3), kind=kLoop, calls=%fused_computation.2 | loop fusion | flops 4716544 | bytes 3153920 | tf_op jit(solution)/shard_map/reduce_sum | solution.py:16
  4.2 2.0 %fusion.13 = (f32[512]{0:T(512)S(1)}, f32[512,2048]{1,0:T(8,128)S(1)}) fusion(bf16[2048,768]{1,0:T(8,128)(2,1)S(1)} %fusion.1, f32[512]{0:T(512)S(1)} %add_rsqrt_fusion.1, bf16[512,768]{1,0:T(8,128)(2,1)S(1)} %copy-done.1), kind=kOutput, calls=%fused_computation.30 | convolution fusion | flops 1613889024 | bytes 8130560 | tf_op jit(solution)/shard_map/dot_general | solution.py:78
  7.5 2.2 %collective-permute-start.1 = (f32[512]{0:T(512)S(1)}, f32[512]{0:T(512)S(1)}, u32[]{:S(2)}, u32[]{:S(2)}) collective-permute-start(f32[512]{0:T(512)S(1)} %add.93), channel_id=1, source_target_pairs={{0,2},{2,0},{4,6},{6,4},{1,3},{3,1},{5,7},{7,5},{8,10},{10,8},{12,... | collective-permute-start | bytes 6152 | tf_op jit(solution)/shard_map/ppermute | solution.py:33
  12.6 2.3 %collective-permute-done.2 = f32[512]{0:T(512)S(1)} collective-permute-done((f32[512]{0:T(512)S(1)}, f32[512]{0:T(512)S(1)}, u32[]{:S(2)}, u32[]{:S(2)}) %collective-permute-start.2) | collective-permute-done | bytes 2080 | tf_op jit(solution)/shard_map/ppermute | solution.py:33
  17.0 2.0 %collective-permute-done.3 = f32[2048]{0:T(1024)S(1)} collective-permute-done((f32[2048]{0:T(1024)S(1)}, f32[2048]{0:T(1024)S(1)}, u32[]{:S(2)}, u32[]{:S(2)}) %collective-permute-start.3) | collective-permute-done | bytes 8224 | tf_op jit(solution)/shard_map/ppermute | solution.py:33
  19.0 3.0 %collective-permute-start.4 = (f32[2048]{0:T(1024)S(1)}, f32[2048]{0:T(1024)S(1)}, u32[]{:S(2)}, u32[]{:S(2)}) collective-permute-start(f32[2048]{0:T(1024)S(1)} %add.96), channel_id=1, source_target_pairs={{0,16},{8,24},{16,0},{24,8},{32,48},{40,56},{48,32},{56,40},{1,17}... | collective-permute-start | bytes 24584 | tf_op jit(solution)/shard_map/ppermute | solution.py:33
  23.7 5.5 %collective-permute-start.5 = (f32[2048]{0:T(1024)S(1)}, f32[2048]{0:T(1024)S(1)}, u32[]{:S(2)}, u32[]{:S(2)}) collective-permute-start(f32[2048]{0:T(1024)S(1)} %add.97), channel_id=1, source_target_pairs={{0,56},{8,48},{16,40},{24,32},{32,24},{40,16},{48,8},{56,0},{1,57}... | collective-permute-start | bytes 24584 | tf_op jit(solution)/shard_map/ppermute | solution.py:33
  32.4 2.1 %collective-permute-done.6 = f32[2048]{0:T(1024)S(1)} collective-permute-done((f32[2048]{0:T(1024)S(1)}, f32[2048]{0:T(1024)S(1)}, u32[]{:S(2)}, u32[]{:S(2)}) %collective-permute-start.6) | collective-permute-done | bytes 8224 | tf_op jit(solution)/shard_map/ppermute | solution.py:33
  34.5 3.1 %collective-permute-start.7 = (f32[2048]{0:T(1024)S(1)}, f32[2048]{0:T(1024)S(1)}, u32[]{:S(2)}, u32[]{:S(2)}) collective-permute-start(f32[2048]{0:T(1024)S(1)} %add.99), channel_id=1, source_target_pairs={{0,192},{64,128},{128,64},{192,0},{1,193},{65,129},{129,65},{193,1... | collective-permute-start | bytes 24584 | tf_op jit(solution)/shard_map/ppermute | solution.py:33
  51.4 2.0 %collective-permute-start.11 = (f32[2048]{0:T(1024)S(1)}, f32[2048]{0:T(1024)S(1)}, u32[]{:S(2)}, u32[]{:S(2)}) collective-permute-start(f32[2048]{0:T(1024)S(1)} %multiply_reduce_fusion.1), channel_id=1, source_target_pairs={{0,8},{8,0},{16,24},{24,16},{32,40},{40,32},{48,56},{56,48},{1,9},... | collective-permute-start | bytes 24584 | tf_op jit(solution)/shard_map/ppermute | solution.py:33
  55.1 2.4 %collective-permute-start.12 = (f32[2048]{0:T(1024)S(1)}, f32[2048]{0:T(1024)S(1)}, u32[]{:S(2)}, u32[]{:S(2)}) collective-permute-start(f32[2048]{0:T(1024)S(1)} %add.104), channel_id=1, source_target_pairs={{0,16},{8,24},{16,0},{24,8},{32,48},{40,56},{48,32},{56,40},{1,17}... | collective-permute-start | bytes 24584 | tf_op jit(solution)/shard_map/ppermute | solution.py:33
  57.6 2.1 %collective-permute-done.12 = f32[2048]{0:T(1024)S(1)} collective-permute-done((f32[2048]{0:T(1024)S(1)}, f32[2048]{0:T(1024)S(1)}, u32[]{:S(2)}, u32[]{:S(2)}) %collective-permute-start.12) | collective-permute-done | bytes 8224 | tf_op jit(solution)/shard_map/ppermute | solution.py:33
  59.7 4.0 %collective-permute-start.13 = (f32[2048]{0:T(1024)S(1)}, f32[2048]{0:T(1024)S(1)}, u32[]{:S(2)}, u32[]{:S(2)}) collective-permute-start(f32[2048]{0:T(1024)S(1)} %add.105), channel_id=1, source_target_pairs={{0,56},{8,48},{16,40},{24,32},{32,24},{40,16},{48,8},{56,0},{1,57}... | collective-permute-start | bytes 24584 | tf_op jit(solution)/shard_map/ppermute | solution.py:33
  65.3 20.9 %collective-permute-start.14 = (f32[2048]{0:T(1024)S(1)}, f32[2048]{0:T(1024)S(1)}, u32[]{:S(2)}, u32[]{:S(2)}) collective-permute-start(f32[2048]{0:T(1024)S(1)} %add.106), channel_id=1, source_target_pairs={{0,64},{64,0},{128,192},{192,128},{1,65},{65,1},{129,193},{193,129... | collective-permute-start | bytes 24584 | tf_op jit(solution)/shard_map/ppermute | solution.py:33
  86.2 18.1 %collective-permute-done.14 = f32[2048]{0:T(1024)S(1)} collective-permute-done((f32[2048]{0:T(1024)S(1)}, f32[2048]{0:T(1024)S(1)}, u32[]{:S(2)}, u32[]{:S(2)}) %collective-permute-start.14) | collective-permute-done | bytes 8224 | tf_op jit(solution)/shard_map/ppermute | solution.py:33
  104.4 4.9 %collective-permute-done.15 = f32[2048]{0:T(1024)S(1)} collective-permute-done((f32[2048]{0:T(1024)S(1)}, f32[2048]{0:T(1024)S(1)}, u32[]{:S(2)}, u32[]{:S(2)}) %collective-permute-start.15) | collective-permute-done | bytes 8224 | tf_op jit(solution)/shard_map/ppermute | solution.py:33
  114.5 1.9 collective-permute-start.18
  119.5 3.3 %collective-permute-done.19 = f32[512]{0:T(512)S(1)} collective-permute-done((f32[512]{0:T(512)S(1)}, f32[512]{0:T(512)S(1)}, u32[]{:S(2)}, u32[]{:S(2)}) %collective-permute-start.19) | collective-permute-done | bytes 2080 | tf_op jit(solution)/shard_map/ppermute | solution.py:57
  124.1 2.3 %collective-permute-done.21 = f32[512]{0:T(512)S(1)} collective-permute-done((f32[512]{0:T(512)S(1)}, f32[512]{0:T(512)S(1)}, u32[]{:S(2)}, u32[]{:S(2)}) %collective-permute-start.21) | collective-permute-done | bytes 2080 | tf_op jit(solution)/shard_map/ppermute | solution.py:57
  126.5 6.6 %convert_reduce_fusion = (f32[512]{0:T(512)S(1)}, bf16[2048,512]{1,0:T(8,128)(2,1)}) fusion(f32[512]{0:T(512)S(1)} %dynamic_slice.7, bf16[2048,768]{1,0:T(8,128)(2,1)S(1)} %fusion.1, s32[]{:T(128)S(6)} %select_n.4, f32[512,768]{1,0:T(8,128)} %collective-permute-done.24, f32[512,768]{1,0:T(8,128)} %collective-permute-done.23, ...), kind=kOutput, calls=%fused_computation.6 | convolution fusion | flops 1624768000 | bytes 9187336 | tf_op jit(solution)/shard_map/dot_general | solution.py:100
  133.7 6.9 %all-to-all-start.1 = ((f32[8,1,64]{2,1,0:T(1,128)}), f32[8,1,64]{2,1,0:T(1,128)S(1)}, u32[]{:S(2)}, u32[]{:S(2)}) async-start(f32[8,1,64]{2,1,0:T(1,128)} %all_to_all.10), calls=%async_computation.1 | async-start | bytes 8192 | tf_op jit(solution)/shard_map/all_to_all | solution.py:64
  140.6 6.5 %fusion.10 = f32[512,768]{1,0:T(8,128)} fusion(bf16[2048,512]{1,0:T(8,128)(2,1)} %get-tuple-element.8, f32[512,768]{1,0:T(8,128)} %collective-permute-done.24, f32[512,768]{1,0:T(8,128)} %collective-permute-done.23, f32[512,768]{1,0:T(8,128)} %collective-permute-done.22, f32[512,768]{1,0:T(8,128)} %convert_multiply_fusion.2, f32[]{:T(128)} %bitcast), kind=kOutput, calls=%fused_computation.29 | convolution fusion | flops 1618477056 | bytes 9961476 | tf_op jit(solution)/shard_map/dot_general | solution.py:108
  148.2 6.1 %all-to-all-start = ((f32[8,64,768]{2,1,0:T(8,128)}), f32[8,64,768]{2,1,0:T(8,128)S(1)}, u32[]{:S(2)}, u32[]{:S(2)}) async-start(f32[8,64,768]{2,1,0:T(8,128)} %bitcast.1), calls=%async_computation | async-start | bytes 3145728 | tf_op jit(solution)/shard_map/all_to_all | solution.py:64
  154.3 35.9 %all-to-all-done = f32[8,64,768]{2,1,0:T(8,128)S(1)} async-done(((f32[8,64,768]{2,1,0:T(8,128)}), f32[8,64,768]{2,1,0:T(8,128)S(1)}, u32[]{:S(2)}, u32[]{:S(2)}) %all-to-all-start) | async-done | bytes 1572896 | tf_op jit(solution)/shard_map/all_to_all | solution.py:64
  (73 shorter events, 41.4 us)
Async XLA Ops:
  7.5 3.8 %collective-permute-start.1 = (f32[512]{0:T(512)S(1)}, f32[512]{0:T(512)S(1)}, u32[]{:S(2)}, u32[]{:S(2)}) collective-permute-start(f32[512]{0:T(512)S(1)} %add.93), channel_id=1, source_target_pairs={{0,2},{2,0},{4,6},{6,4},{1,3},{3,1},{5,7},{7,5},{8,10},{10,8},{12,... | collective-permute-start | bytes 6152 | tf_op jit(solution)/shard_map/ppermute | solution.py:33
  11.3 3.6 %collective-permute-start.2 = (f32[512]{0:T(512)S(1)}, f32[512]{0:T(512)S(1)}, u32[]{:S(2)}, u32[]{:S(2)}) collective-permute-start(f32[512]{0:T(512)S(1)} %add.94), channel_id=1, source_target_pairs={{0,6},{2,4},{4,2},{6,0},{1,7},{3,5},{5,3},{7,1},{8,14},{10,12},{12... | collective-permute-start | bytes 6152 | tf_op jit(solution)/shard_map/ppermute | solution.py:33
  15.2 3.7 %collective-permute-start.3 = (f32[2048]{0:T(1024)S(1)}, f32[2048]{0:T(1024)S(1)}, u32[]{:S(2)}, u32[]{:S(2)}) collective-permute-start(f32[2048]{0:T(1024)S(1)} %multiply_reduce_fusion.3), channel_id=1, source_target_pairs={{0,8},{8,0},{16,24},{24,16},{32,40},{40,32},{48,56},{56,48},{1,9},... | collective-permute-start | bytes 24584 | tf_op jit(solution)/shard_map/ppermute | solution.py:33
  19.0 4.7 %collective-permute-start.4 = (f32[2048]{0:T(1024)S(1)}, f32[2048]{0:T(1024)S(1)}, u32[]{:S(2)}, u32[]{:S(2)}) collective-permute-start(f32[2048]{0:T(1024)S(1)} %add.96), channel_id=1, source_target_pairs={{0,16},{8,24},{16,0},{24,8},{32,48},{40,56},{48,32},{56,40},{1,17}... | collective-permute-start | bytes 24584 | tf_op jit(solution)/shard_map/ppermute | solution.py:33
  23.7 7.1 %collective-permute-start.5 = (f32[2048]{0:T(1024)S(1)}, f32[2048]{0:T(1024)S(1)}, u32[]{:S(2)}, u32[]{:S(2)}) collective-permute-start(f32[2048]{0:T(1024)S(1)} %add.97), channel_id=1, source_target_pairs={{0,56},{8,48},{16,40},{24,32},{32,24},{40,16},{48,8},{56,0},{1,57}... | collective-permute-start | bytes 24584 | tf_op jit(solution)/shard_map/ppermute | solution.py:33
  30.8 3.7 %collective-permute-start.6 = (f32[2048]{0:T(1024)S(1)}, f32[2048]{0:T(1024)S(1)}, u32[]{:S(2)}, u32[]{:S(2)}) collective-permute-start(f32[2048]{0:T(1024)S(1)} %add.98), channel_id=1, source_target_pairs={{0,64},{64,0},{128,192},{192,128},{1,65},{65,1},{129,193},{193,129... | collective-permute-start | bytes 24584 | tf_op jit(solution)/shard_map/ppermute | solution.py:33
  34.5 7.7 %collective-permute-start.7 = (f32[2048]{0:T(1024)S(1)}, f32[2048]{0:T(1024)S(1)}, u32[]{:S(2)}, u32[]{:S(2)}) collective-permute-start(f32[2048]{0:T(1024)S(1)} %add.99), channel_id=1, source_target_pairs={{0,192},{64,128},{128,64},{192,0},{1,193},{65,129},{129,65},{193,1... | collective-permute-start | bytes 24584 | tf_op jit(solution)/shard_map/ppermute | solution.py:33
  39.0 87.5 %collective-permute-start.22 = (f32[512,768]{1,0:T(8,128)}, f32[512,768]{1,0:T(8,128)}, u32[]{:S(2)}, u32[]{:S(2)}) collective-permute-start(f32[512,768]{1,0:T(8,128)} %convert_multiply_fusion.2), channel_id=1, source_target_pairs={{0,64},{64,128},{128,192},{192,0},{1,65},{65,129},{129,193},{193,1... | collective-permute-start | bytes 4718600 | tf_op jit(solution)/shard_map/ppermute | solution.py:57
  39.0 87.4 %collective-permute-start.23 = (f32[512,768]{1,0:T(8,128)}, f32[512,768]{1,0:T(8,128)}, u32[]{:S(2)}, u32[]{:S(2)}) collective-permute-start(f32[512,768]{1,0:T(8,128)} %convert_multiply_fusion.2), channel_id=1, source_target_pairs={{0,128},{64,192},{128,0},{192,64},{1,129},{65,193},{129,1},{193,65... | collective-permute-start | bytes 4718600 | tf_op jit(solution)/shard_map/ppermute | solution.py:57
  40.5 85.9 %collective-permute-start.24 = (f32[512,768]{1,0:T(8,128)}, f32[512,768]{1,0:T(8,128)}, u32[]{:S(2)}, u32[]{:S(2)}) collective-permute-start(f32[512,768]{1,0:T(8,128)} %convert_multiply_fusion.2), channel_id=1, source_target_pairs={{0,192},{64,0},{128,64},{192,128},{1,193},{65,1},{129,65},{193,129... | collective-permute-start | bytes 4718600 | tf_op jit(solution)/shard_map/ppermute | solution.py:57
  43.8 3.6 %collective-permute-start.9 = (f32[512]{0:T(512)S(1)}, f32[512]{0:T(512)S(1)}, u32[]{:S(2)}, u32[]{:S(2)}) collective-permute-start(f32[512]{0:T(512)S(1)} %add.101), channel_id=1, source_target_pairs={{0,2},{2,0},{4,6},{6,4},{1,3},{3,1},{5,7},{7,5},{8,10},{10,8},{12,... | collective-permute-start | bytes 6152 | tf_op jit(solution)/shard_map/ppermute | solution.py:33
  47.4 3.6 %collective-permute-start.10 = (f32[512]{0:T(512)S(1)}, f32[512]{0:T(512)S(1)}, u32[]{:S(2)}, u32[]{:S(2)}) collective-permute-start(f32[512]{0:T(512)S(1)} %add.102), channel_id=1, source_target_pairs={{0,6},{2,4},{4,2},{6,0},{1,7},{3,5},{5,3},{7,1},{8,14},{10,12},{12... | collective-permute-start | bytes 6152 | tf_op jit(solution)/shard_map/ppermute | solution.py:33
  51.4 3.7 %collective-permute-start.11 = (f32[2048]{0:T(1024)S(1)}, f32[2048]{0:T(1024)S(1)}, u32[]{:S(2)}, u32[]{:S(2)}) collective-permute-start(f32[2048]{0:T(1024)S(1)} %multiply_reduce_fusion.1), channel_id=1, source_target_pairs={{0,8},{8,0},{16,24},{24,16},{32,40},{40,32},{48,56},{56,48},{1,9},... | collective-permute-start | bytes 24584 | tf_op jit(solution)/shard_map/ppermute | solution.py:33
  55.1 4.5 %collective-permute-start.12 = (f32[2048]{0:T(1024)S(1)}, f32[2048]{0:T(1024)S(1)}, u32[]{:S(2)}, u32[]{:S(2)}) collective-permute-start(f32[2048]{0:T(1024)S(1)} %add.104), channel_id=1, source_target_pairs={{0,16},{8,24},{16,0},{24,8},{32,48},{40,56},{48,32},{56,40},{1,17}... | collective-permute-start | bytes 24584 | tf_op jit(solution)/shard_map/ppermute | solution.py:33
  59.7 5.6 %collective-permute-start.13 = (f32[2048]{0:T(1024)S(1)}, f32[2048]{0:T(1024)S(1)}, u32[]{:S(2)}, u32[]{:S(2)}) collective-permute-start(f32[2048]{0:T(1024)S(1)} %add.105), channel_id=1, source_target_pairs={{0,56},{8,48},{16,40},{24,32},{32,24},{40,16},{48,8},{56,0},{1,57}... | collective-permute-start | bytes 24584 | tf_op jit(solution)/shard_map/ppermute | solution.py:33
  65.3 39.0 %collective-permute-start.14 = (f32[2048]{0:T(1024)S(1)}, f32[2048]{0:T(1024)S(1)}, u32[]{:S(2)}, u32[]{:S(2)}) collective-permute-start(f32[2048]{0:T(1024)S(1)} %add.106), channel_id=1, source_target_pairs={{0,64},{64,0},{128,192},{192,128},{1,65},{65,1},{129,193},{193,129... | collective-permute-start | bytes 24584 | tf_op jit(solution)/shard_map/ppermute | solution.py:33
  104.4 4.9 %collective-permute-start.15 = (f32[2048]{0:T(1024)S(1)}, f32[2048]{0:T(1024)S(1)}, u32[]{:S(2)}, u32[]{:S(2)}) collective-permute-start(f32[2048]{0:T(1024)S(1)} %add.107), channel_id=1, source_target_pairs={{0,192},{64,128},{128,64},{192,0},{1,193},{65,129},{129,65},{193,1... | collective-permute-start | bytes 24584 | tf_op jit(solution)/shard_map/ppermute | solution.py:33
  110.9 3.6 %collective-permute-start.17 = (f32[512]{0:T(512)S(1)}, f32[512]{0:T(512)S(1)}, u32[]{:S(2)}, u32[]{:S(2)}) collective-permute-start(f32[512]{0:T(512)S(1)} %add.109), channel_id=1, source_target_pairs={{0,2},{2,0},{4,6},{6,4},{1,3},{3,1},{5,7},{7,5},{8,10},{10,8},{12,... | collective-permute-start | bytes 6152 | tf_op jit(solution)/shard_map/ppermute | solution.py:33
  114.5 3.6 %collective-permute-start.18 = (f32[512]{0:T(512)S(1)}, f32[512]{0:T(512)S(1)}, u32[]{:S(2)}, u32[]{:S(2)}) collective-permute-start(f32[512]{0:T(512)S(1)} %add.110), channel_id=1, source_target_pairs={{0,6},{2,4},{4,2},{6,0},{1,7},{3,5},{5,3},{7,1},{8,14},{10,12},{12... | collective-permute-start | bytes 6152 | tf_op jit(solution)/shard_map/ppermute | solution.py:33
  118.1 4.8 %collective-permute-start.19 = (f32[512]{0:T(512)S(1)}, f32[512]{0:T(512)S(1)}, u32[]{:S(2)}, u32[]{:S(2)}) collective-permute-start(f32[512]{0:T(512)S(1)} %add_divide_fusion.2), channel_id=1, source_target_pairs={{0,64},{64,128},{128,192},{192,0},{1,65},{65,129},{129,193},{193,1... | collective-permute-start | bytes 6152 | tf_op jit(solution)/shard_map/ppermute | solution.py:57
  118.1 6.0 %collective-permute-start.20 = (f32[512]{0:T(512)S(1)}, f32[512]{0:T(512)S(1)}, u32[]{:S(2)}, u32[]{:S(2)}) collective-permute-start(f32[512]{0:T(512)S(1)} %add_divide_fusion.2), channel_id=1, source_target_pairs={{0,128},{64,192},{128,0},{192,64},{1,129},{65,193},{129,1},{193,65... | collective-permute-start | bytes 6152 | tf_op jit(solution)/shard_map/ppermute | solution.py:57
  122.9 3.6 %collective-permute-start.21 = (f32[512]{0:T(512)S(1)}, f32[512]{0:T(512)S(1)}, u32[]{:S(2)}, u32[]{:S(2)}) collective-permute-start(f32[512]{0:T(512)S(1)} %add_divide_fusion.2), channel_id=1, source_target_pairs={{0,192},{64,0},{128,64},{192,128},{1,193},{65,1},{129,65},{193,129... | collective-permute-start | bytes 6152 | tf_op jit(solution)/shard_map/ppermute | solution.py:57
  133.7 14.5 %all-to-all-start.1 = ((f32[8,1,64]{2,1,0:T(1,128)}), f32[8,1,64]{2,1,0:T(1,128)S(1)}, u32[]{:S(2)}, u32[]{:S(2)}) async-start(f32[8,1,64]{2,1,0:T(1,128)} %all_to_all.10), calls=%async_computation.1 | async-start | bytes 8192 | tf_op jit(solution)/shard_map/all_to_all | solution.py:64
  148.2 42.0 %all-to-all-start = ((f32[8,64,768]{2,1,0:T(8,128)}), f32[8,64,768]{2,1,0:T(8,128)S(1)}, u32[]{:S(2)}, u32[]{:S(2)}) async-start(f32[8,64,768]{2,1,0:T(8,128)} %bitcast.1), calls=%async_computation | async-start | bytes 3145728 | tf_op jit(solution)/shard_map/all_to_all | solution.py:64
  (5 other events, 7.7 us)

commit v10 on v8

--- a/solution.py
+++ b/solution.py
@@ -40,7 +40,9 @@
 
 
 def dp_sum(x):
-    return doubling_sum(x, ("dz", "dy"))
+    n = lax.axis_size("dy") * lax.axis_size("dz")
+    copies = jnp.broadcast_to(x[None], (n,) + x.shape)
+    return jnp.sum(lax.all_to_all(copies, ("dy", "dz"), 0, 0, tiled=False), axis=0)
 
 
 def doubling_gather(x, axis):

time: 161 us -> 150 us (0.932)
  blocking collectives: 19 us -> 53.7 us
  starting transfers between devices: 42.2 us -> 14.6 us
  waiting for transfers between devices: 64.4 us -> 41.1 us
  other arithmetic: 8.52 us -> 13.3 us
    all_to_all x0 -> x2, blocking collectives: none -> 38 us  [dp_sum(): lax.all_to_all(copies, ('dy', 'dz'), 0, 0, tiled=False)]
    ppermute x21 -> x11, starting transfers between devices: 42.2 us -> 14.5 us  [doubling_sum(): x = x + lax.ppermute(x, a, pairs)]
    ppermute x21 -> x11, waiting for transfers between devices: 39.2 us -> 19.3 us  [doubling_sum(): x = x + lax.ppermute(x, a, pairs)]
    reduce_sum x2, other arithmetic: 0.73 us -> 5.24 us  [row_update(): partial_rows = jnp.sum(boltzmann_affinity * column_factor[None, :], axis=1)]
    reduce_scatter x1, waiting for transfers between devices: 25.2 us -> 21.7 us  [shards(): lax.psum_scatter((weighted, col_mass), 'dz', scatter_dimension=0, tiled=T...]
    unnamed x1, blocking collectives: 19 us -> 15.7 us
  transfers between devices with their start and end apart: 23 -> 13, of which waited for: 22 -> 12; matrix products, arithmetic and copies ran while one was open for 4% -> 8% of each run, Pallas kernels for 0% -> 0%
where the time goes in v10:
time: 150 us
  blocking collectives  53.7 us (36%)
  waiting for transfers between devices  41.1 us (27%)
  between operations  14.9 us (10%)
  starting transfers between devices  14.6 us (10%)
  other arithmetic  13.3 us (9%)
  matrix products  10.6 us (7%)
  local copies, waits for them, and re-layouts  1.65 us (1%)
    all_to_all x2, blocking collectives, dp_sum(): lax.all_to_all(copies, ('dy', 'dz'), 0, 0, tiled=False)  38 us
    reduce_scatter x1, waiting for transfers between devices, shards(): lax.psum_scatter((weighted, col_mass), 'dz', scatter_dimension=0, tiled=T...  21.7 us
    ppermute x11, waiting for transfers between devices, doubling_sum(): x = x + lax.ppermute(x, a, pairs)  19.3 us
    unnamed x1, blocking collectives  15.7 us
    ppermute x11, starting transfers between devices, doubling_sum(): x = x + lax.ppermute(x, a, pairs)  14.5 us
    dot_general x1, matrix products, shards(): lax.dot_general(gathered, sub_normed, (((1,), (1,)), ((), ())), preferred...  5.49 us
    reduce_sum x2, other arithmetic, row_update(): partial_rows = jnp.sum(boltzmann_affinity * column_factor[None, :], axis=1)  5.24 us
    dot_general x1, matrix products, shards(): lax.dot_general(transport, gathered, (((0,), (0,)), ((), ())), preferred_...  3.05 us
  transfers between devices with their start and end apart: 13, of which 12 were waited for; matrix products, arithmetic and copies ran while one was open for 8% of the time, Pallas kernels for 0%

profile of v10, /device:TPU:2, one launch (start us, length us, event | category | flops | bytes accessed | tf_op | source)
XLA Modules:
  0.0 149.9 jit_solution(793608759586358320)
XLA Ops:
  8.1 2.5 %convert_multiply_fusion.2 = f32[512,768]{1,0:T(8,128)} fusion(bf16[512,768]{1,0:T(8,128)(2,1)} %param.2, f32[512]{0:T(512)S(1)} %add_rsqrt_fusion.1), kind=kLoop, calls=%fused_computation.12 | loop fusion | flops 786432 | bytes 2361344 | tf_op jit(solution)/shard_map/mul | solution.py:17
  12.0 2.0 %fusion.8 = (f32[512]{0:T(512)S(1)}, f32[512,2048]{1,0:T(8,128)S(1)}) fusion(bf16[2048,768]{1,0:T(8,128)(2,1)S(1)} %fusion.1, f32[512]{0:T(512)S(1)} %add_rsqrt_fusion.1, bf16[512,768]{1,0:T(8,128)(2,1)S(1)} %copy-done.5), kind=kOutput, calls=%fused_computation.30 | convolution fusion | flops 1613889024 | bytes 8130560 | tf_op jit(solution)/shard_map/dot_general | solution.py:66
  15.3 2.2 %collective-permute-start.1 = (f32[512]{0:T(512)S(1)}, f32[512]{0:T(512)S(1)}, u32[]{:S(2)}, u32[]{:S(2)}) collective-permute-start(f32[512]{0:T(512)S(1)} %add.78), channel_id=1, source_target_pairs={{0,2},{2,0},{4,6},{6,4},{1,3},{3,1},{5,7},{7,5},{8,10},{10,8},{12,... | collective-permute-start | bytes 6152 | tf_op jit(solution)/shard_map/ppermute | solution.py:33
  17.5 1.6 %collective-permute-done.1 = f32[512]{0:T(512)S(1)} collective-permute-done((f32[512]{0:T(512)S(1)}, f32[512]{0:T(512)S(1)}, u32[]{:S(2)}, u32[]{:S(2)}) %collective-permute-start.1) | collective-permute-done | bytes 2080 | tf_op jit(solution)/shard_map/ppermute | solution.py:33
  20.4 2.3 %collective-permute-done.2 = f32[512]{0:T(512)S(1)} collective-permute-done((f32[512]{0:T(512)S(1)}, f32[512]{0:T(512)S(1)}, u32[]{:S(2)}, u32[]{:S(2)}) %collective-permute-start.2) | collective-permute-done | bytes 2080 | tf_op jit(solution)/shard_map/ppermute | solution.py:33
  23.2 22.1 %all_to_all.12 = f32[32,1,2048]{2,1,0:T(1,128)S(1)} all-to-all(f32[32,1,2048]{2,1,0:T(1,128)S(1)} %broadcast_in_dim.10), channel_id=1, replica_groups=mesh['dy'=4,'dz'=8,'cx'=4,'core'=2] {'dy','dz'}, dimensions={0} | all-to-all | bytes 524288 | tf_op jit(solution)/shard_map/all_to_all | solution.py:45
  45.5 2.7 %multiply_reduce_fusion.2 = f32[512]{0:T(512)S(1)} fusion(f32[512,2048]{1,0:T(8,128)} %copy-done, f32[2048]{0:T(1024)S(1)} %broadcast_divide_fusion.2), kind=kLoop, calls=%fused_computation.9 | loop fusion | flops 2096640 | bytes 4204544 | tf_op jit(solution)/shard_map/reduce_sum | solution.py:56
  49.5 1.8 %collective-permute-start.4 = (f32[512]{0:T(512)S(1)}, f32[512]{0:T(512)S(1)}, u32[]{:S(2)}, u32[]{:S(2)}) collective-permute-start(f32[512]{0:T(512)S(1)} %add.81), channel_id=1, source_target_pairs={{0,2},{2,0},{4,6},{6,4},{1,3},{3,1},{5,7},{7,5},{8,10},{10,8},{12,... | collective-permute-start | bytes 6152 | tf_op jit(solution)/shard_map/ppermute | solution.py:33
  51.3 1.8 %collective-permute-done.4 = f32[512]{0:T(512)S(1)} collective-permute-done((f32[512]{0:T(512)S(1)}, f32[512]{0:T(512)S(1)}, u32[]{:S(2)}, u32[]{:S(2)}) %collective-permute-start.4) | collective-permute-done | bytes 2080 | tf_op jit(solution)/shard_map/ppermute | solution.py:33
  53.1 1.9 %collective-permute-start.5 = (f32[512]{0:T(512)S(1)}, f32[512]{0:T(512)S(1)}, u32[]{:S(2)}, u32[]{:S(2)}) collective-permute-start(f32[512]{0:T(512)S(1)} %add.82), channel_id=1, source_target_pairs={{0,6},{2,4},{4,2},{6,0},{1,7},{3,5},{5,3},{7,1},{8,14},{10,12},{12... | collective-permute-start | bytes 6152 | tf_op jit(solution)/shard_map/ppermute | solution.py:33
  55.0 1.6 %collective-permute-done.5 = f32[512]{0:T(512)S(1)} collective-permute-done((f32[512]{0:T(512)S(1)}, f32[512]{0:T(512)S(1)}, u32[]{:S(2)}, u32[]{:S(2)}) %collective-permute-start.5) | collective-permute-done | bytes 2080 | tf_op jit(solution)/shard_map/ppermute | solution.py:33
  57.2 15.9 %all_to_all.13 = f32[32,1,2048]{2,1,0:T(1,128)S(1)} all-to-all(f32[32,1,2048]{2,1,0:T(1,128)S(1)} %broadcast_in_dim.11), channel_id=1, replica_groups=mesh['dy'=4,'dz'=8,'cx'=4,'core'=2] {'dy','dz'}, dimensions={0} | all-to-all | bytes 524288 | tf_op jit(solution)/shard_map/all_to_all | solution.py:45
  73.2 2.5 %multiply_reduce_fusion = f32[512]{0:T(512)S(1)} fusion(f32[512,2048]{1,0:T(8,128)} %copy-done, f32[2048]{0:T(1024)S(1)} %broadcast_divide_fusion.1), kind=kLoop, calls=%fused_computation.7 | loop fusion | flops 2096640 | bytes 4204544 | tf_op jit(solution)/shard_map/reduce_sum | solution.py:56
  77.0 2.7 %collective-permute-start.7 = (f32[512]{0:T(512)S(1)}, f32[512]{0:T(512)S(1)}, u32[]{:S(2)}, u32[]{:S(2)}) collective-permute-start(f32[512]{0:T(512)S(1)} %add.84), channel_id=1, source_target_pairs={{0,2},{2,0},{4,6},{6,4},{1,3},{3,1},{5,7},{7,5},{8,10},{10,8},{12,... | collective-permute-start | bytes 6152 | tf_op jit(solution)/shard_map/ppermute | solution.py:33
  79.6 1.6 %collective-permute-done.7 = f32[512]{0:T(512)S(1)} collective-permute-done((f32[512]{0:T(512)S(1)}, f32[512]{0:T(512)S(1)}, u32[]{:S(2)}, u32[]{:S(2)}) %collective-permute-start.7) | collective-permute-done | bytes 2080 | tf_op jit(solution)/shard_map/ppermute | solution.py:33
  81.2 2.1 %collective-permute-start.8 = (f32[512]{0:T(512)S(1)}, f32[512]{0:T(512)S(1)}, u32[]{:S(2)}, u32[]{:S(2)}) collective-permute-start(f32[512]{0:T(512)S(1)} %add.85), channel_id=1, source_target_pairs={{0,6},{2,4},{4,2},{6,0},{1,7},{3,5},{5,3},{7,1},{8,14},{10,12},{12... | collective-permute-start | bytes 6152 | tf_op jit(solution)/shard_map/ppermute | solution.py:33
  83.3 1.6 %collective-permute-done.8 = f32[512]{0:T(512)S(1)} collective-permute-done((f32[512]{0:T(512)S(1)}, f32[512]{0:T(512)S(1)}, u32[]{:S(2)}, u32[]{:S(2)}) %collective-permute-start.8) | collective-permute-done | bytes 2080 | tf_op jit(solution)/shard_map/ppermute | solution.py:33
  85.7 3.0 %collective-permute-done.9 = f32[4,512]{1,0:T(4,128)S(1)} collective-permute-done((f32[4,512]{1,0:T(4,128)S(1)}, f32[4,512]{1,0:T(4,128)S(1)}, u32[]{:S(2)}, u32[]{:S(2)}) %collective-permute-start.9) | collective-permute-done | bytes 8224 | tf_op jit(solution)/shard_map/ppermute | solution.py:33
  91.5 2.4 %collective-permute-done.10 = f32[4,512]{1,0:T(4,128)S(1)} collective-permute-done((f32[4,512]{1,0:T(4,128)S(1)}, f32[4,512]{1,0:T(4,128)S(1)}, u32[]{:S(2)}, u32[]{:S(2)}) %collective-permute-start.10) | collective-permute-done | bytes 8224 | tf_op jit(solution)/shard_map/ppermute | solution.py:33
  93.9 5.5 %convert_reduce_fusion = (f32[512]{0:T(512)S(1)}, bf16[2048,512]{1,0:T(8,128)(2,1)S(1)}) fusion(f32[512]{0:T(512)S(1)} %dynamic_slice.7, bf16[2048,768]{1,0:T(8,128)(2,1)} %copy-done.4, s32[]{:T(128)S(6)} %select_n.9, f32[2048,768]{1,0:T(8,128)} %all-gather.2.cloned.1.call-done, f32[]{:T(128)} %bitcast.1, f32[2048]{0:T(1024)S(1)} %bitcast.10), kind=kOutput, calls=%fused_computation.5 | convolution fusion | flops 1620049408 | bytes 9187844 | tf_op jit(solution)/shard_map/dot_general | solution.py:88
  99.4 3.1 %fusion.3 = f32[512,768]{1,0:T(8,128)} fusion(bf16[2048,512]{1,0:T(8,128)(2,1)S(1)} %get-tuple-element.8, f32[2048,768]{1,0:T(8,128)S(1)} %copy-done.3, f32[]{:T(128)} %bitcast.1), kind=kOutput, calls=%fused_computation.15 | convolution fusion | flops 1613758464 | bytes 9961476 | tf_op jit(solution)/shard_map/dot_general | solution.py:96
  103.8 15.7 %all-reduce = f32[512]{0:T(512)S(1)} all-reduce(f32[512]{0:T(512)S(1)} %get-tuple-element.7), channel_id=3, replica_groups=mesh['dy'=4,'dz'=8,'cx'=4,'core'=2] {'dz'}, use_global_device_ids=true, to_apply=%region_11.12.clone | all-reduce | flops 512 | bytes 4096
  119.6 21.7 %reduce-scatter.2.cloned.1.call-done = f32[64,768]{1,0:T(8,128)} async-done(((f32[512,768]{1,0:T(8,128)}), f32[64,768]{1,0:T(8,128)}) %reduce-scatter.2.cloned.1.call-update) | async-done | bytes 196624 | tf_op jit(solution)/shard_map/reduce_scatter | solution.py:99
  141.3 1.7 %broadcast_divide_fusion = f32[64,768]{1,0:T(8,128)} fusion(f32[64,768]{1,0:T(8,128)} %reduce-scatter.2.cloned.1.call-done, f32[64]{0:T(128)S(1)} %dynamic-slice.2), kind=kLoop, calls=%fused_computation.19 | loop fusion | flops 49152 | bytes 393472 | tf_op jit(solution)/shard_map/div | solution.py:102
  (60 shorter events, 12.8 us)
Async XLA Ops:
  6.5 4.1 %copy-start.2 = (bf16[2048,768]{1,0:T(8,128)(2,1)S(1)}, bf16[2048,768]{1,0:T(8,128)(2,1)}, u32[]{:S(2)}) copy-start(bf16[2048,768]{1,0:T(8,128)(2,1)} %param.3) | copy-start | bytes 9437188
  6.5 87.4 %all-gather.2.cloned.1.call-start = ((), (), s32[]{:S(2)}) async-start(), calls=%async_computation.3 | async-start | bytes 7864320 | tf_op jit(solution)/shard_map/all_gather | solution.py:80
  10.6 130.7 %reduce-scatter.2.cloned.1.call-start = ((), (), s32[]{:S(2)}) async-start(), calls=%async_computation.4 | async-start | bytes 1769472 | tf_op jit(solution)/shard_map/reduce_scatter | solution.py:99
  10.7 1.3 copy-start.5
  12.0 2.0 %copy-start.4 = (bf16[2048,768]{1,0:T(8,128)(2,1)}, bf16[2048,768]{1,0:T(8,128)(2,1)S(1)}, u32[]{:S(2)}) copy-start(bf16[2048,768]{1,0:T(8,128)(2,1)S(1)} %fusion.1) | copy-start | bytes 9437188
  14.0 8.7 %copy-start = (f32[512,2048]{1,0:T(8,128)}, f32[512,2048]{1,0:T(8,128)S(1)}, u32[]{:S(2)}) copy-start(f32[512,2048]{1,0:T(8,128)S(1)} %get-tuple-element.6) | copy-start | bytes 12582916
  14.0 1.3 collective-permute-start
  15.3 3.8 %collective-permute-start.1 = (f32[512]{0:T(512)S(1)}, f32[512]{0:T(512)S(1)}, u32[]{:S(2)}, u32[]{:S(2)}) collective-permute-start(f32[512]{0:T(512)S(1)} %add.78), channel_id=1, source_target_pairs={{0,2},{2,0},{4,6},{6,4},{1,3},{3,1},{5,7},{7,5},{8,10},{10,8},{12,... | collective-permute-start | bytes 6152 | tf_op jit(solution)/shard_map/ppermute | solution.py:33
  19.1 3.6 %collective-permute-start.2 = (f32[512]{0:T(512)S(1)}, f32[512]{0:T(512)S(1)}, u32[]{:S(2)}, u32[]{:S(2)}) collective-permute-start(f32[512]{0:T(512)S(1)} %add.79), channel_id=1, source_target_pairs={{0,6},{2,4},{4,2},{6,0},{1,7},{3,5},{5,3},{7,1},{8,14},{10,12},{12... | collective-permute-start | bytes 6152 | tf_op jit(solution)/shard_map/ppermute | solution.py:33
  45.5 11.2 %copy-start.1 = (f32[512,2048]{1,0:T(8,128)S(1)}, f32[512,2048]{1,0:T(8,128)}, u32[]{:S(2)}) copy-start(f32[512,2048]{1,0:T(8,128)} %copy-done) | copy-start | bytes 12582916
  48.2 1.2 collective-permute-start.3
  49.5 3.6 %collective-permute-start.4 = (f32[512]{0:T(512)S(1)}, f32[512]{0:T(512)S(1)}, u32[]{:S(2)}, u32[]{:S(2)}) collective-permute-start(f32[512]{0:T(512)S(1)} %add.81), channel_id=1, source_target_pairs={{0,2},{2,0},{4,6},{6,4},{1,3},{3,1},{5,7},{7,5},{8,10},{10,8},{12,... | collective-permute-start | bytes 6152 | tf_op jit(solution)/shard_map/ppermute | solution.py:33
  53.1 3.6 %collective-permute-start.5 = (f32[512]{0:T(512)S(1)}, f32[512]{0:T(512)S(1)}, u32[]{:S(2)}, u32[]{:S(2)}) collective-permute-start(f32[512]{0:T(512)S(1)} %add.82), channel_id=1, source_target_pairs={{0,6},{2,4},{4,2},{6,0},{1,7},{3,5},{5,3},{7,1},{8,14},{10,12},{12... | collective-permute-start | bytes 6152 | tf_op jit(solution)/shard_map/ppermute | solution.py:33
  75.7 1.2 collective-permute-start.6
  77.0 4.2 %collective-permute-start.7 = (f32[512]{0:T(512)S(1)}, f32[512]{0:T(512)S(1)}, u32[]{:S(2)}, u32[]{:S(2)}) collective-permute-start(f32[512]{0:T(512)S(1)} %add.84), channel_id=1, source_target_pairs={{0,2},{2,0},{4,6},{6,4},{1,3},{3,1},{5,7},{7,5},{8,10},{10,8},{12,... | collective-permute-start | bytes 6152 | tf_op jit(solution)/shard_map/ppermute | solution.py:33
  81.2 3.7 %collective-permute-start.8 = (f32[512]{0:T(512)S(1)}, f32[512]{0:T(512)S(1)}, u32[]{:S(2)}, u32[]{:S(2)}) collective-permute-start(f32[512]{0:T(512)S(1)} %add.85), channel_id=1, source_target_pairs={{0,6},{2,4},{4,2},{6,0},{1,7},{3,5},{5,3},{7,1},{8,14},{10,12},{12... | collective-permute-start | bytes 6152 | tf_op jit(solution)/shard_map/ppermute | solution.py:33
  85.0 3.7 %collective-permute-start.9 = (f32[4,512]{1,0:T(4,128)S(1)}, f32[4,512]{1,0:T(4,128)S(1)}, u32[]{:S(2)}, u32[]{:S(2)}) collective-permute-start(f32[4,512]{1,0:T(4,128)S(1)} %dynamic_update_slice.6), channel_id=1, source_target_pairs={{0,64},{64,0},{128,192},{192,128},{1,65},{65,1},{129,193},{193,129... | collective-permute-start | bytes 24584 | tf_op jit(solution)/shard_map/ppermute | solution.py:33
  88.8 5.1 %collective-permute-start.10 = (f32[4,512]{1,0:T(4,128)S(1)}, f32[4,512]{1,0:T(4,128)S(1)}, u32[]{:S(2)}, u32[]{:S(2)}) collective-permute-start(f32[4,512]{1,0:T(4,128)S(1)} %add.88), channel_id=1, source_target_pairs={{0,192},{64,128},{128,64},{192,0},{1,193},{65,129},{129,65},{193,1... | collective-permute-start | bytes 24584 | tf_op jit(solution)/shard_map/ppermute | solution.py:33
  93.9 5.5 %copy-start.3 = (f32[2048,768]{1,0:T(8,128)S(1)}, f32[2048,768]{1,0:T(8,128)}, u32[]{:S(2)}) copy-start(f32[2048,768]{1,0:T(8,128)} %all-gather.2.cloned.1.call-done) | copy-start | bytes 18874372
  99.4 3.1 %copy-start.6 = (u32[256]{0:T(256)S(1)}, u32[256]{0:T(256)}, u32[]{:S(2)}) copy-start(u32[256]{0:T(256)} %constant.41) | copy-start | bytes 3076
Sparse Core Ops, SparseCore 0:
  10.7 76.7 all-gather.1
  102.6 38.6 reduce-scatter.1

commit v11 on v8

--- a/solution.py
+++ b/solution.py
@@ -35,19 +35,27 @@
     return x
 
 
+def exchange_sum(x, axes):
+    n = 1
+    for a in axes:
+        n *= lax.axis_size(a)
+    copies = jnp.broadcast_to(x[None], (n,) + x.shape)
+    return jnp.sum(lax.all_to_all(copies, axes, 0, 0, tiled=False), axis=0)
+
+
 def cent_sum(x):
-    return doubling_sum(x, ("core", "cx"))
+    return exchange_sum(x, ("cx", "core"))
 
 
 def dp_sum(x):
-    return doubling_sum(x, ("dz", "dy"))
+    return exchange_sum(x, ("dy", "dz"))
 
 
-def doubling_gather(x, axis):
+def exchange_gather(x, axis):
     n = lax.axis_size(axis)
-    slots = jnp.zeros((n,) + x.shape, x.dtype)
-    slots = lax.dynamic_update_index_in_dim(slots, x, lax.axis_index(axis), 0)
-    return doubling_sum(slots, (axis,)).reshape((n * x.shape[0],) + x.shape[1:])
+    copies = jnp.broadcast_to(x[None], (n,) + x.shape)
+    blocks = lax.all_to_all(copies, axis, 0, 0, tiled=False)
+    return blocks.reshape((n * x.shape[0],) + x.shape[1:])
 
 
 def row_update(boltzmann_affinity, column_factor):
@@ -78,7 +86,7 @@
     gathered = lax.all_gather(scaled_rows, "dy", axis=0, tiled=True)
     unit = column_factor[0] * 0.0 + 1.0
     gathered = (gathered * unit).astype(jnp.bfloat16)
-    gathered_weight = doubling_gather(row_weight, "dy")
+    gathered_weight = exchange_gather(row_weight, "dy")
     sub_cents = local_cents // ny
     start = lax.axis_index("dy") * sub_cents
     sub_normed = lax.dynamic_slice_in_dim(cent_normed, start, sub_cents, 0)

time: 161 us -> 154 us (0.957)
  blocking collectives: 19 us -> 80.3 us
  waiting for transfers between devices: 64.4 us -> 22.7 us
  starting transfers between devices: 42.2 us -> 3.29 us
  other arithmetic: 8.52 us -> 18.2 us
  matrix products: 10.6 us -> 12.5 us
    all_to_all x0 -> x5, blocking collectives: none -> 64.4 us  [exchange_sum(): return jnp.sum(lax.all_to_all(copies, axes, 0, 0, tiled=False), axis=0)]
    ppermute x21 -> x0, starting transfers between devices: 42.2 us -> none  [doubling_sum(): x = x + lax.ppermute(x, a, pairs)]
    ppermute x21 -> x0, waiting for transfers between devices: 39.2 us -> none  [doubling_sum(): x = x + lax.ppermute(x, a, pairs)]
    reduce_scatter x1, waiting for transfers between devices: 25.2 us -> 18.6 us  [shards(): lax.psum_scatter((weighted, col_mass), 'dz', scatter_dimension=0, tiled=T...]
    reduce_sum x2, other arithmetic: 0.72 us -> 5.57 us  [shards(): partial_cols = jnp.sum(row_weight[:, None] * boltzmann_affinity, axis=0)]
    reduce_sum x2, other arithmetic: 0.73 us -> 5.18 us  [row_update(): partial_rows = jnp.sum(boltzmann_affinity * column_factor[None, :], axis=1)]
    all_to_all x0 -> x1, waiting for transfers between devices: none -> 4.05 us  [exchange_gather(): blocks = lax.all_to_all(copies, axis, 0, 0, tiled=False)]
    all_to_all x0 -> x1, starting transfers between devices: none -> 3.25 us  [exchange_gather(): blocks = lax.all_to_all(copies, axis, 0, 0, tiled=False)]
  transfers between devices with their start and end apart: 23 -> 3, of which waited for: 22 -> 2; matrix products, arithmetic and copies ran while one was open for 4% -> 12% of each run, Pallas kernels for 0% -> 0%
where the time goes in v11:
time: 154 us
  blocking collectives  80.3 us (52%)
  waiting for transfers between devices  22.7 us (15%)
  other arithmetic  18.2 us (12%)
  between operations  14.8 us (10%)
  matrix products  12.5 us (8%)
  starting transfers between devices  3.29 us (2%)
  local copies, waits for them, and re-layouts  2.2 us (1%)
    all_to_all x5, blocking collectives, exchange_sum(): return jnp.sum(lax.all_to_all(copies, axes, 0, 0, tiled=False), axis=0)  64.4 us
    reduce_scatter x1, waiting for transfers between devices, shards(): lax.psum_scatter((weighted, col_mass), 'dz', scatter_dimension=0, tiled=T...  18.6 us
    unnamed x1, blocking collectives  15.8 us
    reduce_sum x2, other arithmetic, shards(): partial_cols = jnp.sum(row_weight[:, None] * boltzmann_affinity, axis=0)  5.57 us
    dot_general x1, matrix products, shards(): lax.dot_general(gathered, sub_normed, (((1,), (1,)), ((), ())), preferred...  5.48 us
    reduce_sum x2, other arithmetic, row_update(): partial_rows = jnp.sum(boltzmann_affinity * column_factor[None, :], axis=1)  5.18 us
    all_to_all x1, waiting for transfers between devices, exchange_gather(): blocks = lax.all_to_all(copies, axis, 0, 0, tiled=False)  4.05 us
    dot_general x1, matrix products, shards(): lax.dot_general(normed, cent_normed, (((1,), (1,)), ((), ())), preferred_...  3.97 us
  transfers between devices with their start and end apart: 3, of which 2 were waited for; matrix products, arithmetic and copies ran while one was open for 12% of the time, Pallas kernels for 0%

profile of v11, /device:TPU:2, one launch (start us, length us, event | category | flops | bytes accessed | tf_op | source)
XLA Modules:
  0.0 153.9 jit_solution(3787223346707175609)
XLA Ops:
  6.5 1.5 fusion.2
  8.1 2.5 %convert_multiply_fusion.2 = f32[512,768]{1,0:T(8,128)} fusion(bf16[512,768]{1,0:T(8,128)(2,1)} %param.2, f32[512]{0:T(512)S(1)} %add_rsqrt_fusion.1), kind=kLoop, calls=%fused_computation.12 | loop fusion | flops 786432 | bytes 2361344 | tf_op jit(solution)/shard_map/mul | solution.py:17
  10.6 0.7 fusion
  11.3 0.6 fusion.1
  11.9 4.0 %fusion.7 = (f32[512]{0:T(512)S(1)}, f32[512,2048]{1,0:T(8,128)}) fusion(bf16[2048,768]{1,0:T(8,128)(2,1)S(1)} %fusion.1, f32[512]{0:T(512)S(1)} %add_rsqrt_fusion.1, bf16[512,768]{1,0:T(8,128)(2,1)S(1)} %copy-done.3), kind=kOutput, calls=%fused_computation.27 | convolution fusion | flops 1613889024 | bytes 8130560 | tf_op jit(solution)/shard_map/dot_general | solution.py:72
  15.9 8.5 %all_to_all.36 = f32[8,1,512]{2,1,0:T(1,128)S(1)} all-to-all(f32[8,1,512]{2,1,0:T(1,128)S(1)} %broadcast_in_dim.12), channel_id=1, replica_groups=mesh['dy'=4,'dz'=8,'cx'=4,'core'=2] {'cx','core'}, dimensions={0} | all-to-all | bytes 32768 | tf_op jit(solution)/shard_map/all_to_all | solution.py:43
  24.5 3.0 %multiply_reduce_fusion.3 = f32[2048]{0:T(1024)S(1)} fusion(f32[512,2048]{1,0:T(8,128)} %get-tuple-element.6, f32[512]{0:T(512)S(1)} %broadcast_divide_fusion.5), kind=kLoop, calls=%fused_computation.10 | loop fusion | flops 2095104 | bytes 4204544 | tf_op jit(solution)/shard_map/reduce_sum | solution.py:83
  27.7 23.7 %all_to_all.37 = f32[32,1,2048]{2,1,0:T(1,128)S(1)} all-to-all(f32[32,1,2048]{2,1,0:T(1,128)S(1)} %broadcast_in_dim.13), channel_id=1, replica_groups=mesh['dy'=4,'dz'=8,'cx'=4,'core'=2] {'dy','dz'}, dimensions={0} | all-to-all | bytes 524288 | tf_op jit(solution)/shard_map/all_to_all | solution.py:43
  51.6 2.6 %multiply_reduce_fusion.2 = f32[512]{0:T(512)S(1)} fusion(f32[512,2048]{1,0:T(8,128)} %get-tuple-element.6, f32[2048]{0:T(1024)S(1)} %broadcast_divide_fusion.2), kind=kLoop, calls=%fused_computation.9 | loop fusion | flops 2096640 | bytes 4204544 | tf_op jit(solution)/shard_map/reduce_sum | solution.py:62
  54.2 7.6 %all_to_all.38 = f32[8,1,512]{2,1,0:T(1,128)S(1)} all-to-all(f32[8,1,512]{2,1,0:T(1,128)S(1)} %broadcast_in_dim.14), channel_id=1, replica_groups=mesh['dy'=4,'dz'=8,'cx'=4,'core'=2] {'cx','core'}, dimensions={0} | all-to-all | bytes 32768 | tf_op jit(solution)/shard_map/all_to_all | solution.py:43
  61.9 2.5 %multiply_reduce_fusion.1 = f32[2048]{0:T(1024)S(1)} fusion(f32[512,2048]{1,0:T(8,128)} %get-tuple-element.6, f32[512]{0:T(512)S(1)} %broadcast_divide_fusion.4), kind=kLoop, calls=%fused_computation.8 | loop fusion | flops 2095104 | bytes 4204544 | tf_op jit(solution)/shard_map/reduce_sum | solution.py:83
  64.6 16.8 %all_to_all.39 = f32[32,1,2048]{2,1,0:T(1,128)S(1)} all-to-all(f32[32,1,2048]{2,1,0:T(1,128)S(1)} %broadcast_in_dim.15), channel_id=1, replica_groups=mesh['dy'=4,'dz'=8,'cx'=4,'core'=2] {'dy','dz'}, dimensions={0} | all-to-all | bytes 524288 | tf_op jit(solution)/shard_map/all_to_all | solution.py:43
  81.5 2.5 %multiply_reduce_fusion = f32[512]{0:T(512)S(1)} fusion(f32[512,2048]{1,0:T(8,128)} %get-tuple-element.6, f32[2048]{0:T(1024)S(1)} %broadcast_divide_fusion.1), kind=kLoop, calls=%fused_computation.7 | loop fusion | flops 2096640 | bytes 4204544 | tf_op jit(solution)/shard_map/reduce_sum | solution.py:62
  84.1 7.8 %all_to_all.40 = f32[8,1,512]{2,1,0:T(1,128)S(1)} all-to-all(f32[8,1,512]{2,1,0:T(1,128)S(1)} %broadcast_in_dim.16), channel_id=1, replica_groups=mesh['dy'=4,'dz'=8,'cx'=4,'core'=2] {'cx','core'}, dimensions={0} | all-to-all | bytes 32768 | tf_op jit(solution)/shard_map/all_to_all | solution.py:43
  91.9 0.6 broadcast_in_dim.17
  92.5 3.2 %all-to-all-start.5 = ((f32[4,1,512]{2,1,0:T(1,128)}), f32[4,1,512]{2,1,0:T(1,128)S(1)}, u32[]{:S(2)}, u32[]{:S(2)}) async-start(f32[4,1,512]{2,1,0:T(1,128)} %broadcast_in_dim.17), calls=%async_computation.5 | async-start | bytes 16384 | tf_op jit(solution)/shard_map/all_to_all | solution.py:57
  95.8 0.5 slice.4
  97.0 4.1 %all-to-all-done.5 = f32[4,1,512]{2,1,0:T(1,128)S(1)} async-done(((f32[4,1,512]{2,1,0:T(1,128)}), f32[4,1,512]{2,1,0:T(1,128)S(1)}, u32[]{:S(2)}, u32[]{:S(2)}) %all-to-all-start.5) | async-done | bytes 8224 | tf_op jit(solution)/shard_map/all_to_all | solution.py:57
  101.1 5.5 %convert_reduce_fusion = (f32[512]{0:T(512)S(1)}, bf16[2048,512]{1,0:T(8,128)(2,1)S(1)}) fusion(f32[512]{0:T(512)S(1)} %dynamic_slice.7, bf16[2048,768]{1,0:T(8,128)(2,1)} %copy-done.2, s32[]{:T(128)S(6)} %select_n.4, f32[2048,768]{1,0:T(8,128)} %all-gather.2.cloned.1.call-done, f32[]{:T(128)} %bitcast.1, f32[2048]{0:T(1024)S(1)} %bitcast.5), kind=kOutput, calls=%fused_computation.5 | convolution fusion | flops 1620049408 | bytes 9187844 | tf_op jit(solution)/shard_map/dot_general | solution.py:94
  106.6 3.1 %fusion.3 = f32[512,768]{1,0:T(8,128)} fusion(bf16[2048,512]{1,0:T(8,128)(2,1)S(1)} %get-tuple-element.8, f32[2048,768]{1,0:T(8,128)S(1)} %copy-done.1, f32[]{:T(128)} %bitcast.1), kind=kOutput, calls=%fused_computation.15 | convolution fusion | flops 1613758464 | bytes 9961476 | tf_op jit(solution)/shard_map/dot_general | solution.py:102
  109.7 0.6 dynamic-slice
  110.9 15.8 %all-reduce = f32[512]{0:T(512)S(1)} all-reduce(f32[512]{0:T(512)S(1)} %get-tuple-element.7), channel_id=3, replica_groups=mesh['dy'=4,'dz'=8,'cx'=4,'core'=2] {'dz'}, use_global_device_ids=true, to_apply=%region_14.0.clone | all-reduce | flops 512 | bytes 4096
  126.8 18.6 %reduce-scatter.2.cloned.1.call-done = f32[64,768]{1,0:T(8,128)} async-done(((f32[512,768]{1,0:T(8,128)}), f32[64,768]{1,0:T(8,128)}) %reduce-scatter.2.cloned.1.call-update) | async-done | bytes 196624 | tf_op jit(solution)/shard_map/reduce_scatter | solution.py:105
  145.4 1.7 %broadcast_divide_fusion = f32[64,768]{1,0:T(8,128)} fusion(f32[64,768]{1,0:T(8,128)} %reduce-scatter.2.cloned.1.call-done, f32[64]{0:T(128)S(1)} %dynamic-slice.1), kind=kLoop, calls=%fused_computation.18 | loop fusion | flops 49152 | bytes 393472 | tf_op jit(solution)/shard_map/div | solution.py:108
  (34 shorter events, 1.0 us)
Async XLA Ops:
  6.5 4.1 %copy-start = (bf16[2048,768]{1,0:T(8,128)(2,1)S(1)}, bf16[2048,768]{1,0:T(8,128)(2,1)}, u32[]{:S(2)}) copy-start(bf16[2048,768]{1,0:T(8,128)(2,1)} %param.3) | copy-start | bytes 9437188
  6.5 94.5 %all-gather.2.cloned.1.call-start = ((), (), s32[]{:S(2)}) async-start(), calls=%async_computation.7 | async-start | bytes 7864320 | tf_op jit(solution)/shard_map/all_gather | solution.py:86
  10.6 1.3 copy-start.3
  11.9 4.0 %copy-start.2 = (bf16[2048,768]{1,0:T(8,128)(2,1)}, bf16[2048,768]{1,0:T(8,128)(2,1)S(1)}, u32[]{:S(2)}) copy-start(bf16[2048,768]{1,0:T(8,128)(2,1)S(1)} %fusion.1) | copy-start | bytes 9437188
  92.5 8.5 %all-to-all-start.5 = ((f32[4,1,512]{2,1,0:T(1,128)}), f32[4,1,512]{2,1,0:T(1,128)S(1)}, u32[]{:S(2)}, u32[]{:S(2)}) async-start(f32[4,1,512]{2,1,0:T(1,128)} %broadcast_in_dim.17), calls=%async_computation.5 | async-start | bytes 16384 | tf_op jit(solution)/shard_map/all_to_all | solution.py:57
  95.8 49.6 %reduce-scatter.2.cloned.1.call-start = ((), (), s32[]{:S(2)}) async-start(), calls=%async_computation.8 | async-start | bytes 1769472 | tf_op jit(solution)/shard_map/reduce_scatter | solution.py:105
  101.1 5.5 %copy-start.1 = (f32[2048,768]{1,0:T(8,128)S(1)}, f32[2048,768]{1,0:T(8,128)}, u32[]{:S(2)}) copy-start(f32[2048,768]{1,0:T(8,128)} %all-gather.2.cloned.1.call-done) | copy-start | bytes 18874372
  106.6 3.1 %copy-start.4 = (u32[256]{0:T(256)S(1)}, u32[256]{0:T(256)}, u32[]{:S(2)}) copy-start(u32[256]{0:T(256)} %constant.35) | copy-start | bytes 3076
Sparse Core Ops, SparseCore 0:
  10.7 76.7 all-gather.1
  109.8 35.5 reduce-scatter.1

commit v12 on v10

--- a/solution.py
+++ b/solution.py
@@ -45,11 +45,11 @@
     return jnp.sum(lax.all_to_all(copies, ("dy", "dz"), 0, 0, tiled=False), axis=0)
 
 
-def doubling_gather(x, axis):
+def exchange_gather(x, axis):
     n = lax.axis_size(axis)
-    slots = jnp.zeros((n,) + x.shape, x.dtype)
-    slots = lax.dynamic_update_index_in_dim(slots, x, lax.axis_index(axis), 0)
-    return doubling_sum(slots, (axis,)).reshape((n * x.shape[0],) + x.shape[1:])
+    copies = jnp.broadcast_to(x[None], (n,) + x.shape)
+    blocks = lax.all_to_all(copies, axis, 0, 0, tiled=False)
+    return blocks.reshape((n * x.shape[0],) + x.shape[1:])
 
 
 def row_update(boltzmann_affinity, column_factor):
@@ -80,7 +80,7 @@
     gathered = lax.all_gather(scaled_rows, "dy", axis=0, tiled=True)
     unit = column_factor[0] * 0.0 + 1.0
     gathered = (gathered * unit).astype(jnp.bfloat16)
-    gathered_weight = doubling_gather(row_weight, "dy")
+    gathered_weight = exchange_gather(row_weight, "dy")
     sub_cents = local_cents // ny
     start = lax.axis_index("dy") * sub_cents
     sub_normed = lax.dynamic_slice_in_dim(cent_normed, start, sub_cents, 0)

time: 150 us -> 150 us (level)
  waiting for transfers between devices: 41.1 us -> 39.5 us
    ppermute x11 -> x9, waiting for transfers between devices: 19.3 us -> 13.9 us  [doubling_sum(): x = x + lax.ppermute(x, a, pairs)]
    all_to_all x0 -> x1, waiting for transfers between devices: none -> 3.87 us  [exchange_gather(): blocks = lax.all_to_all(copies, axis, 0, 0, tiled=False)]
    all_to_all x0 -> x1, starting transfers between devices: none -> 3.25 us  [exchange_gather(): blocks = lax.all_to_all(copies, axis, 0, 0, tiled=False)]
    ppermute x11 -> x9, starting transfers between devices: 14.5 us -> 12.3 us  [doubling_sum(): x = x + lax.ppermute(x, a, pairs)]
  transfers between devices with their start and end apart: 13 -> 12, of which waited for: 12 -> 11; matrix products, arithmetic and copies ran while one was open for 8% -> 8% of each run, Pallas kernels for 0% -> 0%
where the time goes in v12:
time: 150 us
  blocking collectives  53.8 us (36%)
  waiting for transfers between devices  39.5 us (26%)
  starting transfers between devices  15.8 us (11%)
  between operations  14.8 us (10%)
  other arithmetic  13.3 us (9%)
  matrix products  10.6 us (7%)
  local copies, waits for them, and re-layouts  2.17 us (1%)
    all_to_all x2, blocking collectives, dp_sum(): lax.all_to_all(copies, ('dy', 'dz'), 0, 0, tiled=False)  38 us
    reduce_scatter x1, waiting for transfers between devices, shards(): lax.psum_scatter((weighted, col_mass), 'dz', scatter_dimension=0, tiled=T...  21.7 us
    unnamed x1, blocking collectives  15.8 us
    ppermute x9, waiting for transfers between devices, doubling_sum(): x = x + lax.ppermute(x, a, pairs)  13.9 us
    ppermute x9, starting transfers between devices, doubling_sum(): x = x + lax.ppermute(x, a, pairs)  12.3 us
    dot_general x1, matrix products, shards(): lax.dot_general(gathered, sub_normed, (((1,), (1,)), ((), ())), preferred...  5.48 us
    reduce_sum x2, other arithmetic, row_update(): partial_rows = jnp.sum(boltzmann_affinity * column_factor[None, :], axis=1)  5.24 us
    all_to_all x1, waiting for transfers between devices, exchange_gather(): blocks = lax.all_to_all(copies, axis, 0, 0, tiled=False)  3.87 us
  transfers between devices with their start and end apart: 12, of which 11 were waited for; matrix products, arithmetic and copies ran while one was open for 8% of the time, Pallas kernels for 0%

profile of v12, /device:TPU:2, one launch (start us, length us, event | category | flops | bytes accessed | tf_op | source)
XLA Modules:
  0.0 150.0 jit_solution(1693005849919323901)
XLA Ops:
  8.1 2.5 %convert_multiply_fusion.2 = f32[512,768]{1,0:T(8,128)} fusion(bf16[512,768]{1,0:T(8,128)(2,1)} %param.2, f32[512]{0:T(512)S(1)} %add_rsqrt_fusion.1), kind=kLoop, calls=%fused_computation.12 | loop fusion | flops 786432 | bytes 2361344 | tf_op jit(solution)/shard_map/mul | solution.py:17
  11.9 2.0 %fusion.7 = (f32[512]{0:T(512)S(1)}, f32[512,2048]{1,0:T(8,128)S(1)}) fusion(bf16[2048,768]{1,0:T(8,128)(2,1)S(1)} %fusion.1, f32[512]{0:T(512)S(1)} %add_rsqrt_fusion.1, bf16[512,768]{1,0:T(8,128)(2,1)S(1)} %copy-done.5), kind=kOutput, calls=%fused_computation.27 | convolution fusion | flops 1613889024 | bytes 8130560 | tf_op jit(solution)/shard_map/dot_general | solution.py:66
  15.2 2.2 %collective-permute-start.1 = (f32[512]{0:T(512)S(1)}, f32[512]{0:T(512)S(1)}, u32[]{:S(2)}, u32[]{:S(2)}) collective-permute-start(f32[512]{0:T(512)S(1)} %add.67), channel_id=1, source_target_pairs={{0,2},{2,0},{4,6},{6,4},{1,3},{3,1},{5,7},{7,5},{8,10},{10,8},{12,... | collective-permute-start | bytes 6152 | tf_op jit(solution)/shard_map/ppermute | solution.py:33
  17.5 1.6 %collective-permute-done.1 = f32[512]{0:T(512)S(1)} collective-permute-done((f32[512]{0:T(512)S(1)}, f32[512]{0:T(512)S(1)}, u32[]{:S(2)}, u32[]{:S(2)}) %collective-permute-start.1) | collective-permute-done | bytes 2080 | tf_op jit(solution)/shard_map/ppermute | solution.py:33
  20.3 2.3 %collective-permute-done.2 = f32[512]{0:T(512)S(1)} collective-permute-done((f32[512]{0:T(512)S(1)}, f32[512]{0:T(512)S(1)}, u32[]{:S(2)}, u32[]{:S(2)}) %collective-permute-start.2) | collective-permute-done | bytes 2080 | tf_op jit(solution)/shard_map/ppermute | solution.py:33
  23.1 22.1 %all_to_all.18 = f32[32,1,2048]{2,1,0:T(1,128)S(1)} all-to-all(f32[32,1,2048]{2,1,0:T(1,128)S(1)} %broadcast_in_dim.6), channel_id=1, replica_groups=mesh['dy'=4,'dz'=8,'cx'=4,'core'=2] {'dy','dz'}, dimensions={0} | all-to-all | bytes 524288 | tf_op jit(solution)/shard_map/all_to_all | solution.py:45
  45.5 2.7 %multiply_reduce_fusion.2 = f32[512]{0:T(512)S(1)} fusion(f32[512,2048]{1,0:T(8,128)} %copy-done, f32[2048]{0:T(1024)S(1)} %broadcast_divide_fusion.2), kind=kLoop, calls=%fused_computation.9 | loop fusion | flops 2096640 | bytes 4204544 | tf_op jit(solution)/shard_map/reduce_sum | solution.py:56
  49.4 1.8 %collective-permute-start.4 = (f32[512]{0:T(512)S(1)}, f32[512]{0:T(512)S(1)}, u32[]{:S(2)}, u32[]{:S(2)}) collective-permute-start(f32[512]{0:T(512)S(1)} %add.70), channel_id=1, source_target_pairs={{0,2},{2,0},{4,6},{6,4},{1,3},{3,1},{5,7},{7,5},{8,10},{10,8},{12,... | collective-permute-start | bytes 6152 | tf_op jit(solution)/shard_map/ppermute | solution.py:33
  51.2 1.8 %collective-permute-done.4 = f32[512]{0:T(512)S(1)} collective-permute-done((f32[512]{0:T(512)S(1)}, f32[512]{0:T(512)S(1)}, u32[]{:S(2)}, u32[]{:S(2)}) %collective-permute-start.4) | collective-permute-done | bytes 2080 | tf_op jit(solution)/shard_map/ppermute | solution.py:33
  53.0 1.9 %collective-permute-start.5 = (f32[512]{0:T(512)S(1)}, f32[512]{0:T(512)S(1)}, u32[]{:S(2)}, u32[]{:S(2)}) collective-permute-start(f32[512]{0:T(512)S(1)} %add.71), channel_id=1, source_target_pairs={{0,6},{2,4},{4,2},{6,0},{1,7},{3,5},{5,3},{7,1},{8,14},{10,12},{12... | collective-permute-start | bytes 6152 | tf_op jit(solution)/shard_map/ppermute | solution.py:33
  55.0 1.6 %collective-permute-done.5 = f32[512]{0:T(512)S(1)} collective-permute-done((f32[512]{0:T(512)S(1)}, f32[512]{0:T(512)S(1)}, u32[]{:S(2)}, u32[]{:S(2)}) %collective-permute-start.5) | collective-permute-done | bytes 2080 | tf_op jit(solution)/shard_map/ppermute | solution.py:33
  57.1 15.9 %all_to_all.19 = f32[32,1,2048]{2,1,0:T(1,128)S(1)} all-to-all(f32[32,1,2048]{2,1,0:T(1,128)S(1)} %broadcast_in_dim.7), channel_id=1, replica_groups=mesh['dy'=4,'dz'=8,'cx'=4,'core'=2] {'dy','dz'}, dimensions={0} | all-to-all | bytes 524288 | tf_op jit(solution)/shard_map/all_to_all | solution.py:45
  73.1 2.5 %multiply_reduce_fusion = f32[512]{0:T(512)S(1)} fusion(f32[512,2048]{1,0:T(8,128)} %copy-done, f32[2048]{0:T(1024)S(1)} %broadcast_divide_fusion.1), kind=kLoop, calls=%fused_computation.7 | loop fusion | flops 2096640 | bytes 4204544 | tf_op jit(solution)/shard_map/reduce_sum | solution.py:56
  76.9 2.6 %collective-permute-start.7 = (f32[512]{0:T(512)S(1)}, f32[512]{0:T(512)S(1)}, u32[]{:S(2)}, u32[]{:S(2)}) collective-permute-start(f32[512]{0:T(512)S(1)} %add.73), channel_id=1, source_target_pairs={{0,2},{2,0},{4,6},{6,4},{1,3},{3,1},{5,7},{7,5},{8,10},{10,8},{12,... | collective-permute-start | bytes 6152 | tf_op jit(solution)/shard_map/ppermute | solution.py:33
  79.6 1.6 %collective-permute-done.7 = f32[512]{0:T(512)S(1)} collective-permute-done((f32[512]{0:T(512)S(1)}, f32[512]{0:T(512)S(1)}, u32[]{:S(2)}, u32[]{:S(2)}) %collective-permute-start.7) | collective-permute-done | bytes 2080 | tf_op jit(solution)/shard_map/ppermute | solution.py:33
  81.1 2.2 %collective-permute-start.8 = (f32[512]{0:T(512)S(1)}, f32[512]{0:T(512)S(1)}, u32[]{:S(2)}, u32[]{:S(2)}) collective-permute-start(f32[512]{0:T(512)S(1)} %add.74), channel_id=1, source_target_pairs={{0,6},{2,4},{4,2},{6,0},{1,7},{3,5},{5,3},{7,1},{8,14},{10,12},{12... | collective-permute-start | bytes 6152 | tf_op jit(solution)/shard_map/ppermute | solution.py:33
  83.3 1.6 %collective-permute-done.8 = f32[512]{0:T(512)S(1)} collective-permute-done((f32[512]{0:T(512)S(1)}, f32[512]{0:T(512)S(1)}, u32[]{:S(2)}, u32[]{:S(2)}) %collective-permute-start.8) | collective-permute-done | bytes 2080 | tf_op jit(solution)/shard_map/ppermute | solution.py:33
  85.5 3.2 %all-to-all-start.2 = ((f32[4,1,512]{2,1,0:T(1,128)}), f32[4,1,512]{2,1,0:T(1,128)S(1)}, u32[]{:S(2)}, u32[]{:S(2)}) async-start(f32[4,1,512]{2,1,0:T(1,128)} %broadcast_in_dim.8), calls=%async_computation.2 | async-start | bytes 16384 | tf_op jit(solution)/shard_map/all_to_all | solution.py:51
  90.1 3.9 %all-to-all-done.2 = f32[4,1,512]{2,1,0:T(1,128)S(1)} async-done(((f32[4,1,512]{2,1,0:T(1,128)}), f32[4,1,512]{2,1,0:T(1,128)S(1)}, u32[]{:S(2)}, u32[]{:S(2)}) %all-to-all-start.2) | async-done | bytes 8224 | tf_op jit(solution)/shard_map/all_to_all | solution.py:51
  94.0 5.5 %convert_reduce_fusion = (f32[512]{0:T(512)S(1)}, bf16[2048,512]{1,0:T(8,128)(2,1)S(1)}) fusion(f32[512]{0:T(512)S(1)} %dynamic_slice.7, bf16[2048,768]{1,0:T(8,128)(2,1)} %copy-done.4, s32[]{:T(128)S(6)} %select_n.4, f32[2048,768]{1,0:T(8,128)} %all-gather.2.cloned.1.call-done, f32[]{:T(128)} %bitcast.1, f32[2048]{0:T(1024)S(1)} %bitcast.5), kind=kOutput, calls=%fused_computation.5 | convolution fusion | flops 1620049408 | bytes 9187844 | tf_op jit(solution)/shard_map/dot_general | solution.py:88
  99.5 3.1 %fusion.3 = f32[512,768]{1,0:T(8,128)} fusion(bf16[2048,512]{1,0:T(8,128)(2,1)S(1)} %get-tuple-element.8, f32[2048,768]{1,0:T(8,128)S(1)} %copy-done.3, f32[]{:T(128)} %bitcast.1), kind=kOutput, calls=%fused_computation.15 | convolution fusion | flops 1613758464 | bytes 9961476 | tf_op jit(solution)/shard_map/dot_general | solution.py:96
  103.9 15.8 %all-reduce = f32[512]{0:T(512)S(1)} all-reduce(f32[512]{0:T(512)S(1)} %get-tuple-element.7), channel_id=3, replica_groups=mesh['dy'=4,'dz'=8,'cx'=4,'core'=2] {'dz'}, use_global_device_ids=true, to_apply=%region_11.0.clone | all-reduce | flops 512 | bytes 4096
  119.7 21.7 %reduce-scatter.2.cloned.1.call-done = f32[64,768]{1,0:T(8,128)} async-done(((f32[512,768]{1,0:T(8,128)}), f32[64,768]{1,0:T(8,128)}) %reduce-scatter.2.cloned.1.call-update) | async-done | bytes 196624 | tf_op jit(solution)/shard_map/reduce_scatter | solution.py:99
  141.4 1.7 %broadcast_divide_fusion = f32[64,768]{1,0:T(8,128)} fusion(f32[64,768]{1,0:T(8,128)} %reduce-scatter.2.cloned.1.call-done, f32[64]{0:T(128)S(1)} %dynamic-slice.1), kind=kLoop, calls=%fused_computation.18 | loop fusion | flops 49152 | bytes 393472 | tf_op jit(solution)/shard_map/div | solution.py:102
  (53 shorter events, 11.3 us)
Async XLA Ops:
  6.5 4.1 %copy-start.2 = (bf16[2048,768]{1,0:T(8,128)(2,1)S(1)}, bf16[2048,768]{1,0:T(8,128)(2,1)}, u32[]{:S(2)}) copy-start(bf16[2048,768]{1,0:T(8,128)(2,1)} %param.3) | copy-start | bytes 9437188
  6.5 87.5 %all-gather.2.cloned.1.call-start = ((), (), s32[]{:S(2)}) async-start(), calls=%async_computation.4 | async-start | bytes 7864320 | tf_op jit(solution)/shard_map/all_gather | solution.py:80
  10.6 1.3 copy-start.5
  11.9 2.0 %copy-start.4 = (bf16[2048,768]{1,0:T(8,128)(2,1)}, bf16[2048,768]{1,0:T(8,128)(2,1)S(1)}, u32[]{:S(2)}) copy-start(bf16[2048,768]{1,0:T(8,128)(2,1)S(1)} %fusion.1) | copy-start | bytes 9437188
  14.0 8.7 %copy-start = (f32[512,2048]{1,0:T(8,128)}, f32[512,2048]{1,0:T(8,128)S(1)}, u32[]{:S(2)}) copy-start(f32[512,2048]{1,0:T(8,128)S(1)} %get-tuple-element.6) | copy-start | bytes 12582916
  14.0 1.3 collective-permute-start
  15.2 3.8 %collective-permute-start.1 = (f32[512]{0:T(512)S(1)}, f32[512]{0:T(512)S(1)}, u32[]{:S(2)}, u32[]{:S(2)}) collective-permute-start(f32[512]{0:T(512)S(1)} %add.67), channel_id=1, source_target_pairs={{0,2},{2,0},{4,6},{6,4},{1,3},{3,1},{5,7},{7,5},{8,10},{10,8},{12,... | collective-permute-start | bytes 6152 | tf_op jit(solution)/shard_map/ppermute | solution.py:33
  19.0 3.6 %collective-permute-start.2 = (f32[512]{0:T(512)S(1)}, f32[512]{0:T(512)S(1)}, u32[]{:S(2)}, u32[]{:S(2)}) collective-permute-start(f32[512]{0:T(512)S(1)} %add.68), channel_id=1, source_target_pairs={{0,6},{2,4},{4,2},{6,0},{1,7},{3,5},{5,3},{7,1},{8,14},{10,12},{12... | collective-permute-start | bytes 6152 | tf_op jit(solution)/shard_map/ppermute | solution.py:33
  45.4 11.2 %copy-start.1 = (f32[512,2048]{1,0:T(8,128)S(1)}, f32[512,2048]{1,0:T(8,128)}, u32[]{:S(2)}) copy-start(f32[512,2048]{1,0:T(8,128)} %copy-done) | copy-start | bytes 12582916
  48.2 1.2 collective-permute-start.3
  49.4 3.6 %collective-permute-start.4 = (f32[512]{0:T(512)S(1)}, f32[512]{0:T(512)S(1)}, u32[]{:S(2)}, u32[]{:S(2)}) collective-permute-start(f32[512]{0:T(512)S(1)} %add.70), channel_id=1, source_target_pairs={{0,2},{2,0},{4,6},{6,4},{1,3},{3,1},{5,7},{7,5},{8,10},{10,8},{12,... | collective-permute-start | bytes 6152 | tf_op jit(solution)/shard_map/ppermute | solution.py:33
  53.0 3.6 %collective-permute-start.5 = (f32[512]{0:T(512)S(1)}, f32[512]{0:T(512)S(1)}, u32[]{:S(2)}, u32[]{:S(2)}) collective-permute-start(f32[512]{0:T(512)S(1)} %add.71), channel_id=1, source_target_pairs={{0,6},{2,4},{4,2},{6,0},{1,7},{3,5},{5,3},{7,1},{8,14},{10,12},{12... | collective-permute-start | bytes 6152 | tf_op jit(solution)/shard_map/ppermute | solution.py:33
  75.7 1.2 collective-permute-start.6
  76.9 4.2 %collective-permute-start.7 = (f32[512]{0:T(512)S(1)}, f32[512]{0:T(512)S(1)}, u32[]{:S(2)}, u32[]{:S(2)}) collective-permute-start(f32[512]{0:T(512)S(1)} %add.73), channel_id=1, source_target_pairs={{0,2},{2,0},{4,6},{6,4},{1,3},{3,1},{5,7},{7,5},{8,10},{10,8},{12,... | collective-permute-start | bytes 6152 | tf_op jit(solution)/shard_map/ppermute | solution.py:33
  81.1 3.7 %collective-permute-start.8 = (f32[512]{0:T(512)S(1)}, f32[512]{0:T(512)S(1)}, u32[]{:S(2)}, u32[]{:S(2)}) collective-permute-start(f32[512]{0:T(512)S(1)} %add.74), channel_id=1, source_target_pairs={{0,6},{2,4},{4,2},{6,0},{1,7},{3,5},{5,3},{7,1},{8,14},{10,12},{12... | collective-permute-start | bytes 6152 | tf_op jit(solution)/shard_map/ppermute | solution.py:33
  85.5 8.5 %all-to-all-start.2 = ((f32[4,1,512]{2,1,0:T(1,128)}), f32[4,1,512]{2,1,0:T(1,128)S(1)}, u32[]{:S(2)}, u32[]{:S(2)}) async-start(f32[4,1,512]{2,1,0:T(1,128)} %broadcast_in_dim.8), calls=%async_computation.2 | async-start | bytes 16384 | tf_op jit(solution)/shard_map/all_to_all | solution.py:51
  88.7 52.7 %reduce-scatter.2.cloned.1.call-start = ((), (), s32[]{:S(2)}) async-start(), calls=%async_computation.5 | async-start | bytes 1769472 | tf_op jit(solution)/shard_map/reduce_scatter | solution.py:99
  94.0 5.5 %copy-start.3 = (f32[2048,768]{1,0:T(8,128)S(1)}, f32[2048,768]{1,0:T(8,128)}, u32[]{:S(2)}) copy-start(f32[2048,768]{1,0:T(8,128)} %all-gather.2.cloned.1.call-done) | copy-start | bytes 18874372
  99.5 3.1 %copy-start.6 = (u32[256]{0:T(256)S(1)}, u32[256]{0:T(256)}, u32[]{:S(2)}) copy-start(u32[256]{0:T(256)} %constant.35) | copy-start | bytes 3076
Sparse Core Ops, SparseCore 0:
  10.7 76.7 all-gather.1
  102.7 38.6 reduce-scatter.1

commit v13 on v10

--- a/solution.py
+++ b/solution.py
@@ -76,11 +76,15 @@
         row_weight = row_update(boltzmann_affinity, column_factor)
         partial_cols = jnp.sum(row_weight[:, None] * boltzmann_affinity, axis=0)
         column_factor = balance_ratio / dp_sum(partial_cols)
-    row_weight = row_update(boltzmann_affinity, column_factor)
+    partial_rows = jnp.sum(boltzmann_affinity * column_factor[None, :], axis=1)
+    slots = jnp.zeros((ny,) + partial_rows.shape, jnp.float32)
+    slots = lax.dynamic_update_index_in_dim(slots, partial_rows, lax.axis_index("dy"), 0)
+    copies = jnp.broadcast_to(slots[None], (ny * lax.axis_size("cx") * lax.axis_size("core"),) + slots.shape)
+    row_totals = jnp.sum(lax.all_to_all(copies, ("dy", "cx", "core"), 0, 0, tiled=False), axis=0)
     gathered = lax.all_gather(scaled_rows, "dy", axis=0, tiled=True)
     unit = column_factor[0] * 0.0 + 1.0
     gathered = (gathered * unit).astype(jnp.bfloat16)
-    gathered_weight = doubling_gather(row_weight, "dy")
+    gathered_weight = (1.0 / row_totals).reshape(-1)
     sub_cents = local_cents // ny
     start = lax.axis_index("dy") * sub_cents
     sub_normed = lax.dynamic_slice_in_dim(cent_normed, start, sub_cents, 0)

time: 150 us -> 150 us (level)
  blocking collectives: 53.7 us -> 37.7 us
  waiting for transfers between devices: 41.1 us -> 49.4 us
  starting transfers between devices: 14.6 us -> 19.9 us
    all_to_all x0 -> x2, waiting for transfers between devices: none -> 17.7 us  [the longest x1 11.6 us: dp_sum(): lax.all_to_all(copies, ('dy', 'dz'), 0, 0, tiled=False)]
    all_to_all x2 -> x1, blocking collectives: 38 us -> 22.1 us  [dp_sum(): lax.all_to_all(copies, ('dy', 'dz'), 0, 0, tiled=False)]
    all_to_all x0 -> x2, starting transfers between devices: none -> 12.3 us  [the longest x1 7.82 us: shards(): lax.all_to_all(copies, ('dy', 'cx', 'core'), 0, 0, tiled=False)]
    ppermute x11 -> x6, waiting for transfers between devices: 19.3 us -> 9.6 us  [doubling_sum(): x = x + lax.ppermute(x, a, pairs)]
    ppermute x11 -> x6, starting transfers between devices: 14.5 us -> 7.44 us  [doubling_sum(): x = x + lax.ppermute(x, a, pairs)]
    reduce_sum x0 -> x2, other arithmetic: none -> 2.6 us  [the longest x1 2.54 us: shards(): partial_rows = jnp.sum(boltzmann_affinity * column_factor[None, :], axis=1)]
    reduce_sum x2 -> x1, other arithmetic: 5.24 us -> 2.7 us  [row_update(): partial_rows = jnp.sum(boltzmann_affinity * column_factor[None, :], axis=1)]
  transfers between devices with their start and end apart: 13 -> 10, of which waited for: 12 -> 9; matrix products, arithmetic and copies ran while one was open for 8% -> 9% of each run, Pallas kernels for 0% -> 0%
where the time goes in v13:
time: 150 us; the launch traced here: 149 us
  waiting for transfers between devices  49.4 us (33%)
  blocking collectives  37.7 us (25%)
  starting transfers between devices  19.9 us (13%)
  between operations  14.9 us (10%)
  other arithmetic  13.4 us (9%)
  matrix products  10.6 us (7%)
  local copies, waits for them, and re-layouts  3.07 us (2%)
    all_to_all x1, blocking collectives, dp_sum(): lax.all_to_all(copies, ('dy', 'dz'), 0, 0, tiled=False)  22.1 us
    reduce_scatter x1, waiting for transfers between devices, shards(): lax.psum_scatter((weighted, col_mass), 'dz', scatter_dimension=0, tiled=T...  22.1 us
    unnamed x1, blocking collectives  15.5 us
    all_to_all x1, waiting for transfers between devices, dp_sum(): lax.all_to_all(copies, ('dy', 'dz'), 0, 0, tiled=False)  11.6 us
    ppermute x6, waiting for transfers between devices, doubling_sum(): x = x + lax.ppermute(x, a, pairs)  9.6 us
    all_to_all x1, starting transfers between devices, shards(): lax.all_to_all(copies, ('dy', 'cx', 'core'), 0, 0, tiled=False)  7.82 us
    ppermute x6, starting transfers between devices, doubling_sum(): x = x + lax.ppermute(x, a, pairs)  7.44 us
    all_to_all x1, waiting for transfers between devices, shards(): lax.all_to_all(copies, ('dy', 'cx', 'core'), 0, 0, tiled=False)  6.09 us
  transfers between devices with their start and end apart: 10, of which 9 were waited for; matrix products, arithmetic and copies ran while one was open for 9% of the time, Pallas kernels for 0%

profile of v13, /device:TPU:2, one launch (start us, length us, event | category | flops | bytes accessed | tf_op | source)
XLA Modules:
  0.0 149.0 jit_solution(17181839631841303031)
XLA Ops:
  6.5 1.5 %fusion.2 = f32[512]{0:T(512)S(1)} fusion(bf16[512,768]{1,0:T(8,128)(2,1)} %param.2), kind=kLoop, calls=%fused_computation.14 | loop fusion | flops 1179136 | bytes 788480 | tf_op jit(solution)/shard_map/reduce_sum | solution.py:16
  8.1 2.5 %convert_multiply_fusion.2 = f32[512,768]{1,0:T(8,128)} fusion(bf16[512,768]{1,0:T(8,128)(2,1)} %param.2, f32[512]{0:T(512)S(1)} %add_rsqrt_fusion.1), kind=kLoop, calls=%fused_computation.12 | loop fusion | flops 786432 | bytes 2361344 | tf_op jit(solution)/shard_map/mul | solution.py:17
  11.9 2.0 %fusion.7 = (f32[512]{0:T(512)S(1)}, f32[512,2048]{1,0:T(8,128)S(1)}) fusion(bf16[2048,768]{1,0:T(8,128)(2,1)S(1)} %fusion.1, f32[512]{0:T(512)S(1)} %add_rsqrt_fusion.1, bf16[512,768]{1,0:T(8,128)(2,1)S(1)} %copy-done.5), kind=kOutput, calls=%fused_computation.27 | convolution fusion | flops 1613889024 | bytes 8130560 | tf_op jit(solution)/shard_map/dot_general | solution.py:66
  14.1 1.1 collective-permute-done
  15.2 2.2 %collective-permute-start.1 = (f32[512]{0:T(512)S(1)}, f32[512]{0:T(512)S(1)}, u32[]{:S(2)}, u32[]{:S(2)}) collective-permute-start(f32[512]{0:T(512)S(1)} %add.62), channel_id=1, source_target_pairs={{0,2},{2,0},{4,6},{6,4},{1,3},{3,1},{5,7},{7,5},{8,10},{10,8},{12,... | collective-permute-start | bytes 6152 | tf_op jit(solution)/shard_map/ppermute | solution.py:33
  17.5 1.6 %collective-permute-done.1 = f32[512]{0:T(512)S(1)} collective-permute-done((f32[512]{0:T(512)S(1)}, f32[512]{0:T(512)S(1)}, u32[]{:S(2)}, u32[]{:S(2)}) %collective-permute-start.1) | collective-permute-done | bytes 2080 | tf_op jit(solution)/shard_map/ppermute | solution.py:33
  19.0 1.3 collective-permute-start.2
  20.3 2.3 %collective-permute-done.2 = f32[512]{0:T(512)S(1)} collective-permute-done((f32[512]{0:T(512)S(1)}, f32[512]{0:T(512)S(1)}, u32[]{:S(2)}, u32[]{:S(2)}) %collective-permute-start.2) | collective-permute-done | bytes 2080 | tf_op jit(solution)/shard_map/ppermute | solution.py:33
  23.1 22.1 %all_to_all.17 = f32[32,1,2048]{2,1,0:T(1,128)S(1)} all-to-all(f32[32,1,2048]{2,1,0:T(1,128)S(1)} %broadcast_in_dim.12), channel_id=1, replica_groups=mesh['dy'=4,'dz'=8,'cx'=4,'core'=2] {'dy','dz'}, dimensions={0} | all-to-all | bytes 524288 | tf_op jit(solution)/shard_map/all_to_all | solution.py:45
  45.5 2.7 %multiply_reduce_fusion.2 = f32[512]{0:T(512)S(1)} fusion(f32[512,2048]{1,0:T(8,128)} %copy-done, f32[2048]{0:T(1024)S(1)} %broadcast_divide_fusion.2), kind=kLoop, calls=%fused_computation.9 | loop fusion | flops 2096640 | bytes 4204544 | tf_op jit(solution)/shard_map/reduce_sum | solution.py:56
  49.4 1.8 %collective-permute-start.4 = (f32[512]{0:T(512)S(1)}, f32[512]{0:T(512)S(1)}, u32[]{:S(2)}, u32[]{:S(2)}) collective-permute-start(f32[512]{0:T(512)S(1)} %add.65), channel_id=1, source_target_pairs={{0,2},{2,0},{4,6},{6,4},{1,3},{3,1},{5,7},{7,5},{8,10},{10,8},{12,... | collective-permute-start | bytes 6152 | tf_op jit(solution)/shard_map/ppermute | solution.py:33
  51.2 1.8 %collective-permute-done.4 = f32[512]{0:T(512)S(1)} collective-permute-done((f32[512]{0:T(512)S(1)}, f32[512]{0:T(512)S(1)}, u32[]{:S(2)}, u32[]{:S(2)}) %collective-permute-start.4) | collective-permute-done | bytes 2080 | tf_op jit(solution)/shard_map/ppermute | solution.py:33
  53.0 1.9 %collective-permute-start.5 = (f32[512]{0:T(512)S(1)}, f32[512]{0:T(512)S(1)}, u32[]{:S(2)}, u32[]{:S(2)}) collective-permute-start(f32[512]{0:T(512)S(1)} %add.66), channel_id=1, source_target_pairs={{0,6},{2,4},{4,2},{6,0},{1,7},{3,5},{5,3},{7,1},{8,14},{10,12},{12... | collective-permute-start | bytes 6152 | tf_op jit(solution)/shard_map/ppermute | solution.py:33
  55.0 1.6 %collective-permute-done.5 = f32[512]{0:T(512)S(1)} collective-permute-done((f32[512]{0:T(512)S(1)}, f32[512]{0:T(512)S(1)}, u32[]{:S(2)}, u32[]{:S(2)}) %collective-permute-start.5) | collective-permute-done | bytes 2080 | tf_op jit(solution)/shard_map/ppermute | solution.py:33
  57.8 4.4 %all-to-all-start.1 = ((f32[32,1,2048]{2,1,0:T(1,128)}), f32[32,1,2048]{2,1,0:T(1,128)S(1)}, u32[]{:S(2)}, u32[]{:S(2)}) async-start(f32[32,1,2048]{2,1,0:T(1,128)} %broadcast_in_dim.13), calls=%async_computation.1 | async-start | bytes 524288 | tf_op jit(solution)/shard_map/all_to_all | solution.py:45
  62.3 11.6 %all-to-all-done.1 = f32[32,1,2048]{2,1,0:T(1,128)S(1)} async-done(((f32[32,1,2048]{2,1,0:T(1,128)}), f32[32,1,2048]{2,1,0:T(1,128)S(1)}, u32[]{:S(2)}, u32[]{:S(2)}) %all-to-all-start.1) | async-done | bytes 262176 | tf_op jit(solution)/shard_map/all_to_all | solution.py:45
  74.0 2.5 %multiply_reduce_fusion = f32[512]{0:T(512)S(1)} fusion(f32[512,2048]{1,0:T(8,128)} %copy-done, f32[2048]{0:T(1024)S(1)} %broadcast_divide_fusion.1), kind=kLoop, calls=%fused_computation.7 | loop fusion | flops 2096640 | bytes 4204544 | tf_op jit(solution)/shard_map/reduce_sum | solution.py:79
  77.4 7.8 %all-to-all-start.2 = ((f32[32,4,512]{2,1,0:T(4,128)}), f32[32,4,512]{2,1,0:T(4,128)S(1)}, u32[]{:S(2)}, u32[]{:S(2)}) async-start(f32[32,4,512]{2,1,0:T(4,128)} %broadcast_in_dim.15), calls=%async_computation.2 | async-start | bytes 524288 | tf_op jit(solution)/shard_map/all_to_all | solution.py:83
  86.7 6.1 %all-to-all-done.2 = f32[32,4,512]{2,1,0:T(4,128)S(1)} async-done(((f32[32,4,512]{2,1,0:T(4,128)}), f32[32,4,512]{2,1,0:T(4,128)S(1)}, u32[]{:S(2)}, u32[]{:S(2)}) %all-to-all-start.2) | async-done | bytes 262176 | tf_op jit(solution)/shard_map/all_to_all | solution.py:83
  92.9 5.5 %convert_reduce_fusion = (f32[512]{0:T(512)S(1)}, bf16[2048,512]{1,0:T(8,128)(2,1)S(1)}) fusion(f32[512]{0:T(512)S(1)} %dynamic_slice.7, bf16[2048,768]{1,0:T(8,128)(2,1)} %copy-done.4, s32[]{:T(128)S(6)} %select_n.9, f32[2048,768]{1,0:T(8,128)} %all-gather.2.cloned.1.call-done, f32[]{:T(128)} %bitcast.1, f32[2048]{0:T(1024)S(1)} %bitcast.9), kind=kOutput, calls=%fused_computation.5 | convolution fusion | flops 1620049408 | bytes 9187844 | tf_op jit(solution)/shard_map/dot_general | solution.py:92
  98.4 3.0 %fusion.3 = f32[512,768]{1,0:T(8,128)} fusion(bf16[2048,512]{1,0:T(8,128)(2,1)S(1)} %get-tuple-element.8, f32[2048,768]{1,0:T(8,128)S(1)} %copy-done.3, f32[]{:T(128)} %bitcast.1), kind=kOutput, calls=%fused_computation.15 | convolution fusion | flops 1613758464 | bytes 9961476 | tf_op jit(solution)/shard_map/dot_general | solution.py:100
  102.7 15.5 %all-reduce = f32[512]{0:T(512)S(1)} all-reduce(f32[512]{0:T(512)S(1)} %get-tuple-element.7), channel_id=3, replica_groups=mesh['dy'=4,'dz'=8,'cx'=4,'core'=2] {'dz'}, use_global_device_ids=true, to_apply=%region_12.13.clone | all-reduce | flops 512 | bytes 4096
  118.4 22.1 %reduce-scatter.2.cloned.1.call-done = f32[64,768]{1,0:T(8,128)} async-done(((f32[512,768]{1,0:T(8,128)}), f32[64,768]{1,0:T(8,128)}) %reduce-scatter.2.cloned.1.call-update) | async-done | bytes 196624 | tf_op jit(solution)/shard_map/reduce_scatter | solution.py:103
  140.5 1.7 %broadcast_divide_fusion = f32[64,768]{1,0:T(8,128)} fusion(f32[64,768]{1,0:T(8,128)} %reduce-scatter.2.cloned.1.call-done, f32[64]{0:T(128)S(1)} %dynamic-slice.1), kind=kLoop, calls=%fused_computation.18 | loop fusion | flops 49152 | bytes 393472 | tf_op jit(solution)/shard_map/div | solution.py:106
  (50 shorter events, 7.1 us)
Async XLA Ops:
  6.5 4.1 %copy-start.2 = (bf16[2048,768]{1,0:T(8,128)(2,1)S(1)}, bf16[2048,768]{1,0:T(8,128)(2,1)}, u32[]{:S(2)}) copy-start(bf16[2048,768]{1,0:T(8,128)(2,1)} %param.3) | copy-start | bytes 9437188
  6.5 86.4 %all-gather.2.cloned.1.call-start = ((), (), s32[]{:S(2)}) async-start(), calls=%async_computation.4 | async-start | bytes 7864320 | tf_op jit(solution)/shard_map/all_gather | solution.py:84
  10.6 1.3 copy-start.5
  11.9 2.0 %copy-start.4 = (bf16[2048,768]{1,0:T(8,128)(2,1)}, bf16[2048,768]{1,0:T(8,128)(2,1)S(1)}, u32[]{:S(2)}) copy-start(bf16[2048,768]{1,0:T(8,128)(2,1)S(1)} %fusion.1) | copy-start | bytes 9437188
  14.0 8.7 %copy-start = (f32[512,2048]{1,0:T(8,128)}, f32[512,2048]{1,0:T(8,128)S(1)}, u32[]{:S(2)}) copy-start(f32[512,2048]{1,0:T(8,128)S(1)} %get-tuple-element.6) | copy-start | bytes 12582916
  14.0 1.3 collective-permute-start
  15.2 3.8 %collective-permute-start.1 = (f32[512]{0:T(512)S(1)}, f32[512]{0:T(512)S(1)}, u32[]{:S(2)}, u32[]{:S(2)}) collective-permute-start(f32[512]{0:T(512)S(1)} %add.62), channel_id=1, source_target_pairs={{0,2},{2,0},{4,6},{6,4},{1,3},{3,1},{5,7},{7,5},{8,10},{10,8},{12,... | collective-permute-start | bytes 6152 | tf_op jit(solution)/shard_map/ppermute | solution.py:33
  19.0 3.6 %collective-permute-start.2 = (f32[512]{0:T(512)S(1)}, f32[512]{0:T(512)S(1)}, u32[]{:S(2)}, u32[]{:S(2)}) collective-permute-start(f32[512]{0:T(512)S(1)} %add.63), channel_id=1, source_target_pairs={{0,6},{2,4},{4,2},{6,0},{1,7},{3,5},{5,3},{7,1},{8,14},{10,12},{12... | collective-permute-start | bytes 6152 | tf_op jit(solution)/shard_map/ppermute | solution.py:33
  45.4 11.2 %copy-start.1 = (f32[512,2048]{1,0:T(8,128)S(1)}, f32[512,2048]{1,0:T(8,128)}, u32[]{:S(2)}) copy-start(f32[512,2048]{1,0:T(8,128)} %copy-done) | copy-start | bytes 12582916
  48.2 1.2 collective-permute-start.3
  49.4 3.6 %collective-permute-start.4 = (f32[512]{0:T(512)S(1)}, f32[512]{0:T(512)S(1)}, u32[]{:S(2)}, u32[]{:S(2)}) collective-permute-start(f32[512]{0:T(512)S(1)} %add.65), channel_id=1, source_target_pairs={{0,2},{2,0},{4,6},{6,4},{1,3},{3,1},{5,7},{7,5},{8,10},{10,8},{12,... | collective-permute-start | bytes 6152 | tf_op jit(solution)/shard_map/ppermute | solution.py:33
  53.0 3.6 %collective-permute-start.5 = (f32[512]{0:T(512)S(1)}, f32[512]{0:T(512)S(1)}, u32[]{:S(2)}, u32[]{:S(2)}) collective-permute-start(f32[512]{0:T(512)S(1)} %add.66), channel_id=1, source_target_pairs={{0,6},{2,4},{4,2},{6,0},{1,7},{3,5},{5,3},{7,1},{8,14},{10,12},{12... | collective-permute-start | bytes 6152 | tf_op jit(solution)/shard_map/ppermute | solution.py:33
  57.8 16.1 %all-to-all-start.1 = ((f32[32,1,2048]{2,1,0:T(1,128)}), f32[32,1,2048]{2,1,0:T(1,128)S(1)}, u32[]{:S(2)}, u32[]{:S(2)}) async-start(f32[32,1,2048]{2,1,0:T(1,128)} %broadcast_in_dim.13), calls=%async_computation.1 | async-start | bytes 524288 | tf_op jit(solution)/shard_map/all_to_all | solution.py:45
  77.4 15.4 %all-to-all-start.2 = ((f32[32,4,512]{2,1,0:T(4,128)}), f32[32,4,512]{2,1,0:T(4,128)S(1)}, u32[]{:S(2)}, u32[]{:S(2)}) async-start(f32[32,4,512]{2,1,0:T(4,128)} %broadcast_in_dim.15), calls=%async_computation.2 | async-start | bytes 524288 | tf_op jit(solution)/shard_map/all_to_all | solution.py:83
  85.2 55.2 %reduce-scatter.2.cloned.1.call-start = ((), (), s32[]{:S(2)}) async-start(), calls=%async_computation.5 | async-start | bytes 1769472 | tf_op jit(solution)/shard_map/reduce_scatter | solution.py:103
  92.9 5.5 %copy-start.3 = (f32[2048,768]{1,0:T(8,128)S(1)}, f32[2048,768]{1,0:T(8,128)}, u32[]{:S(2)}) copy-start(f32[2048,768]{1,0:T(8,128)} %all-gather.2.cloned.1.call-done) | copy-start | bytes 18874372
  98.4 3.1 %copy-start.6 = (u32[256]{0:T(256)S(1)}, u32[256]{0:T(256)}, u32[]{:S(2)}) copy-start(u32[256]{0:T(256)} %constant.44) | copy-start | bytes 3076
Sparse Core Ops, SparseCore 0:
  10.7 76.7 all-gather.1
  101.6 38.7 reduce-scatter.1
